TPU v7x, 32 devices: a whole 2x2x4 slice. The times are simulated.
32 devices in a mesh: grp: 2 (over x), hist: 16 (over z, y, core).
Axes of the slice: x: 2, y: 2, z: 4, core: 2. Of those that a mesh axis runs over, the one named last changes fastest.
Arguments:
- item_ids: int32 [512], P(('grp', 'hist')), parts along dimension 0, may hold values from 0 to 16383
- item_table: bfloat16 [16384, 1024], P('hist'), may hold values from -6 to 6
- key_cache: bfloat16 [32768, 1024], P(('grp', 'hist')), parts along dimension 0, may hold values from -6 to 6
- value_cache: bfloat16 [32768, 1024], P(('grp', 'hist')), parts along dimension 0, may hold values from -6 to 6
- time_buckets: int32 [32768], P(('grp', 'hist')), parts along dimension 0, may hold values from 0 to 127
- window_start: int32 [2], P('grp'), parts along dimension 0, may hold values from 0 to 16384
- norm_gain: float32 [1024], replicated, may hold values from 0.25 to 1.75
- proj_in: bfloat16 [1024, 2048], replicated, may hold values from -0.1875 to 0.1875
- time_bias: float32 [16, 128], replicated, may hold values from -3 to 3
- pos_bias: float32 [16, 18], replicated, may hold values from -1 to 1
- out_gain: float32 [1024], replicated, may hold values from 0.25 to 1.75
- proj_out: bfloat16 [1024, 1024], replicated, may hold values from -0.1875 to 0.1875
Outputs:
- scored: bfloat16 [512, 1024], P(('grp', 'hist')), parts along dimension 0
There are 2 independent parts, one for each index of `grp`. A program takes and returns all parts, laid end to end along the dimension named above; an argument that names none is the same for every part. Nothing has to cross between parts.
All inputs are finite; a program needn't handle non-finite values.
Results may differ from a plain program's by a relative error of at most 0.0075.
Values may be sent and summed in bfloat16 or wider, within the bound.
No kernel may reach another device: no remote copies, remote signals or barrier semaphores. Data moves between devices by JAX's collectives and lax.ppermute only.
A program may use at most 128 MiB of HBM per device.

v0:
```python
import functools

import jax
import jax.numpy as jnp
from jax import lax
from jax.experimental import pallas as pl
from jax.experimental.pallas import tpu as pltpu
from jax.sharding import PartitionSpec as P


BF16 = jnp.bfloat16
F32 = jnp.float32
LANES = 128
ROWS_AT_ONCE = 128
EVENTS_AT_ONCE = 512
STEPS_AHEAD = 2
BLOCK = 16
TN = (((0,), (0,)), ((), ()))
NT = (((1,), (1,)), ((), ()))
VMEM = pl.BlockSpec(memory_space=pltpu.VMEM)
SMEM = pl.BlockSpec(memory_space=pltpu.SMEM)
HBM = pl.BlockSpec(memory_space=pltpu.HBM)


def params(mib):
    return pltpu.CompilerParams(vmem_limit_bytes=mib << 20)


PARTNER = 1


def stage_masks(size):
    bits = [1 << k for k in range(1, size.bit_length() - 1)][::-1]
    far = bits[:-1]
    return [sorted(far[k : k + 2]) for k in range(0, len(far), 2)] + [bits[-1:]]


def combos(bits):
    out = [0]
    for b in bits:
        out = out + [m | b for m in out]
    return out


def swap(x, mask, axis, size):
    return lax.ppermute(x, axis, [(i, i ^ mask) for i in range(size)])


def join_kernel(*refs):
    *parts, out_ref = refs
    rows = parts[0].shape[0]
    for k, p in enumerate(parts):
        out_ref[k * rows : (k + 1) * rows, :] = p[...]


def join(pieces, dim):
    if dim:
        return jnp.concatenate(pieces, axis=dim)
    rows, width = pieces[0].shape
    return pl.pallas_call(
        join_kernel,
        out_shape=jax.ShapeDtypeStruct((len(pieces) * rows, width), BF16),
        in_specs=[VMEM] * len(pieces),
        out_specs=VMEM,
        compiler_params=params(16),
        name="join",
    )(*pieces)


def gather_relative(x, dim, axis, size):
    *far, near = stage_masks(size)
    for bits in far:
        x = join([x] + [swap(x, m, axis, size) for m in combos(bits)[1:]], dim)
    return [x, swap(x, near[0], axis, size)]


def gather_rows(x, axis, size):
    *far, near = stage_masks(size)
    for bits in far[:-1]:
        x = join([x] + [swap(x, m, axis, size) for m in combos(bits)[1:]], 0)
    pieces = [x, join([swap(x, m, axis, size) for m in combos(far[-1])[1:]], 0)]
    return pieces + [swap(p, near[0], axis, size) for p in pieces]


def position_bits(size):
    return [b for stage in stage_masks(size) for b in stage]


def candidates_info(ids_refs, me, size, table_rows):
    ids = jnp.concatenate([r[...] for r in ids_refs], axis=1)
    count = ids.shape[1]
    each = count // (size // 2)
    owner = ids // table_rows
    place = lax.broadcasted_iota(jnp.int32, (1, count), 1)
    block = place // each
    mask = jnp.zeros_like(place)
    for k, b in enumerate(position_bits(size)):
        mask = mask + ((block >> k) & 1) * b
    pair = owner >> 1
    key = pair * count + ((mask ^ me) >> 1) * each + place % each
    return pair, key, ids - owner * table_rows + ((owner ^ me) & 1) * table_rows


def to_column(row):
    count = row.shape[1]
    r = lax.broadcasted_iota(jnp.int32, (count, count), 0)
    c = lax.broadcasted_iota(jnp.int32, (count, count), 1)
    return jnp.sum(jnp.where(r == c, row, 0), axis=1, keepdims=True)


def lookup_kernel(place_ref, *refs, size, resident):
    if resident:
        *ids_refs, own_ref, other_ref, out_ref, rounds_ref, blocks_ref = refs
        copies = []
    else:
        *ids_refs, own_hbm, other_hbm, out_ref, rounds_ref, blocks_ref, own_ref, other_ref, sems = refs
        copies = [
            pltpu.make_async_copy(own_hbm, own_ref, sems.at[0]),
            pltpu.make_async_copy(other_hbm, other_ref, sems.at[1]),
        ]
    for c in copies:
        c.start()
    me, turn = place_ref[0], place_ref[1]
    slots = out_ref.shape[0]
    rows = own_ref.shape[0]
    pair, key, offset = candidates_info(ids_refs, me, size, rows)
    count = pair.shape[1]
    key_col = to_column(key)
    before = (key_col < key) & (key_col >= pair * count)
    rank = jnp.sum(before.astype(jnp.int32), axis=0, keepdims=True)
    slot = lax.broadcasted_iota(jnp.int32, (slots, count), 0) + turn * slots
    hit = (pair == (me >> 1)) & (rank == slot)
    want = jnp.sum(jnp.where(hit, offset + 1, 0), axis=1, keepdims=True) - 1
    rounds_ref[0] = jnp.max(rank) // slots + 1
    for c in copies:
        c.wait()
    near = jnp.where(want < 0, 0, want // BLOCK)
    for k in range(slots):
        block = near[k, 0]
        in_own = block < rows // BLOCK
        at = pl.multiple_of((block - jnp.where(in_own, 0, rows // BLOCK)) * BLOCK, BLOCK)
        own, other = own_ref[pl.ds(at, BLOCK), :], other_ref[pl.ds(at, BLOCK), :]
        blocks_ref[k * BLOCK : (k + 1) * BLOCK, :] = jnp.where(in_own, own, other)
    column = lax.broadcasted_iota(jnp.int32, (slots, slots * BLOCK), 1)
    line = lax.broadcasted_iota(jnp.int32, (slots, slots * BLOCK), 0)
    pick = (want >= 0) & (column == line * BLOCK + (want - near * BLOCK))
    found = jnp.dot(pick.astype(F32).astype(BF16), blocks_ref[...], preferred_element_type=F32)
    out_ref[...] = found.astype(BF16)


def lookup(place, ids, tables, slots, size, resident):
    if not resident:
        tables = [pltpu.with_memory_space_constraint(t, pltpu.HBM) for t in tables]
    rows, width = tables[0].shape
    return pl.pallas_call(
        functools.partial(lookup_kernel, size=size, resident=resident),
        out_shape=(
            jax.ShapeDtypeStruct((slots, width), BF16),
            jax.ShapeDtypeStruct((1,), jnp.int32),
        ),
        in_specs=[SMEM] + [VMEM] * len(ids) + [VMEM if resident else HBM] * 2,
        out_specs=(VMEM, SMEM),
        scratch_shapes=[pltpu.VMEM((slots * BLOCK, width), BF16)]
        + ([] if resident else [pltpu.VMEM((rows, width), BF16)] * 2 + [pltpu.SemaphoreType.DMA((2,))]),
        compiler_params=params(16),
        name="lookup",
    )(place, *ids, *tables)


def plan_kernel(place_ref, *refs, size, slots, table_rows):
    *ids_refs, pick_ref = refs
    me, turn = place_ref[0], place_ref[1]
    pair, key, _ = candidates_info(ids_refs, me, size, table_rows)
    count = pair.shape[1]
    key_col = to_column(key)
    pair_col = key_col // count
    before = (key < key_col) & (key >= pair_col * count)
    rank = jnp.sum(before.astype(jnp.int32), axis=1, keepdims=True)
    away = pair_col ^ (me >> 1)
    block = jnp.zeros_like(away)
    for k, b in enumerate(position_bits(size)):
        block = block + jnp.where((away & (b >> 1)) != 0, 1 << k, 0)
    mine = rank - turn * slots
    slot = jnp.where((mine >= 0) & (mine < slots), block * slots + mine, -1)
    pick = slot == lax.broadcasted_iota(jnp.int32, pick_ref.shape, 1)
    pick_ref[...] = pick.astype(F32).astype(BF16)


def plan(place, ids, slots, table_rows, size):
    count = sum(i.shape[1] for i in ids)
    return pl.pallas_call(
        functools.partial(plan_kernel, size=size, slots=slots, table_rows=table_rows),
        out_shape=jax.ShapeDtypeStruct((count, size // 2 * slots), BF16),
        in_specs=[SMEM] + [VMEM] * len(ids),
        out_specs=VMEM,
        compiler_params=params(16),
        name="plan",
    )(place, *ids)


def select_kernel(pick_ref, rows_ref, out_ref):
    out_ref[...] = jnp.dot(pick_ref[...], rows_ref[...], preferred_element_type=F32).astype(BF16)


def select(pick, pieces):
    rows = jnp.concatenate(pieces, axis=0)
    return pl.pallas_call(
        select_kernel,
        out_shape=jax.ShapeDtypeStruct((pick.shape[0], rows.shape[1]), BF16),
        in_specs=[VMEM, VMEM],
        out_specs=VMEM,
        compiler_params=params(12),
        name="select",
    )(pick, rows)


def three_parts(x):
    high = x.astype(BF16)
    rest = x - high.astype(F32)
    middle = rest.astype(BF16)
    return [high, middle, (rest - middle.astype(F32)).astype(BF16)]


def prepare_kernel(
    place_ref, start_ref, times_hbm, time_bias_hbm, pos_bias_hbm, table_hbm, out_ref, table_ref,
    times_ref, time_bias_ref, pos_bias_ref, sems, *, npos, history
):
    pairs = ((times_hbm, times_ref), (time_bias_hbm, time_bias_ref), (pos_bias_hbm, pos_bias_ref), (table_hbm, table_ref))
    copies = [pltpu.make_async_copy(a, b, sems.at[k]) for k, (a, b) in enumerate(pairs)]
    for c in copies:
        c.start()
    events = times_ref.shape[1]
    first = history - start_ref[0] - place_ref[0] * events
    distance = first - lax.broadcasted_iota(jnp.int32, (1, events), 1)
    bucket = jnp.zeros((1, events), jnp.int32)
    for k in range(1, npos):
        bucket = bucket + (distance >= (1 << k)).astype(jnp.int32)
    for c in copies[:3]:
        c.wait()
    columns = []
    for table_ref_, index in ((time_bias_ref, times_ref[...]), (pos_bias_ref, bucket)):
        table = jnp.concatenate(three_parts(table_ref_[...] * 0.5), axis=0)
        kinds = table.shape[1]
        hot = lax.broadcasted_iota(jnp.int32, (kinds, events), 0) == index
        columns.append(jnp.dot(table, hot.astype(F32).astype(BF16), preferred_element_type=F32))
    used = sum(c.shape[0] for c in columns)
    columns.append(jnp.zeros((LANES - used, events), F32))
    out_ref[...] = jnp.concatenate(columns, axis=0).T.astype(BF16)
    copies[3].wait()


def prepare(place, start, times, time_bias, pos_bias, table, history):
    arrays = [times, time_bias, pos_bias, table]
    return pl.pallas_call(
        functools.partial(prepare_kernel, npos=pos_bias.shape[1], history=history),
        out_shape=(
            jax.ShapeDtypeStruct((times.shape[1], LANES), BF16),
            jax.ShapeDtypeStruct(table.shape, BF16),
        ),
        in_specs=[SMEM, SMEM] + [HBM] * 4,
        out_specs=(VMEM, VMEM),
        scratch_shapes=[pltpu.VMEM(a.shape, a.dtype) for a in arrays[:3]] + [pltpu.SemaphoreType.DMA((4,))],
        compiler_params=params(8),
        name="prepare",
    )(place, start, *(pltpu.with_memory_space_constraint(a, pltpu.HBM) for a in arrays))


def silu(x):
    return x / (1.0 + jnp.exp(-x))


def normalise(embedded, gain):
    x = embedded.astype(F32)
    meansq = jnp.mean(x * x, axis=-1, keepdims=True)
    return (x * lax.rsqrt(meansq + 1e-06) * gain).astype(BF16)


def attend_groups(query_ref, caches, groups, heads, keep_ref, send_ref):
    keys, values, biases = caches
    count = query_ref.shape[0]
    width = keys[0].shape[1]
    head_dim = width // heads
    per = LANES // head_dim
    half = count // 2
    rows = min(ROWS_AT_ONCE, count)
    events = keys[0].shape[0]
    step = min(EVENTS_AT_ONCE, events)
    base = groups[0]
    for first in range(0, count, rows):
        lane = lax.broadcasted_iota(jnp.int32, (rows, LANES), 1)
        stacks = {}

        def stack(group):
            if group not in stacks:
                at = (group - base) * LANES
                part = query_ref[first : first + rows, at : at + LANES]
                zero, one = jnp.zeros_like(part), jnp.ones_like(part)
                blocks = []
                for k in range(per):
                    own = jnp.where(lane // head_dim == k, part, zero)
                    chosen = jnp.where(lane % heads == group * per + k, one, zero)
                    blocks.append(jnp.concatenate([own, chosen], axis=1))
                stacks[group] = jnp.concatenate(blocks, axis=0)
            return stacks[group]

        def halves(group, block, j):
            at = slice(group * LANES, (group + 1) * LANES)
            left = jnp.concatenate([keys[block][j : j + step, at], biases[block][j : j + step, :]], axis=1)
            return lax.dot_general(left, stack(group), NT, preferred_element_type=F32)

        steps = [
            (group, block, j) for group in groups for block in range(len(keys)) for j in range(0, events, step)
        ]
        ahead = [halves(*s) for s in steps[:STEPS_AHEAD]]
        total = None
        for n, (group, block, j) in enumerate(steps):
            if n + STEPS_AHEAD < len(steps):
                ahead.append(halves(*steps[n + STEPS_AHEAD]))
            t = ahead.pop(0)
            weights = (t + t * jnp.tanh(t)).astype(BF16)
            at = slice(group * LANES, (group + 1) * LANES)
            term = lax.dot_general(values[block][j : j + step, at], weights, TN, preferred_element_type=F32)
            total = term if total is None else total + term
            if n + 1 < len(steps) and steps[n + 1][0] == group:
                continue
            out = jnp.concatenate(
                [total[k * head_dim : (k + 1) * head_dim, k * rows : (k + 1) * rows] for k in range(per)], axis=0
            ).T
            total = None
            at = slice((group - base) * LANES, (group - base + 1) * LANES)
            if first + rows <= half:
                keep_ref[first : first + rows, at] = out
            elif first >= half:
                send_ref[first - half : first - half + rows, at] = out.astype(BF16)
            else:
                keep_ref[first:half, at] = out[: half - first]
                send_ref[: first + rows - half, at] = out[half - first :].astype(BF16)


def attend_first_kernel(rounds_ref, pick_ref, *refs, heads, blocks, split):
    *row_refs, extra_hbm, gain_ref, proj_ref = refs[: -7 - 3 * blocks]
    caches = refs[-7 - 3 * blocks : -7]
    own_ref, keep_ref, send_ref, later_ref, emb_ref, query_ref, sem = refs[-7:]
    count, width = emb_ref.shape
    rows = jnp.concatenate([r[...] for r in row_refs], axis=0)
    emb_ref[...] = jnp.dot(pick_ref[...], rows, preferred_element_type=F32).astype(BF16)

    @pl.when(rounds_ref[0] > 1)
    def _():
        extra = pltpu.make_async_copy(extra_hbm, query_ref, sem)
        extra.start()
        extra.wait()
        emb_ref[...] = emb_ref[...] + query_ref[...]

    own_ref[...] = emb_ref[: own_ref.shape[0], :]
    head_dim = width // heads
    rows = min(ROWS_AT_ONCE, count)
    for first in range(0, count, rows):
        normed = normalise(emb_ref[first : first + rows, :], gain_ref[...])
        projected = jnp.dot(normed, proj_ref[:, :width], preferred_element_type=F32)
        query = silu(projected).astype(BF16) * jnp.asarray(0.5 * head_dim**-0.5, BF16)
        query_ref[first : first + rows, :] = query
        later_ref[first : first + rows, :] = query[:, split * LANES :]
    parts = [caches[k * blocks : (k + 1) * blocks] for k in range(3)]
    attend_groups(query_ref, parts, range(split), heads, keep_ref, send_ref)


def attend_later_kernel(query_ref, *refs, heads, blocks, split):
    *caches, keep_ref, send_ref = refs
    parts = [caches[k * blocks : (k + 1) * blocks] for k in range(3)]
    attend_groups(query_ref, parts, range(split, parts[0][0].shape[1] // LANES), heads, keep_ref, send_ref)


def attention_cost(count, columns, keys, head_dim):
    events = len(keys) * keys[0].shape[0]
    return pl.CostEstimate(
        flops=8 * count * columns * events,
        transcendentals=count * columns // head_dim * events,
        bytes_accessed=4 * columns * events,
    )


def attend_first(rounds, pick, pieces, extra, gain, proj, keys, values, biases, heads, each, split):
    count, width = extra.shape
    columns = split * LANES
    blocks = len(keys)
    return pl.pallas_call(
        functools.partial(attend_first_kernel, heads=heads, blocks=blocks, split=split),
        out_shape=(
            jax.ShapeDtypeStruct((each, width), BF16),
            jax.ShapeDtypeStruct((count // 2, columns), F32),
            jax.ShapeDtypeStruct((count // 2, columns), BF16),
            jax.ShapeDtypeStruct((count, width - columns), BF16),
        ),
        in_specs=[SMEM, VMEM] + [VMEM] * len(pieces) + [HBM] + [VMEM] * (2 + 3 * blocks),
        out_specs=(VMEM,) * 4,
        scratch_shapes=[
            pltpu.VMEM((count, width), BF16),
            pltpu.VMEM((count, width), BF16),
            pltpu.SemaphoreType.DMA,
        ],
        compiler_params=params(20),
        cost_estimate=attention_cost(count, columns, keys, width // heads),
        name="attend_first",
    )(rounds, pick, *pieces, extra, gain, proj, *keys, *values, *biases)


def attend_later(queries, keys, values, biases, heads, split):
    count, columns = queries.shape
    blocks = len(keys)
    return pl.pallas_call(
        functools.partial(attend_later_kernel, heads=heads, blocks=blocks, split=split),
        out_shape=(
            jax.ShapeDtypeStruct((count // 2, columns), F32),
            jax.ShapeDtypeStruct((count // 2, columns), BF16),
        ),
        in_specs=[VMEM] * (1 + 3 * blocks),
        out_specs=(VMEM, VMEM),
        compiler_params=params(20),
        cost_estimate=attention_cost(count, columns, keys, keys[0].shape[1] // heads),
        name="attend_later",
    )(queries, *keys, *values, *biases)


def combine_kernel(*refs, count):
    halves, (own_ref, *go_refs) = refs[:count], refs[count:]
    rows = own_ref.shape[0]
    for k, out_ref in enumerate([own_ref, *go_refs]):
        at = 0
        for keep_ref, came_ref in zip(halves[::2], halves[1::2]):
            to = at + keep_ref.shape[1]
            block = slice(k * rows, (k + 1) * rows)
            total = keep_ref[block, :] + came_ref[block, :].astype(F32)
            out_ref[:, at:to] = total.astype(out_ref.dtype)
            at = to


def combine(halves, blocks):
    rows = halves[0].shape[0] // blocks
    width = sum(h.shape[1] for h in halves[::2])
    return pl.pallas_call(
        functools.partial(combine_kernel, count=len(halves)),
        out_shape=tuple(jax.ShapeDtypeStruct((rows, width), BF16 if k else F32) for k in range(blocks)),
        in_specs=[VMEM] * len(halves),
        out_specs=(VMEM,) * blocks,
        compiler_params=params(12),
        name="combine",
    )(*halves)


def stage_kernel(*refs, width):
    *refs, sems = refs
    count = len(refs) // 2
    copies = [
        pltpu.make_async_copy(
            a if a.shape[1] == width else a.at[:, pl.ds(0, width)], b, sems.at[k]
        )
        for k, (a, b) in enumerate(zip(refs[:count], refs[count:]))
    ]
    for c in copies:
        c.start()
    for c in copies:
        c.wait()


def stage(width, *arrays, held=True):
    return pl.pallas_call(
        functools.partial(stage_kernel, width=width),
        out_shape=tuple(jax.ShapeDtypeStruct((a.shape[0], width), BF16) for a in arrays),
        in_specs=[HBM if held else pl.BlockSpec(memory_space=pl.ANY)] * len(arrays),
        out_specs=(VMEM,) * len(arrays),
        scratch_shapes=[pltpu.SemaphoreType.DMA((len(arrays),))],
        compiler_params=params(4),
        name="stage",
    )(*(pltpu.with_memory_space_constraint(a, pltpu.HBM) if held else a for a in arrays))


def gates_kernel(emb_ref, gain_ref, proj_ref, out_ref):
    normed = normalise(emb_ref[...], gain_ref[...])
    projected = jnp.dot(normed, proj_ref[...], preferred_element_type=F32)
    out_ref[...] = silu(projected).astype(BF16)


def gates_of(embedded, gain, proj_in):
    return pl.pallas_call(
        gates_kernel,
        out_shape=jax.ShapeDtypeStruct(embedded.shape, BF16),
        grid=(1,),
        in_specs=[VMEM, VMEM, pl.BlockSpec(proj_in.shape[:1] * 2, lambda i: (0, 1))],
        out_specs=VMEM,
        compiler_params=params(16),
        cost_estimate=pl.CostEstimate(flops=1 << 26, transcendentals=1 << 14, bytes_accessed=1 << 22),
        name="gates",
    )(embedded, gain, proj_in)


def finish_kernel(own_ref, *refs):
    *parts, emb_ref, gates_ref, gain_ref, proj_ref, out_ref = refs
    attended = own_ref[...]
    for p in parts:
        attended = attended + p[...].astype(F32)
    centred = attended - jnp.mean(attended, axis=-1, keepdims=True)
    variance = jnp.mean(centred * centred, axis=-1, keepdims=True)
    gated = centred * lax.rsqrt(variance + 1e-05) * gain_ref[...] * gates_ref[...].astype(F32)
    product = jnp.dot(gated.astype(BF16), proj_ref[...], preferred_element_type=F32)
    out_ref[...] = (emb_ref[...].astype(F32) + product).astype(BF16)


def finish(own, parts, embedded, gates, gain, proj_out):
    return pl.pallas_call(
        finish_kernel,
        out_shape=jax.ShapeDtypeStruct(embedded.shape, BF16),
        in_specs=[VMEM] * (len(parts) + 5),
        out_specs=VMEM,
        compiler_params=params(16),
        name="finish",
    )(own, *parts, embedded, gates, gain, proj_out)


def on_device(
    item_ids,
    item_table,
    key_cache,
    value_cache,
    time_buckets,
    window_start,
    norm_gain,
    proj_in,
    time_bias,
    pos_bias,
    out_gain,
    proj_out,
):
    axis = "hist"
    size = lax.axis_size(axis)
    me = lax.axis_index(axis).astype(jnp.int32)
    each = item_ids.shape[0]
    slots = 2 * each
    heads = time_bias.shape[0]
    events, width = key_cache.shape
    table_rows = item_table.shape[0]
    gain = norm_gain[None, :]

    def place(turn):
        return jnp.stack([me, jnp.asarray(turn, jnp.int32)])

    def partners(x):
        return swap(x, PARTNER, axis, size)

    here = place(0)
    other_table = partners(item_table)
    other_keys = partners(key_cache)
    other_values = partners(value_cache)
    bias, own_table = prepare(
        here, window_start, time_buckets[None, :], time_bias, pos_bias, item_table, 2 * events * size
    )
    other_bias = partners(bias)
    ids = gather_relative(item_ids[None, :], 1, axis, size)

    (near_table,) = stage(width, other_table, held=False)
    found, rounds = lookup(here, ids, [own_table, near_table], slots, size, True)
    pieces = gather_rows(found, axis, size)
    pick = plan(here, ids, slots, table_rows, size)

    def more(state):
        turn, so_far = state
        picked = plan(place(turn), ids, slots, table_rows, size)
        found, _ = lookup(place(turn), ids, [item_table, other_table], slots, size, False)
        return turn + 1, so_far + select(picked, gather_rows(found, axis, size))

    none = jnp.zeros((each * (size // 2), width), BF16)
    _, extra = lax.while_loop(lambda s: s[0] < rounds[0], more, (jnp.int32(1), none))

    keys, values = stage(width, key_cache, value_cache)
    proj, other_keys, other_values = stage(width, proj_in, other_keys, other_values)
    caches = ([keys, other_keys], [values, other_values], [bias, other_bias])
    *far, near = stage_masks(size)
    split = max(1, width // LANES * 7 // 8)
    own, keep, send, later = attend_first(rounds, pick, pieces, extra, gain, proj, *caches, heads, each, split)
    halves = [keep, swap(send, near[0], axis, size)]
    keep, send = attend_later(later, *caches, heads, split)
    halves += [keep, swap(send, near[0], axis, size)]
    gates = gates_of(own, gain, proj_in)

    total, *going = combine(halves, len(combos(far[-1])))
    for bits in far[::-1]:
        parts = [swap(g, m, axis, size) for g, m in zip(going, combos(bits)[1:])]
        if bits is far[0]:
            break
        total, *going = combine([total, sum(p.astype(F32) for p in parts)], len(combos(bits)))
    return finish(total, parts, own, gates, out_gain[None, :], proj_out)


def solution(mesh):
    placed = (
        P(("grp", "hist")),
        P("hist", None),
        P(("grp", "hist"), None),
        P(("grp", "hist"), None),
        P(("grp", "hist")),
        P("grp"),
        P(),
        P(),
        P(),
        P(),
        P(),
        P(),
    )

    return jax.shard_map(on_device, mesh=mesh, in_specs=placed, out_specs=P(("grp", "hist"), None), check_vma=False)
```

profile of v0, /device:TPU:0, one launch (start us, length us, event | category | flops | bytes accessed | tf_op | source)
XLA Modules:
  0.0 75.4 jit_solution(3366154297123014244)
XLA Ops:
  0.0 0.5 collective-permute-start.9
  0.5 0.1 collective-permute-start.15
  0.6 0.4 collective-permute-start.16
  1.7 0.1 pad_add_fusion.1.place_ref
  1.7 2.2 %prepare.1 = (bf16[1024,128]{1,0:T(8,128)(2,1)S(1)}, bf16[1024,1024]{1,0:T(8,128)(2,1)S(1)}) custom-call(s32[2]{0:T(128)S(1)} %pad_add_fusion.1.place_ref, s32[1]{0:T(128)S(6)} %copy.19.start_ref, s32[1,1024]{1,0:T(1,128)} %bitcast.16, f32[16,128]{1,0:T(8,128)} %time_bias_hbm.1, f32[16,18]{1,0:T(8,128)} %pos_bias_hbm.1, bf16[1024,1024]{1,0:T(8,128)(2,1)} %table_hbm.1), custom_call_target="tpu_custom_call" | custom-call | tf_op jit(solution)/shard_map/prepare/pallas_call | solution.py:254
  4.0 0.1 collective-permute-start.17
  4.1 0.0 copy-done.14
  4.1 3.0 %collective-permute-start.5 = (s32[1,16]{1,0:T(1,128)S(1)}, s32[1,16]{1,0:T(1,128)S(1)}, u32[]{:S(2)}, u32[]{:S(2)}) collective-permute-start(s32[1,16]{1,0:T(1,128)S(1)} %bitcast.17), channel_id=1, source_target_pairs={{0,4},{1,5},{2,6},{3,7},{4,0},{5,1},{6,2},{7,3},{8,12},{9,13},{10,... | collective-permute-start | bytes 200 | tf_op jit(solution)/shard_map/ppermute | solution.py:46
  7.1 1.5 %collective-permute-done.5 = s32[1,16]{1,0:T(1,128)S(1)} collective-permute-done((s32[1,16]{1,0:T(1,128)S(1)}, s32[1,16]{1,0:T(1,128)S(1)}, u32[]{:S(2)}, u32[]{:S(2)}) %collective-permute-start.5) | collective-permute-done | bytes 96 | tf_op jit(solution)/shard_map/ppermute | solution.py:46
  8.6 3.0 %collective-permute-start.6 = (s32[1,16]{1,0:T(1,128)S(1)}, s32[1,16]{1,0:T(1,128)S(1)}, u32[]{:S(2)}, u32[]{:S(2)}) collective-permute-start(s32[1,16]{1,0:T(1,128)S(1)} %bitcast.18), channel_id=1, source_target_pairs={{0,8},{1,9},{2,10},{3,11},{4,12},{5,13},{6,14},{7,15},{8,0},{9,1},... | collective-permute-start | bytes 200 | tf_op jit(solution)/shard_map/ppermute | solution.py:46
  11.7 1.5 %collective-permute-done.6 = s32[1,16]{1,0:T(1,128)S(1)} collective-permute-done((s32[1,16]{1,0:T(1,128)S(1)}, s32[1,16]{1,0:T(1,128)S(1)}, u32[]{:S(2)}, u32[]{:S(2)}) %collective-permute-start.6) | collective-permute-done | bytes 96 | tf_op jit(solution)/shard_map/ppermute | solution.py:46
  13.2 3.9 %collective-permute-start.7 = (s32[1,16]{1,0:T(1,128)S(1)}, s32[1,16]{1,0:T(1,128)S(1)}, u32[]{:S(2)}, u32[]{:S(2)}) collective-permute-start(s32[1,16]{1,0:T(1,128)S(1)} %bitcast.19), channel_id=1, source_target_pairs={{0,12},{1,13},{2,14},{3,15},{4,8},{5,9},{6,10},{7,11},{8,4},{9,5},... | collective-permute-start | bytes 200 | tf_op jit(solution)/shard_map/ppermute | solution.py:46
  17.2 1.5 %collective-permute-done.7 = s32[1,16]{1,0:T(1,128)S(1)} collective-permute-done((s32[1,16]{1,0:T(1,128)S(1)}, s32[1,16]{1,0:T(1,128)S(1)}, u32[]{:S(2)}, u32[]{:S(2)}) %collective-permute-start.7) | collective-permute-done | bytes 96 | tf_op jit(solution)/shard_map/ppermute | solution.py:46
  18.7 0.1 pad_add_fusion.2.refs_0_
  18.8 1.7 %collective-permute-start.8 = (s32[1,64]{1,0:T(1,128)S(1)}, s32[1,64]{1,0:T(1,128)S(1)}, u32[]{:S(2)}, u32[]{:S(2)}) collective-permute-start(s32[1,64]{1,0:T(1,128)S(1)} %pad_add_fusion.2.refs_0_), channel_id=1, source_target_pairs={{0,2},{1,3},{2,0},{3,1},{4,6},{5,7},{6,4},{7,5},{8,10},{9,11},{10,... | collective-permute-start | bytes 776 | tf_op jit(solution)/shard_map/ppermute | solution.py:46
  20.5 0.0 collective-permute-done.9.refs_0_
  20.5 1.6 %stage.3.refs_3_ = bf16[1024,1024]{1,0:T(8,128)(2,1)S(1)} custom-call(bf16[1024,1024]{1,0:T(8,128)(2,1)} %collective-permute-done.9.refs_0_), custom_call_target="tpu_custom_call" | custom-call | tf_op jit(solution)/shard_map/stage/pallas_call | solution.py:467
  22.1 0.2 collective-permute-done.8.refs_1_
  22.4 1.6 %lookup.2 = (bf16[32,1024]{1,0:T(8,128)(2,1)S(1)}, s32[1]{0:T(128)}) custom-call(s32[2]{0:T(128)S(1)} %pad_add_fusion.1.place_ref, s32[1,64]{1,0:T(1,128)S(1)} %pad_add_fusion.2.refs_0_, s32[1,64]{1,0:T(1,128)S(1)} %collective-permute-done.8.refs_1_, bf16[1024,1024]{1,0:T(8,128)(2,1)S(1)} %get-tuple-element.68.refs_2_, bf16[1024,1024]{1,0:T(8,128)(2,1)S(1)} %stage.3.refs_3_), custom_call_target="tpu_custom_call" | custom-call | tf_op jit(solution)/shard_map/lookup/pallas_call | solution.py:155
  24.0 0.1 collective-permute-start.10
  24.0 4.4 %collective-permute-start.11 = (bf16[32,1024]{1,0:T(8,128)(2,1)S(1)}, bf16[32,1024]{1,0:T(8,128)(2,1)S(1)}, u32[]{:S(2)}, u32[]{:S(2)}) collective-permute-start(bf16[32,1024]{1,0:T(8,128)(2,1)S(1)} %get-tuple-element.70.refs_0_), channel_id=1, source_target_pairs={{0,8},{1,9},{2,10},{3,11},{4,12},{5,13},{6,14},{7,15},{8,0},{9,1},... | collective-permute-start | bytes 196616 | tf_op jit(solution)/shard_map/ppermute | solution.py:46
  28.4 0.0 collective-permute-done.15.refs_1_
  28.4 0.0 collective-permute-start.12
  28.4 2.2 %stage.5 = (bf16[1024,1024]{1,0:T(8,128)(2,1)S(1)}, bf16[1024,1024]{1,0:T(8,128)(2,1)S(1)}) custom-call(bf16[1024,1024]{1,0:T(8,128)(2,1)} %refs_0_.3, bf16[1024,1024]{1,0:T(8,128)(2,1)} %refs_1_.1), custom_call_target="tpu_custom_call" | custom-call | tf_op jit(solution)/shard_map/stage/pallas_call | solution.py:467
  30.7 0.0 copy-start.1
  30.7 1.3 %copy-done.1 = bf16[1024,1024]{1,0:T(8,128)(2,1)} copy-done((bf16[1024,1024]{1,0:T(8,128)(2,1)}, bf16[1024,1024]{1,0:T(8,128)(2,1)S(1)}, u32[]{:S(2)}) %copy-start.1) | copy-done | bytes 2097176
  32.0 0.9 %plan.2.pick_ref = bf16[128,256]{1,0:T(8,128)(2,1)S(1)} custom-call(s32[2]{0:T(128)S(1)} %pad_add_fusion.1.place_ref, s32[1,64]{1,0:T(1,128)S(1)} %pad_add_fusion.2.refs_0_, s32[1,64]{1,0:T(1,128)S(1)} %collective-permute-done.8.refs_1_), custom_call_target="tpu_custom_call" | custom-call | tf_op jit(solution)/shard_map/plan/pallas_call | solution.py:191
  32.9 0.0 collective-permute-done.16.refs_2_
  32.9 2.9 %stage.4 = (bf16[1024,1024]{1,0:T(8,128)(2,1)S(1)}, bf16[1024,1024]{1,0:T(8,128)(2,1)S(1)}, bf16[1024,1024]{1,0:T(8,128)(2,1)S(1)}) custom-call(bf16[1024,2048]{1,0:T(8,128)(2,1)} %proj_ref.1, bf16[1024,1024]{1,0:T(8,128)(2,1)} %collective-permute-done.15.refs_1_, bf16[1024,1024]{1,0:T(8,128)(2,1)} %collective-permute-done.16.refs_2_), custom_call_target="tpu_custom_call" | custom-call | tf_op jit(solution)/shard_map/stage/pallas_call | solution.py:467
  35.8 0.0 copy-start.4
  35.8 1.3 %copy-done.4 = bf16[1024,1024]{1,0:T(8,128)(2,1)} copy-done((bf16[1024,1024]{1,0:T(8,128)(2,1)}, bf16[1024,1024]{1,0:T(8,128)(2,1)S(1)}, u32[]{:S(2)}) %copy-start.4) | copy-done | bytes 2097176
  37.1 1.3 %copy-done.7 = bf16[1024,1024]{1,0:T(8,128)(2,1)} copy-done((bf16[1024,1024]{1,0:T(8,128)(2,1)}, bf16[1024,1024]{1,0:T(8,128)(2,1)S(1)}, u32[]{:S(2)}) %copy-start.7) | copy-done | bytes 2097176
  38.5 1.4 %copy-done.10 = bf16[1024,1024]{1,0:T(8,128)(2,1)} copy-done((bf16[1024,1024]{1,0:T(8,128)(2,1)}, bf16[1024,1024]{1,0:T(8,128)(2,1)S(1)}, u32[]{:S(2)}) %copy-start.10) | copy-done | bytes 2097176
  39.8 1.7 %collective-permute-start.13 = (bf16[32,1024]{1,0:T(8,128)(2,1)S(1)}, bf16[32,1024]{1,0:T(8,128)(2,1)S(1)}, u32[]{:S(2)}, u32[]{:S(2)}) collective-permute-start(bf16[32,1024]{1,0:T(8,128)(2,1)S(1)} %get-tuple-element.70.refs_0_), channel_id=1, source_target_pairs={{0,2},{1,3},{2,0},{3,1},{4,6},{5,7},{6,4},{7,5},{8,10},{9,11},{10,... | collective-permute-start | bytes 196616 | tf_op jit(solution)/shard_map/ppermute | solution.py:46
  41.6 0.0 collective-permute-done.10.refs_0_
  41.6 0.0 collective-permute-done.11.refs_1_
  41.6 0.0 collective-permute-done.12.refs_2_
  41.6 0.4 collective-permute-start.14
  42.0 0.0 collective-permute-done.17.refs_12_.refs_5_
  42.0 0.7 broadcast_in_dim.17
  42.7 0.7 while.10
  43.4 0.7 collective-permute-done.13.refs_2_
  44.1 3.2 %collective-permute-done.14.refs_3_ = bf16[96,1024]{1,0:T(8,128)(2,1)S(1)} collective-permute-done((bf16[96,1024]{1,0:T(8,128)(2,1)S(1)}, bf16[96,1024]{1,0:T(8,128)(2,1)S(1)}, u32[]{:S(2)}, u32[]{:S(2)}) %collective-permute-start.14) | collective-permute-done | bytes 196640 | tf_op jit(solution)/shard_map/ppermute | solution.py:46
  47.3 0.0 copy-done.12
  47.4 1.6 %copy-done.2 = bf16[1024,1024]{1,0:T(8,128)(2,1)S(1)} copy-done((bf16[1024,1024]{1,0:T(8,128)(2,1)S(1)}, bf16[1024,1024]{1,0:T(8,128)(2,1)}, u32[]{:S(2)}) %copy-start.2) | copy-done | bytes 2097176
  48.9 1.6 %copy-done.5 = bf16[1024,1024]{1,0:T(8,128)(2,1)S(1)} copy-done((bf16[1024,1024]{1,0:T(8,128)(2,1)S(1)}, bf16[1024,1024]{1,0:T(8,128)(2,1)}, u32[]{:S(2)}) %copy-start.5) | copy-done | bytes 2097176
  50.5 1.6 %copy-done.8 = bf16[1024,1024]{1,0:T(8,128)(2,1)S(1)} copy-done((bf16[1024,1024]{1,0:T(8,128)(2,1)S(1)}, bf16[1024,1024]{1,0:T(8,128)(2,1)}, u32[]{:S(2)}) %copy-start.8) | copy-done | bytes 2097176
  52.1 1.6 %copy-done.11 = bf16[1024,1024]{1,0:T(8,128)(2,1)S(1)} copy-done((bf16[1024,1024]{1,0:T(8,128)(2,1)S(1)}, bf16[1024,1024]{1,0:T(8,128)(2,1)}, u32[]{:S(2)}) %copy-start.11) | copy-done | bytes 2097176
  53.7 5.1 %attend_first.1 = (bf16[16,1024]{1,0:T(8,128)(2,1)S(1)}, f32[64,896]{1,0:T(8,128)S(1)}, bf16[64,896]{1,0:T(8,128)(2,1)S(1)}, bf16[128,128]{1,0:T(8,128)(2,1)S(1)}) custom-call(s32[1]{0:T(128)} %get-tuple-element.158.rounds_ref, bf16[128,256]{1,0:T(8,128)(2,1)S(1)} %plan.2.pick_ref, bf16[32,1024]{1,0:T(8,128)(2,1)S(1)} %get-tuple-element.70.refs_0_, ...), custom_call_target="tpu_custom_call" | custom-call | flops 1879048192 | bytes 7340032 | tf_op jit(solution)/shard_map/attend_first/pallas_call | solution.py:387
  58.9 0.7 collective-permute-start.18
  59.5 0.0 copy-done.3
  59.5 0.0 copy-done.6
  59.5 0.9 %attend_later.1 = (f32[64,128]{1,0:T(8,128)S(1)}, bf16[64,128]{1,0:T(8,128)(2,1)S(1)}) custom-call(bf16[128,128]{1,0:T(8,128)(2,1)S(1)} %get-tuple-element.80.query_ref, bf16[1024,1024]{1,0:T(8,128)(2,1)S(1)} %get-tuple-element.73.refs_7_.refs_0_, bf16[1024,1024]{1,0:T(8,128)(2,1)S(1)} %copy-done.6, bf16[1024,1024]{1,0:T(8,128)(2,1)S(1)} %copy-done.3, ...), custom_call_target="tpu_custom_call" | custom-call | flops 268435456 | bytes 1048576 | tf_op jit(solution)/shard_map/attend_later/pallas_call | solution.py:411
  60.4 1.5 %collective-permute-start.19 = (bf16[64,128]{1,0:T(8,128)(2,1)S(1)}, bf16[64,128]{1,0:T(8,128)(2,1)S(1)}, u32[]{:S(2)}, u32[]{:S(2)}) collective-permute-start(bf16[64,128]{1,0:T(8,128)(2,1)S(1)} %get-tuple-element.82), channel_id=1, source_target_pairs={{0,2},{1,3},{2,0},{3,1},{4,6},{5,7},{6,4},{7,5},{8,10},{9,11},{10,... | collective-permute-start | bytes 49160 | tf_op jit(solution)/shard_map/ppermute | solution.py:46
  61.9 2.3 %collective-permute-done.19.refs_3_ = bf16[64,128]{1,0:T(8,128)(2,1)S(1)} collective-permute-done((bf16[64,128]{1,0:T(8,128)(2,1)S(1)}, bf16[64,128]{1,0:T(8,128)(2,1)S(1)}, u32[]{:S(2)}, u32[]{:S(2)}) %collective-permute-start.19) | collective-permute-done | bytes 16416 | tf_op jit(solution)/shard_map/ppermute | solution.py:46
  64.2 0.0 collective-permute-done.18.refs_1_
  64.3 0.4 collective-permute-start.20
  64.7 3.8 %collective-permute-start.21 = (bf16[16,1024]{1,0:T(8,128)(2,1)S(1)}, bf16[16,1024]{1,0:T(8,128)(2,1)S(1)}, u32[]{:S(2)}, u32[]{:S(2)}) collective-permute-start(bf16[16,1024]{1,0:T(8,128)(2,1)S(1)} %get-tuple-element.85), channel_id=1, source_target_pairs={{0,8},{1,9},{2,10},{3,11},{4,12},{5,13},{6,14},{7,15},{8,0},{9,1},... | collective-permute-start | bytes 98312 | tf_op jit(solution)/shard_map/ppermute | solution.py:46
  68.5 0.2 collective-permute-start.22
  68.7 0.5 gates.1.refs_4_
  69.2 0.0 collective-permute-done.20.refs_0_
  69.2 1.5 %collective-permute-done.21.refs_1_ = bf16[16,1024]{1,0:T(8,128)(2,1)S(1)} collective-permute-done((bf16[16,1024]{1,0:T(8,128)(2,1)S(1)}, bf16[16,1024]{1,0:T(8,128)(2,1)S(1)}, u32[]{:S(2)}, u32[]{:S(2)}) %collective-permute-start.21) | collective-permute-done | bytes 32800 | tf_op jit(solution)/shard_map/ppermute | solution.py:46
  70.8 3.5 %collective-permute-done.22.refs_2_ = bf16[16,1024]{1,0:T(8,128)(2,1)S(1)} collective-permute-done((bf16[16,1024]{1,0:T(8,128)(2,1)S(1)}, bf16[16,1024]{1,0:T(8,128)(2,1)S(1)}, u32[]{:S(2)}, u32[]{:S(2)}) %collective-permute-start.22) | collective-permute-done | bytes 32800 | tf_op jit(solution)/shard_map/ppermute | solution.py:46
  74.2 1.2 %finish.1 = bf16[16,1024]{1,0:T(8,128)(2,1)} custom-call(f32[16,1024]{1,0:T(8,128)S(1)} %get-tuple-element.83.own_ref, bf16[16,1024]{1,0:T(8,128)(2,1)S(1)} %collective-permute-done.20.refs_0_, bf16[16,1024]{1,0:T(8,128)(2,1)S(1)} %collective-permute-done.21.refs_1_, bf16[16,1024]{1,0:T(8,128)(2,1)S(1)} %collective-permute-done.22.refs_2_, ...), custom_call_target="tpu_custom_call" | custom-call | tf_op jit(solution)/shard_map/finish/pallas_call | solution.py:510
  (18 shorter events, 0.1 us)
Async XLA Ops:
  0.0 4.1 %copy-start.14 = (s32[16]{0:T(128)S(1)}, s32[16]{0:T(128)}, u32[]{:S(2)}) copy-start(s32[16]{0:T(128)} %param.14) | copy-start | bytes 196
  0.0 20.5 %collective-permute-start.9 = (bf16[1024,1024]{1,0:T(8,128)(2,1)}, bf16[1024,1024]{1,0:T(8,128)(2,1)}, u32[]{:S(2)}, u32[]{:S(2)}) collective-permute-start(bf16[1024,1024]{1,0:T(8,128)(2,1)} %table_hbm.1), channel_id=1, source_target_pairs={{0,1},{1,0},{2,3},{3,2},{4,5},{5,4},{6,7},{7,6},{8,9},{9,8},{10,11... | collective-permute-start | bytes 6291464 | tf_op jit(solution)/shard_map/ppermute | solution.py:46
  0.5 27.9 %collective-permute-start.15 = (bf16[1024,1024]{1,0:T(8,128)(2,1)}, bf16[1024,1024]{1,0:T(8,128)(2,1)}, u32[]{:S(2)}, u32[]{:S(2)}) collective-permute-start(bf16[1024,1024]{1,0:T(8,128)(2,1)} %refs_0_.3), channel_id=1, source_target_pairs={{0,1},{1,0},{2,3},{3,2},{4,5},{5,4},{6,7},{7,6},{8,9},{9,8},{10,11... | collective-permute-start | bytes 6291464 | tf_op jit(solution)/shard_map/ppermute | solution.py:46
  0.6 32.3 %collective-permute-start.16 = (bf16[1024,1024]{1,0:T(8,128)(2,1)}, bf16[1024,1024]{1,0:T(8,128)(2,1)}, u32[]{:S(2)}, u32[]{:S(2)}) collective-permute-start(bf16[1024,1024]{1,0:T(8,128)(2,1)} %refs_1_.1), channel_id=1, source_target_pairs={{0,1},{1,0},{2,3},{3,2},{4,5},{5,4},{6,7},{7,6},{8,9},{9,8},{10,11... | collective-permute-start | bytes 6291464 | tf_op jit(solution)/shard_map/ppermute | solution.py:46
  4.0 38.0 %collective-permute-start.17 = (bf16[1024,128]{1,0:T(8,128)(2,1)S(1)}, bf16[1024,128]{1,0:T(8,128)(2,1)S(1)}, u32[]{:S(2)}, u32[]{:S(2)}) collective-permute-start(bf16[1024,128]{1,0:T(8,128)(2,1)S(1)} %get-tuple-element.77.refs_11_.refs_4_), channel_id=1, source_target_pairs={{0,1},{1,0},{2,3},{3,2},{4,5},{5,4},{6,7},{7,6},{8,9},{9,8},{10,11... | collective-permute-start | bytes 786440 | tf_op jit(solution)/shard_map/ppermute | solution.py:46
  4.1 4.6 %collective-permute-start.5 = (s32[1,16]{1,0:T(1,128)S(1)}, s32[1,16]{1,0:T(1,128)S(1)}, u32[]{:S(2)}, u32[]{:S(2)}) collective-permute-start(s32[1,16]{1,0:T(1,128)S(1)} %bitcast.17), channel_id=1, source_target_pairs={{0,4},{1,5},{2,6},{3,7},{4,0},{5,1},{6,2},{7,3},{8,12},{9,13},{10,... | collective-permute-start | bytes 200 | tf_op jit(solution)/shard_map/ppermute | solution.py:46
  8.6 4.6 %collective-permute-start.6 = (s32[1,16]{1,0:T(1,128)S(1)}, s32[1,16]{1,0:T(1,128)S(1)}, u32[]{:S(2)}, u32[]{:S(2)}) collective-permute-start(s32[1,16]{1,0:T(1,128)S(1)} %bitcast.18), channel_id=1, source_target_pairs={{0,8},{1,9},{2,10},{3,11},{4,12},{5,13},{6,14},{7,15},{8,0},{9,1},... | collective-permute-start | bytes 200 | tf_op jit(solution)/shard_map/ppermute | solution.py:46
  13.2 5.5 %collective-permute-start.7 = (s32[1,16]{1,0:T(1,128)S(1)}, s32[1,16]{1,0:T(1,128)S(1)}, u32[]{:S(2)}, u32[]{:S(2)}) collective-permute-start(s32[1,16]{1,0:T(1,128)S(1)} %bitcast.19), channel_id=1, source_target_pairs={{0,12},{1,13},{2,14},{3,15},{4,8},{5,9},{6,10},{7,11},{8,4},{9,5},... | collective-permute-start | bytes 200 | tf_op jit(solution)/shard_map/ppermute | solution.py:46
  18.8 3.6 %collective-permute-start.8 = (s32[1,64]{1,0:T(1,128)S(1)}, s32[1,64]{1,0:T(1,128)S(1)}, u32[]{:S(2)}, u32[]{:S(2)}) collective-permute-start(s32[1,64]{1,0:T(1,128)S(1)} %pad_add_fusion.2.refs_0_), channel_id=1, source_target_pairs={{0,2},{1,3},{2,0},{3,1},{4,6},{5,7},{6,4},{7,5},{8,10},{9,11},{10,... | collective-permute-start | bytes 776 | tf_op jit(solution)/shard_map/ppermute | solution.py:46
  24.0 17.6 %collective-permute-start.10 = (bf16[32,1024]{1,0:T(8,128)(2,1)S(1)}, bf16[32,1024]{1,0:T(8,128)(2,1)S(1)}, u32[]{:S(2)}, u32[]{:S(2)}) collective-permute-start(bf16[32,1024]{1,0:T(8,128)(2,1)S(1)} %get-tuple-element.70.refs_0_), channel_id=1, source_target_pairs={{0,4},{1,5},{2,6},{3,7},{4,0},{5,1},{6,2},{7,3},{8,12},{9,13},{10,... | collective-permute-start | bytes 196616 | tf_op jit(solution)/shard_map/ppermute | solution.py:46
  24.0 17.5 %collective-permute-start.11 = (bf16[32,1024]{1,0:T(8,128)(2,1)S(1)}, bf16[32,1024]{1,0:T(8,128)(2,1)S(1)}, u32[]{:S(2)}, u32[]{:S(2)}) collective-permute-start(bf16[32,1024]{1,0:T(8,128)(2,1)S(1)} %get-tuple-element.70.refs_0_), channel_id=1, source_target_pairs={{0,8},{1,9},{2,10},{3,11},{4,12},{5,13},{6,14},{7,15},{8,0},{9,1},... | collective-permute-start | bytes 196616 | tf_op jit(solution)/shard_map/ppermute | solution.py:46
  28.4 13.2 %collective-permute-start.12 = (bf16[32,1024]{1,0:T(8,128)(2,1)S(1)}, bf16[32,1024]{1,0:T(8,128)(2,1)S(1)}, u32[]{:S(2)}, u32[]{:S(2)}) collective-permute-start(bf16[32,1024]{1,0:T(8,128)(2,1)S(1)} %get-tuple-element.70.refs_0_), channel_id=1, source_target_pairs={{0,12},{1,13},{2,14},{3,15},{4,8},{5,9},{6,10},{7,11},{8,4},{9,5},... | collective-permute-start | bytes 196616 | tf_op jit(solution)/shard_map/ppermute | solution.py:46
  30.7 1.3 %copy-start.1 = (bf16[1024,1024]{1,0:T(8,128)(2,1)}, bf16[1024,1024]{1,0:T(8,128)(2,1)S(1)}, u32[]{:S(2)}) copy-start(bf16[1024,1024]{1,0:T(8,128)(2,1)S(1)} %get-tuple-element.75.refs_9_.refs_2_) | copy-start | bytes 6291460
  35.8 1.3 %copy-start.4 = (bf16[1024,1024]{1,0:T(8,128)(2,1)}, bf16[1024,1024]{1,0:T(8,128)(2,1)S(1)}, u32[]{:S(2)}) copy-start(bf16[1024,1024]{1,0:T(8,128)(2,1)S(1)} %get-tuple-element.74.refs_8_.refs_1_) | copy-start | bytes 6291460
  37.1 1.3 %copy-start.7 = (bf16[1024,1024]{1,0:T(8,128)(2,1)}, bf16[1024,1024]{1,0:T(8,128)(2,1)S(1)}, u32[]{:S(2)}) copy-start(bf16[1024,1024]{1,0:T(8,128)(2,1)S(1)} %get-tuple-element.76.refs_10_.refs_3_) | copy-start | bytes 6291460
  38.4 1.4 %copy-start.10 = (bf16[1024,1024]{1,0:T(8,128)(2,1)}, bf16[1024,1024]{1,0:T(8,128)(2,1)S(1)}, u32[]{:S(2)}) copy-start(bf16[1024,1024]{1,0:T(8,128)(2,1)S(1)} %get-tuple-element.72.refs_6_) | copy-start | bytes 6291460
  39.8 4.3 %collective-permute-start.13 = (bf16[32,1024]{1,0:T(8,128)(2,1)S(1)}, bf16[32,1024]{1,0:T(8,128)(2,1)S(1)}, u32[]{:S(2)}, u32[]{:S(2)}) collective-permute-start(bf16[32,1024]{1,0:T(8,128)(2,1)S(1)} %get-tuple-element.70.refs_0_), channel_id=1, source_target_pairs={{0,2},{1,3},{2,0},{3,1},{4,6},{5,7},{6,4},{7,5},{8,10},{9,11},{10,... | collective-permute-start | bytes 196616 | tf_op jit(solution)/shard_map/ppermute | solution.py:46
  41.6 5.7 %collective-permute-start.14 = (bf16[96,1024]{1,0:T(8,128)(2,1)S(1)}, bf16[96,1024]{1,0:T(8,128)(2,1)S(1)}, u32[]{:S(2)}, u32[]{:S(2)}) collective-permute-start(bf16[96,1024]{1,0:T(8,128)(2,1)S(1)} %join.2.refs_1_), channel_id=1, source_target_pairs={{0,2},{1,3},{2,0},{3,1},{4,6},{5,7},{6,4},{7,5},{8,10},{9,11},{10,... | collective-permute-start | bytes 589832 | tf_op jit(solution)/shard_map/ppermute | solution.py:46
  42.7 4.6 %copy-start.12 = (f32[1024]{0:T(1024)S(1)}, f32[1024]{0:T(1024)}, u32[]{:S(2)}) copy-start(f32[1024]{0:T(1024)} %param.20) | copy-start | bytes 12292
  47.4 1.6 %copy-start.2 = (bf16[1024,1024]{1,0:T(8,128)(2,1)S(1)}, bf16[1024,1024]{1,0:T(8,128)(2,1)}, u32[]{:S(2)}) copy-start(bf16[1024,1024]{1,0:T(8,128)(2,1)} %copy-done.1) | copy-start | bytes 6291460
  48.9 1.6 %copy-start.5 = (bf16[1024,1024]{1,0:T(8,128)(2,1)S(1)}, bf16[1024,1024]{1,0:T(8,128)(2,1)}, u32[]{:S(2)}) copy-start(bf16[1024,1024]{1,0:T(8,128)(2,1)} %copy-done.4) | copy-start | bytes 6291460
  50.5 1.6 %copy-start.8 = (bf16[1024,1024]{1,0:T(8,128)(2,1)S(1)}, bf16[1024,1024]{1,0:T(8,128)(2,1)}, u32[]{:S(2)}) copy-start(bf16[1024,1024]{1,0:T(8,128)(2,1)} %copy-done.7) | copy-start | bytes 6291460
  52.1 1.6 %copy-start.11 = (bf16[1024,1024]{1,0:T(8,128)(2,1)S(1)}, bf16[1024,1024]{1,0:T(8,128)(2,1)}, u32[]{:S(2)}) copy-start(bf16[1024,1024]{1,0:T(8,128)(2,1)} %copy-done.10) | copy-start | bytes 6291460
  53.7 5.8 %copy-start.3 = (bf16[1024,1024]{1,0:T(8,128)(2,1)S(1)}, bf16[1024,1024]{1,0:T(8,128)(2,1)}, u32[]{:S(2)}) copy-start(bf16[1024,1024]{1,0:T(8,128)(2,1)} %copy-done.1) | copy-start | bytes 6291460
  53.7 5.8 %copy-start.6 = (bf16[1024,1024]{1,0:T(8,128)(2,1)S(1)}, bf16[1024,1024]{1,0:T(8,128)(2,1)}, u32[]{:S(2)}) copy-start(bf16[1024,1024]{1,0:T(8,128)(2,1)} %copy-done.4) | copy-start | bytes 6291460
  58.9 5.4 %collective-permute-start.18 = (bf16[64,896]{1,0:T(8,128)(2,1)S(1)}, bf16[64,896]{1,0:T(8,128)(2,1)S(1)}, u32[]{:S(2)}, u32[]{:S(2)}) collective-permute-start(bf16[64,896]{1,0:T(8,128)(2,1)S(1)} %get-tuple-element.79), channel_id=1, source_target_pairs={{0,2},{1,3},{2,0},{3,1},{4,6},{5,7},{6,4},{7,5},{8,10},{9,11},{10,... | collective-permute-start | bytes 344072 | tf_op jit(solution)/shard_map/ppermute | solution.py:46
  59.5 9.2 %copy-start = (bf16[1024,2048]{1,0:T(8,128)(2,1)S(1)}, bf16[1024,2048]{1,0:T(8,128)(2,1)}, u32[]{:S(2)}) copy-start(bf16[1024,2048]{1,0:T(8,128)(2,1)} %proj_ref.1) | copy-start | bytes 12582916
  60.4 3.8 %collective-permute-start.19 = (bf16[64,128]{1,0:T(8,128)(2,1)S(1)}, bf16[64,128]{1,0:T(8,128)(2,1)S(1)}, u32[]{:S(2)}, u32[]{:S(2)}) collective-permute-start(bf16[64,128]{1,0:T(8,128)(2,1)S(1)} %get-tuple-element.82), channel_id=1, source_target_pairs={{0,2},{1,3},{2,0},{3,1},{4,6},{5,7},{6,4},{7,5},{8,10},{9,11},{10,... | collective-permute-start | bytes 49160 | tf_op jit(solution)/shard_map/ppermute | solution.py:46
  64.3 4.9 %collective-permute-start.20 = (bf16[16,1024]{1,0:T(8,128)(2,1)S(1)}, bf16[16,1024]{1,0:T(8,128)(2,1)S(1)}, u32[]{:S(2)}, u32[]{:S(2)}) collective-permute-start(bf16[16,1024]{1,0:T(8,128)(2,1)S(1)} %get-tuple-element.84), channel_id=1, source_target_pairs={{0,4},{1,5},{2,6},{3,7},{4,0},{5,1},{6,2},{7,3},{8,12},{9,13},{10,... | collective-permute-start | bytes 98312 | tf_op jit(solution)/shard_map/ppermute | solution.py:46
  64.7 6.1 %collective-permute-start.21 = (bf16[16,1024]{1,0:T(8,128)(2,1)S(1)}, bf16[16,1024]{1,0:T(8,128)(2,1)S(1)}, u32[]{:S(2)}, u32[]{:S(2)}) collective-permute-start(bf16[16,1024]{1,0:T(8,128)(2,1)S(1)} %get-tuple-element.85), channel_id=1, source_target_pairs={{0,8},{1,9},{2,10},{3,11},{4,12},{5,13},{6,14},{7,15},{8,0},{9,1},... | collective-permute-start | bytes 98312 | tf_op jit(solution)/shard_map/ppermute | solution.py:46
  68.5 5.7 %collective-permute-start.22 = (bf16[16,1024]{1,0:T(8,128)(2,1)S(1)}, bf16[16,1024]{1,0:T(8,128)(2,1)S(1)}, u32[]{:S(2)}, u32[]{:S(2)}) collective-permute-start(bf16[16,1024]{1,0:T(8,128)(2,1)S(1)} %get-tuple-element.86), channel_id=1, source_target_pairs={{0,12},{1,13},{2,14},{3,15},{4,8},{5,9},{6,10},{7,11},{8,4},{9,5},... | collective-permute-start | bytes 98312 | tf_op jit(solution)/shard_map/ppermute | solution.py:46
  68.7 5.5 %copy-start.9 = (bf16[1024,1024]{1,0:T(8,128)(2,1)S(1)}, bf16[1024,1024]{1,0:T(8,128)(2,1)}, u32[]{:S(2)}) copy-start(bf16[1024,1024]{1,0:T(8,128)(2,1)} %refs_6_.1) | copy-start | bytes 6291460
  68.7 5.5 %copy-start.13 = (f32[1024]{0:T(1024)S(1)}, f32[1024]{0:T(1024)}, u32[]{:S(2)}) copy-start(f32[1024]{0:T(1024)} %param.24) | copy-start | bytes 12292
where the time goes:
time: 75.7 us; the launch traced here: 75.4 us
  starting transfers between devices  26 us (34%)
  Pallas kernels  19.1 us (25%)
  waiting for transfers between devices  16.1 us (21%)
  local copies, waits for them, and re-layouts  12.5 us (17%)
  between operations  0.82 us (1%)
    ppermute x18, starting transfers between devices, swap(): return lax.ppermute(x, axis, [(i, i ^ mask) for i in range(size)])  26 us
    ppermute x18, waiting for transfers between devices, swap(): return lax.ppermute(x, axis, [(i, i ^ mask) for i in range(size)])  16.1 us
    unnamed x30, local copies, waits for them, and re-layouts  11.8 us
    pallas_call x3, Pallas kernels, stage(): pl.pallas_call(functools.partial(stage_kernel, width=width), out_shape=tu...  6.73 us
    pallas_call x1, Pallas kernels, attend_first(): pl.pallas_call(functools.partial(attend_first_kernel, heads=heads, blocks...  5.13 us
    pallas_call x1, Pallas kernels, prepare(): pl.pallas_call(functools.partial(prepare_kernel, npos=pos_bias.shape[1],...  2.21 us
    pallas_call x1, Pallas kernels, lookup(): pl.pallas_call(functools.partial(lookup_kernel, size=size, resident=resid...  1.6 us
  transfers between devices with their start and end apart: 18, of which 9 were waited for; matrix products, arithmetic and copies ran while one was open for 1% of the time, Pallas kernels for 17%

commit v1 on v0

--- a/solution.py
+++ b/solution.py
@@ -108,19 +108,20 @@
     return jnp.sum(jnp.where(r == c, row, 0), axis=1, keepdims=True)
 
 
-def lookup_kernel(place_ref, *refs, size, resident):
-    if resident:
-        *ids_refs, own_ref, other_ref, out_ref, rounds_ref, blocks_ref = refs
-        copies = []
+def lookup_kernel(*refs, axis, size, first_turn):
+    if first_turn:
+        *ids_refs, own_ref, other_ref, out_ref, blocks_ref = refs
+        turn, copies = 0, []
     else:
-        *ids_refs, own_hbm, other_hbm, out_ref, rounds_ref, blocks_ref, own_ref, other_ref, sems = refs
+        turn_ref, *ids_refs, own_hbm, other_hbm, out_ref, blocks_ref, own_ref, other_ref, sems = refs
+        turn = turn_ref[0]
         copies = [
             pltpu.make_async_copy(own_hbm, own_ref, sems.at[0]),
             pltpu.make_async_copy(other_hbm, other_ref, sems.at[1]),
         ]
     for c in copies:
         c.start()
-    me, turn = place_ref[0], place_ref[1]
+    me = lax.axis_index(axis)
     slots = out_ref.shape[0]
     rows = own_ref.shape[0]
     pair, key, offset = candidates_info(ids_refs, me, size, rows)
@@ -131,7 +132,6 @@
     slot = lax.broadcasted_iota(jnp.int32, (slots, count), 0) + turn * slots
     hit = (pair == (me >> 1)) & (rank == slot)
     want = jnp.sum(jnp.where(hit, offset + 1, 0), axis=1, keepdims=True) - 1
-    rounds_ref[0] = jnp.max(rank) // slots + 1
     for c in copies:
         c.wait()
     near = jnp.where(want < 0, 0, want // BLOCK)
@@ -148,34 +148,38 @@
     out_ref[...] = found.astype(BF16)
 
 
-def lookup(place, ids, tables, slots, size, resident):
-    if not resident:
+def lookup(ids, tables, slots, axis, size, turn=None):
+    first_turn = turn is None
+    if not first_turn:
         tables = [pltpu.with_memory_space_constraint(t, pltpu.HBM) for t in tables]
     rows, width = tables[0].shape
     return pl.pallas_call(
-        functools.partial(lookup_kernel, size=size, resident=resident),
-        out_shape=(
-            jax.ShapeDtypeStruct((slots, width), BF16),
-            jax.ShapeDtypeStruct((1,), jnp.int32),
-        ),
-        in_specs=[SMEM] + [VMEM] * len(ids) + [VMEM if resident else HBM] * 2,
-        out_specs=(VMEM, SMEM),
+        functools.partial(lookup_kernel, axis=axis, size=size, first_turn=first_turn),
+        out_shape=jax.ShapeDtypeStruct((slots, width), BF16),
+        in_specs=([] if first_turn else [SMEM]) + [VMEM] * len(ids) + [VMEM if first_turn else HBM] * 2,
+        out_specs=VMEM,
         scratch_shapes=[pltpu.VMEM((slots * BLOCK, width), BF16)]
-        + ([] if resident else [pltpu.VMEM((rows, width), BF16)] * 2 + [pltpu.SemaphoreType.DMA((2,))]),
+        + ([] if first_turn else [pltpu.VMEM((rows, width), BF16)] * 2 + [pltpu.SemaphoreType.DMA((2,))]),
         compiler_params=params(16),
         name="lookup",
-    )(place, *ids, *tables)
-
-
-def plan_kernel(place_ref, *refs, size, slots, table_rows):
-    *ids_refs, pick_ref = refs
-    me, turn = place_ref[0], place_ref[1]
+    )(*([] if first_turn else [turn]), *ids, *tables)
+
+
+def plan_kernel(*refs, axis, size, slots, table_rows, first_turn):
+    if first_turn:
+        *ids_refs, pick_ref, rounds_ref = refs
+        turn = 0
+    else:
+        turn_ref, *ids_refs, pick_ref, rounds_ref = refs
+        turn = turn_ref[0]
+    me = lax.axis_index(axis)
     pair, key, _ = candidates_info(ids_refs, me, size, table_rows)
     count = pair.shape[1]
     key_col = to_column(key)
     pair_col = key_col // count
     before = (key < key_col) & (key >= pair_col * count)
     rank = jnp.sum(before.astype(jnp.int32), axis=1, keepdims=True)
+    rounds_ref[0] = jnp.max(rank) // slots + 1
     away = pair_col ^ (me >> 1)
     block = jnp.zeros_like(away)
     for k, b in enumerate(position_bits(size)):
@@ -186,16 +190,22 @@
     pick_ref[...] = pick.astype(F32).astype(BF16)
 
 
-def plan(place, ids, slots, table_rows, size):
+def plan(ids, slots, table_rows, axis, size, turn=None):
     count = sum(i.shape[1] for i in ids)
-    return pl.pallas_call(
-        functools.partial(plan_kernel, size=size, slots=slots, table_rows=table_rows),
-        out_shape=jax.ShapeDtypeStruct((count, size // 2 * slots), BF16),
-        in_specs=[SMEM] + [VMEM] * len(ids),
-        out_specs=VMEM,
+    first_turn = turn is None
+    return pl.pallas_call(
+        functools.partial(
+            plan_kernel, axis=axis, size=size, slots=slots, table_rows=table_rows, first_turn=first_turn
+        ),
+        out_shape=(
+            jax.ShapeDtypeStruct((count, size // 2 * slots), BF16),
+            jax.ShapeDtypeStruct((1,), jnp.int32),
+        ),
+        in_specs=([] if first_turn else [SMEM]) + [VMEM] * len(ids),
+        out_specs=(VMEM, SMEM),
         compiler_params=params(16),
         name="plan",
-    )(place, *ids)
+    )(*([] if first_turn else [turn]), *ids)
 
 
 def select_kernel(pick_ref, rows_ref, out_ref):
@@ -222,15 +232,15 @@
 
 
 def prepare_kernel(
-    place_ref, start_ref, times_hbm, time_bias_hbm, pos_bias_hbm, table_hbm, out_ref, table_ref,
-    times_ref, time_bias_ref, pos_bias_ref, sems, *, npos, history
+    start_ref, times_hbm, time_bias_hbm, pos_bias_hbm, table_hbm, out_ref, table_ref,
+    times_ref, time_bias_ref, pos_bias_ref, sems, *, axis, npos, history
 ):
     pairs = ((times_hbm, times_ref), (time_bias_hbm, time_bias_ref), (pos_bias_hbm, pos_bias_ref), (table_hbm, table_ref))
     copies = [pltpu.make_async_copy(a, b, sems.at[k]) for k, (a, b) in enumerate(pairs)]
     for c in copies:
         c.start()
     events = times_ref.shape[1]
-    first = history - start_ref[0] - place_ref[0] * events
+    first = history - start_ref[0] - lax.axis_index(axis) * events
     distance = first - lax.broadcasted_iota(jnp.int32, (1, events), 1)
     bucket = jnp.zeros((1, events), jnp.int32)
     for k in range(1, npos):
@@ -249,20 +259,20 @@
     copies[3].wait()
 
 
-def prepare(place, start, times, time_bias, pos_bias, table, history):
+def prepare(start, times, time_bias, pos_bias, table, axis, history):
     arrays = [times, time_bias, pos_bias, table]
     return pl.pallas_call(
-        functools.partial(prepare_kernel, npos=pos_bias.shape[1], history=history),
+        functools.partial(prepare_kernel, axis=axis, npos=pos_bias.shape[1], history=history),
         out_shape=(
             jax.ShapeDtypeStruct((times.shape[1], LANES), BF16),
             jax.ShapeDtypeStruct(table.shape, BF16),
         ),
-        in_specs=[SMEM, SMEM] + [HBM] * 4,
+        in_specs=[SMEM] + [HBM] * 4,
         out_specs=(VMEM, VMEM),
         scratch_shapes=[pltpu.VMEM(a.shape, a.dtype) for a in arrays[:3]] + [pltpu.SemaphoreType.DMA((4,))],
         compiler_params=params(8),
         name="prepare",
-    )(place, start, *(pltpu.with_memory_space_constraint(a, pltpu.HBM) for a in arrays))
+    )(start, *(pltpu.with_memory_space_constraint(a, pltpu.HBM) for a in arrays))
 
 
 def silu(x):
@@ -337,17 +347,21 @@
                 send_ref[: first + rows - half, at] = out[half - first :].astype(BF16)
 
 
-def attend_first_kernel(rounds_ref, pick_ref, *refs, heads, blocks, split):
-    *row_refs, extra_hbm, gain_ref, proj_ref = refs[: -7 - 3 * blocks]
-    caches = refs[-7 - 3 * blocks : -7]
-    own_ref, keep_ref, send_ref, later_ref, emb_ref, query_ref, sem = refs[-7:]
+def attend_first_kernel(rounds_hbm, pick_ref, *refs, heads, blocks, split):
+    *row_refs, extra_hbm, gain_ref, proj_ref = refs[: -8 - 3 * blocks]
+    caches = refs[-8 - 3 * blocks : -8]
+    own_ref, keep_ref, send_ref, later_ref, emb_ref, query_ref, rounds_ref, sems = refs[-8:]
     count, width = emb_ref.shape
+    told = pltpu.make_async_copy(rounds_hbm, rounds_ref, sems.at[0])
+    told.start()
     rows = jnp.concatenate([r[...] for r in row_refs], axis=0)
     emb_ref[...] = jnp.dot(pick_ref[...], rows, preferred_element_type=F32).astype(BF16)
 
+    told.wait()
+
     @pl.when(rounds_ref[0] > 1)
     def _():
-        extra = pltpu.make_async_copy(extra_hbm, query_ref, sem)
+        extra = pltpu.make_async_copy(extra_hbm, query_ref, sems.at[1])
         extra.start()
         extra.wait()
         emb_ref[...] = emb_ref[...] + query_ref[...]
@@ -392,12 +406,13 @@
             jax.ShapeDtypeStruct((count // 2, columns), BF16),
             jax.ShapeDtypeStruct((count, width - columns), BF16),
         ),
-        in_specs=[SMEM, VMEM] + [VMEM] * len(pieces) + [HBM] + [VMEM] * (2 + 3 * blocks),
+        in_specs=[HBM, VMEM] + [VMEM] * len(pieces) + [HBM] + [VMEM] * (2 + 3 * blocks),
         out_specs=(VMEM,) * 4,
         scratch_shapes=[
             pltpu.VMEM((count, width), BF16),
             pltpu.VMEM((count, width), BF16),
-            pltpu.SemaphoreType.DMA,
+            pltpu.SMEM((1,), jnp.int32),
+            pltpu.SemaphoreType.DMA((2,)),
         ],
         compiler_params=params(20),
         cost_estimate=attention_cost(count, columns, keys, width // heads),
@@ -533,7 +548,6 @@
 ):
     axis = "hist"
     size = lax.axis_size(axis)
-    me = lax.axis_index(axis).astype(jnp.int32)
     each = item_ids.shape[0]
     slots = 2 * each
     heads = time_bias.shape[0]
@@ -541,38 +555,34 @@
     table_rows = item_table.shape[0]
     gain = norm_gain[None, :]
 
-    def place(turn):
-        return jnp.stack([me, jnp.asarray(turn, jnp.int32)])
-
     def partners(x):
         return swap(x, PARTNER, axis, size)
 
-    here = place(0)
     other_table = partners(item_table)
     other_keys = partners(key_cache)
     other_values = partners(value_cache)
     bias, own_table = prepare(
-        here, window_start, time_buckets[None, :], time_bias, pos_bias, item_table, 2 * events * size
+        window_start, time_buckets[None, :], time_bias, pos_bias, item_table, axis, 2 * events * size
     )
     other_bias = partners(bias)
     ids = gather_relative(item_ids[None, :], 1, axis, size)
 
     (near_table,) = stage(width, other_table, held=False)
-    found, rounds = lookup(here, ids, [own_table, near_table], slots, size, True)
+    found = lookup(ids, [own_table, near_table], slots, axis, size)
     pieces = gather_rows(found, axis, size)
-    pick = plan(here, ids, slots, table_rows, size)
+    pick, rounds = plan(ids, slots, table_rows, axis, size)
 
     def more(state):
         turn, so_far = state
-        picked = plan(place(turn), ids, slots, table_rows, size)
-        found, _ = lookup(place(turn), ids, [item_table, other_table], slots, size, False)
+        picked, _ = plan(ids, slots, table_rows, axis, size, turn[None])
+        found = lookup(ids, [item_table, other_table], slots, axis, size, turn[None])
         return turn + 1, so_far + select(picked, gather_rows(found, axis, size))
 
     none = jnp.zeros((each * (size // 2), width), BF16)
     _, extra = lax.while_loop(lambda s: s[0] < rounds[0], more, (jnp.int32(1), none))
 
-    keys, values = stage(width, key_cache, value_cache)
-    proj, other_keys, other_values = stage(width, proj_in, other_keys, other_values)
+    (keys,) = stage(width, key_cache)
+    proj, values, other_keys, other_values = stage(width, proj_in, value_cache, other_keys, other_values)
     caches = ([keys, other_keys], [values, other_values], [bias, other_bias])
     *far, near = stage_masks(size)
     split = max(1, width // LANES * 7 // 8)

time: 75.7 us -> 75.8 us (level)
  Pallas kernels: 19.1 us -> 16.6 us
  local copies, waits for them, and re-layouts: 12.5 us -> 15 us
    unnamed x30 -> x36, local copies, waits for them, and re-layouts: 11.8 us -> 14.3 us
    pallas_call x3, Pallas kernels: 6.73 us -> 5.26 us  [stage(): pl.pallas_call(functools.partial(stage_kernel, width=width), out_shape=tu...]
    pallas_call x3, Pallas kernels: 4.68 us -> 3.25 us  [the longest x1 1.68 us: prepare(): pl.pallas_call(functools.partial(prepare_kernel, axis=axis, npos=pos_bias...]
  transfers between devices with their start and end apart: 18 -> 18, of which waited for: 9 -> 9; matrix products, arithmetic and copies ran while one was open for 1% -> 1% of each run, Pallas kernels for 17% -> 13%
where the time goes in v1:
time: 75.8 us; the launch traced here: 75.5 us
  starting transfers between devices  26 us (34%)
  Pallas kernels  16.6 us (22%)
  waiting for transfers between devices  16.4 us (22%)
  local copies, waits for them, and re-layouts  15 us (20%)
  between operations  0.81 us (1%)
    ppermute x18, starting transfers between devices, swap(): return lax.ppermute(x, axis, [(i, i ^ mask) for i in range(size)])  26 us
    ppermute x18, waiting for transfers between devices, swap(): return lax.ppermute(x, axis, [(i, i ^ mask) for i in range(size)])  16.4 us
    unnamed x36, local copies, waits for them, and re-layouts  14.3 us
    pallas_call x1, Pallas kernels, attend_first(): pl.pallas_call(functools.partial(attend_first_kernel, heads=heads, blocks...  5.51 us
    pallas_call x3, Pallas kernels, stage(): pl.pallas_call(functools.partial(stage_kernel, width=width), out_shape=tu...  5.26 us
    pallas_call x1, Pallas kernels, prepare(): pl.pallas_call(functools.partial(prepare_kernel, axis=axis, npos=pos_bias...  1.68 us
  transfers between devices with their start and end apart: 18, of which 9 were waited for; matrix products, arithmetic and copies ran while one was open for 1% of the time, Pallas kernels for 13%

profile of v1, /device:TPU:0, one launch (start us, length us, event | category | flops | bytes accessed | tf_op | source)
XLA Modules:
  0.0 75.5 jit_solution(15756368958783701736)
XLA Ops:
  0.0 0.5 collective-permute-start.9
  0.5 0.1 collective-permute-start.15
  0.6 0.4 collective-permute-start.16
  1.7 1.7 %prepare.1 = (bf16[1024,128]{1,0:T(8,128)(2,1)S(1)}, bf16[1024,1024]{1,0:T(8,128)(2,1)S(1)}) custom-call(s32[1]{0:T(128)S(6)} %copy.19.start_ref, s32[1,1024]{1,0:T(1,128)} %bitcast.12, f32[16,128]{1,0:T(8,128)} %time_bias_hbm.1, f32[16,18]{1,0:T(8,128)} %pos_bias_hbm.1, bf16[1024,1024]{1,0:T(8,128)(2,1)} %table_hbm.1), custom_call_target="tpu_custom_call" | custom-call | tf_op jit(solution)/shard_map/prepare/pallas_call | solution.py:264
  3.3 0.1 collective-permute-start.17
  3.5 0.0 copy-done.17
  3.5 3.0 %collective-permute-start.5 = (s32[1,16]{1,0:T(1,128)S(1)}, s32[1,16]{1,0:T(1,128)S(1)}, u32[]{:S(2)}, u32[]{:S(2)}) collective-permute-start(s32[1,16]{1,0:T(1,128)S(1)} %bitcast.13), channel_id=1, source_target_pairs={{0,4},{1,5},{2,6},{3,7},{4,0},{5,1},{6,2},{7,3},{8,12},{9,13},{10,... | collective-permute-start | bytes 200 | tf_op jit(solution)/shard_map/ppermute | solution.py:46
  6.5 1.5 %collective-permute-done.5 = s32[1,16]{1,0:T(1,128)S(1)} collective-permute-done((s32[1,16]{1,0:T(1,128)S(1)}, s32[1,16]{1,0:T(1,128)S(1)}, u32[]{:S(2)}, u32[]{:S(2)}) %collective-permute-start.5) | collective-permute-done | bytes 96 | tf_op jit(solution)/shard_map/ppermute | solution.py:46
  8.0 3.0 %collective-permute-start.6 = (s32[1,16]{1,0:T(1,128)S(1)}, s32[1,16]{1,0:T(1,128)S(1)}, u32[]{:S(2)}, u32[]{:S(2)}) collective-permute-start(s32[1,16]{1,0:T(1,128)S(1)} %bitcast.14), channel_id=1, source_target_pairs={{0,8},{1,9},{2,10},{3,11},{4,12},{5,13},{6,14},{7,15},{8,0},{9,1},... | collective-permute-start | bytes 200 | tf_op jit(solution)/shard_map/ppermute | solution.py:46
  11.1 1.5 %collective-permute-done.6 = s32[1,16]{1,0:T(1,128)S(1)} collective-permute-done((s32[1,16]{1,0:T(1,128)S(1)}, s32[1,16]{1,0:T(1,128)S(1)}, u32[]{:S(2)}, u32[]{:S(2)}) %collective-permute-start.6) | collective-permute-done | bytes 96 | tf_op jit(solution)/shard_map/ppermute | solution.py:46
  12.6 3.9 %collective-permute-start.7 = (s32[1,16]{1,0:T(1,128)S(1)}, s32[1,16]{1,0:T(1,128)S(1)}, u32[]{:S(2)}, u32[]{:S(2)}) collective-permute-start(s32[1,16]{1,0:T(1,128)S(1)} %bitcast.15), channel_id=1, source_target_pairs={{0,12},{1,13},{2,14},{3,15},{4,8},{5,9},{6,10},{7,11},{8,4},{9,5},... | collective-permute-start | bytes 200 | tf_op jit(solution)/shard_map/ppermute | solution.py:46
  16.5 1.5 %collective-permute-done.7 = s32[1,16]{1,0:T(1,128)S(1)} collective-permute-done((s32[1,16]{1,0:T(1,128)S(1)}, s32[1,16]{1,0:T(1,128)S(1)}, u32[]{:S(2)}, u32[]{:S(2)}) %collective-permute-start.7) | collective-permute-done | bytes 96 | tf_op jit(solution)/shard_map/ppermute | solution.py:46
  18.1 0.1 pad_add_fusion.refs_0_
  18.2 1.7 %collective-permute-start.8 = (s32[1,64]{1,0:T(1,128)S(1)}, s32[1,64]{1,0:T(1,128)S(1)}, u32[]{:S(2)}, u32[]{:S(2)}) collective-permute-start(s32[1,64]{1,0:T(1,128)S(1)} %pad_add_fusion.refs_0_), channel_id=1, source_target_pairs={{0,2},{1,3},{2,0},{3,1},{4,6},{5,7},{6,4},{7,5},{8,10},{9,11},{10,... | collective-permute-start | bytes 776 | tf_op jit(solution)/shard_map/ppermute | solution.py:46
  19.9 0.0 collective-permute-done.9.refs_0_
  19.9 0.2 stage.3.refs_3_
  20.1 1.2 %copy-done.15 = bf16[1024,1024]{1,0:T(8,128)(2,1)} copy-done((bf16[1024,1024]{1,0:T(8,128)(2,1)}, bf16[1024,1024]{1,0:T(8,128)(2,1)S(1)}, u32[]{:S(2)}) %copy-start.15) | copy-done | bytes 2097176
  21.3 0.4 collective-permute-done.8.refs_1_
  21.7 0.7 lookup.2.refs_0_
  22.4 0.0 collective-permute-start.10
  22.5 4.4 %collective-permute-start.11 = (bf16[32,1024]{1,0:T(8,128)(2,1)S(1)}, bf16[32,1024]{1,0:T(8,128)(2,1)S(1)}, u32[]{:S(2)}, u32[]{:S(2)}) collective-permute-start(bf16[32,1024]{1,0:T(8,128)(2,1)S(1)} %lookup.2.refs_0_), channel_id=1, source_target_pairs={{0,8},{1,9},{2,10},{3,11},{4,12},{5,13},{6,14},{7,15},{8,0},{9,1},... | collective-permute-start | bytes 196616 | tf_op jit(solution)/shard_map/ppermute | solution.py:46
  26.8 0.0 collective-permute-done.15.refs_2_
  26.9 1.3 %copy-done.16 = bf16[1024,1024]{1,0:T(8,128)(2,1)} copy-done((bf16[1024,1024]{1,0:T(8,128)(2,1)}, bf16[1024,1024]{1,0:T(8,128)(2,1)S(1)}, u32[]{:S(2)}) %copy-start.16) | copy-done | bytes 2097176
  28.2 0.0 collective-permute-start.12
  28.2 1.6 %stage.5.refs_7_.refs_0_ = bf16[1024,1024]{1,0:T(8,128)(2,1)S(1)} custom-call(bf16[1024,1024]{1,0:T(8,128)(2,1)} %refs_0_.3), custom_call_target="tpu_custom_call" | custom-call | tf_op jit(solution)/shard_map/stage/pallas_call | solution.py:482
  29.8 0.9 %plan.2 = (bf16[128,256]{1,0:T(8,128)(2,1)S(1)}, s32[1]{0:T(128)}) custom-call(s32[1,64]{1,0:T(1,128)S(1)} %pad_add_fusion.refs_0_, s32[1,64]{1,0:T(1,128)S(1)} %collective-permute-done.8.refs_1_), custom_call_target="tpu_custom_call" | custom-call | tf_op jit(solution)/shard_map/plan/pallas_call | solution.py:196
  30.7 0.0 collective-permute-done.16.refs_3_
  30.7 3.5 %stage.4 = (bf16[1024,1024]{1,0:T(8,128)(2,1)S(1)}, bf16[1024,1024]{1,0:T(8,128)(2,1)S(1)}, bf16[1024,1024]{1,0:T(8,128)(2,1)S(1)}, bf16[1024,1024]{1,0:T(8,128)(2,1)S(1)}) custom-call(bf16[1024,2048]{1,0:T(8,128)(2,1)} %proj_ref.1, bf16[1024,1024]{1,0:T(8,128)(2,1)} %refs_1_.1, bf16[1024,1024]{1,0:T(8,128)(2,1)} %copy-done.16, ...), custom_call_target="tpu_custom_call" | custom-call | tf_op jit(solution)/shard_map/stage/pallas_call | solution.py:482
  34.2 0.0 copy-start.1
  34.2 1.3 %copy-done.1 = bf16[1024,1024]{1,0:T(8,128)(2,1)} copy-done((bf16[1024,1024]{1,0:T(8,128)(2,1)}, bf16[1024,1024]{1,0:T(8,128)(2,1)S(1)}, u32[]{:S(2)}) %copy-start.1) | copy-done | bytes 2097176
  35.6 1.3 %copy-done.4 = bf16[1024,1024]{1,0:T(8,128)(2,1)} copy-done((bf16[1024,1024]{1,0:T(8,128)(2,1)}, bf16[1024,1024]{1,0:T(8,128)(2,1)S(1)}, u32[]{:S(2)}) %copy-start.4) | copy-done | bytes 2097176
  36.9 1.4 %copy-done.7 = bf16[1024,1024]{1,0:T(8,128)(2,1)} copy-done((bf16[1024,1024]{1,0:T(8,128)(2,1)}, bf16[1024,1024]{1,0:T(8,128)(2,1)S(1)}, u32[]{:S(2)}) %copy-start.7) | copy-done | bytes 2097176
  38.3 1.3 %copy-done.11 = bf16[1024,1024]{1,0:T(8,128)(2,1)} copy-done((bf16[1024,1024]{1,0:T(8,128)(2,1)}, bf16[1024,1024]{1,0:T(8,128)(2,1)S(1)}, u32[]{:S(2)}) %copy-start.11) | copy-done | bytes 2097176
  39.6 1.7 %collective-permute-start.13 = (bf16[32,1024]{1,0:T(8,128)(2,1)S(1)}, bf16[32,1024]{1,0:T(8,128)(2,1)S(1)}, u32[]{:S(2)}, u32[]{:S(2)}) collective-permute-start(bf16[32,1024]{1,0:T(8,128)(2,1)S(1)} %lookup.2.refs_0_), channel_id=1, source_target_pairs={{0,2},{1,3},{2,0},{3,1},{4,6},{5,7},{6,4},{7,5},{8,10},{9,11},{10,... | collective-permute-start | bytes 196616 | tf_op jit(solution)/shard_map/ppermute | solution.py:46
  41.3 0.0 collective-permute-done.10.refs_0_
  41.3 0.0 collective-permute-done.11.refs_1_
  41.3 0.0 collective-permute-done.12.refs_2_
  41.3 0.4 collective-permute-start.14
  41.7 0.0 collective-permute-done.17.refs_12_.refs_5_
  41.7 0.7 broadcast_in_dim.21
  42.4 0.7 while.10
  43.1 0.7 collective-permute-done.13.refs_2_
  43.8 3.2 %collective-permute-done.14.refs_3_ = bf16[96,1024]{1,0:T(8,128)(2,1)S(1)} collective-permute-done((bf16[96,1024]{1,0:T(8,128)(2,1)S(1)}, bf16[96,1024]{1,0:T(8,128)(2,1)S(1)}, u32[]{:S(2)}, u32[]{:S(2)}) %collective-permute-start.14) | collective-permute-done | bytes 196640 | tf_op jit(solution)/shard_map/ppermute | solution.py:46
  47.1 0.0 copy-done.13
  47.1 1.6 %copy-done.2 = bf16[1024,1024]{1,0:T(8,128)(2,1)S(1)} copy-done((bf16[1024,1024]{1,0:T(8,128)(2,1)S(1)}, bf16[1024,1024]{1,0:T(8,128)(2,1)}, u32[]{:S(2)}) %copy-start.2) | copy-done | bytes 2097176
  48.7 1.6 %copy-done.5 = bf16[1024,1024]{1,0:T(8,128)(2,1)S(1)} copy-done((bf16[1024,1024]{1,0:T(8,128)(2,1)S(1)}, bf16[1024,1024]{1,0:T(8,128)(2,1)}, u32[]{:S(2)}) %copy-start.5) | copy-done | bytes 2097176
  50.3 1.6 %copy-done.8 = bf16[1024,1024]{1,0:T(8,128)(2,1)S(1)} copy-done((bf16[1024,1024]{1,0:T(8,128)(2,1)S(1)}, bf16[1024,1024]{1,0:T(8,128)(2,1)}, u32[]{:S(2)}) %copy-start.8) | copy-done | bytes 2097176
  51.9 1.6 %copy-done.12 = bf16[1024,1024]{1,0:T(8,128)(2,1)S(1)} copy-done((bf16[1024,1024]{1,0:T(8,128)(2,1)S(1)}, bf16[1024,1024]{1,0:T(8,128)(2,1)}, u32[]{:S(2)}) %copy-start.12) | copy-done | bytes 2097176
  53.5 5.5 %attend_first.1 = (bf16[16,1024]{1,0:T(8,128)(2,1)S(1)}, f32[64,896]{1,0:T(8,128)S(1)}, bf16[64,896]{1,0:T(8,128)(2,1)S(1)}, bf16[128,128]{1,0:T(8,128)(2,1)S(1)}) custom-call(s32[1]{0:T(128)} %get-tuple-element.143.rounds_hbm, bf16[128,256]{1,0:T(8,128)(2,1)S(1)} %get-tuple-element.63.pick_ref, bf16[32,1024]{1,0:T(8,128)(2,1)S(1)} %lookup.2.refs_0_, ...), custom_call_target="tpu_custom_call" | custom-call | flops 1879048192 | bytes 7340032 | tf_op jit(solution)/shard_map/attend_first/pallas_call | solution.py:401
  59.0 0.7 collective-permute-start.18
  59.7 0.9 %attend_later.1 = (f32[64,128]{1,0:T(8,128)S(1)}, bf16[64,128]{1,0:T(8,128)(2,1)S(1)}) custom-call(bf16[128,128]{1,0:T(8,128)(2,1)S(1)} %get-tuple-element.73.query_ref, bf16[1024,1024]{1,0:T(8,128)(2,1)S(1)} %stage.5.refs_7_.refs_0_, bf16[1024,1024]{1,0:T(8,128)(2,1)S(1)} %copy-done.6, bf16[1024,1024]{1,0:T(8,128)(2,1)S(1)} %copy-done.3, ...), custom_call_target="tpu_custom_call" | custom-call | flops 268435456 | bytes 1048576 | tf_op jit(solution)/shard_map/attend_later/pallas_call | solution.py:426
  60.6 1.5 %collective-permute-start.19 = (bf16[64,128]{1,0:T(8,128)(2,1)S(1)}, bf16[64,128]{1,0:T(8,128)(2,1)S(1)}, u32[]{:S(2)}, u32[]{:S(2)}) collective-permute-start(bf16[64,128]{1,0:T(8,128)(2,1)S(1)} %get-tuple-element.75), channel_id=1, source_target_pairs={{0,2},{1,3},{2,0},{3,1},{4,6},{5,7},{6,4},{7,5},{8,10},{9,11},{10,... | collective-permute-start | bytes 49160 | tf_op jit(solution)/shard_map/ppermute | solution.py:46
  62.1 2.3 %collective-permute-done.19.refs_3_ = bf16[64,128]{1,0:T(8,128)(2,1)S(1)} collective-permute-done((bf16[64,128]{1,0:T(8,128)(2,1)S(1)}, bf16[64,128]{1,0:T(8,128)(2,1)S(1)}, u32[]{:S(2)}, u32[]{:S(2)}) %collective-permute-start.19) | collective-permute-done | bytes 16416 | tf_op jit(solution)/shard_map/ppermute | solution.py:46
  64.4 0.0 collective-permute-done.18.refs_1_
  64.4 0.4 collective-permute-start.20
  64.8 3.8 %collective-permute-start.21 = (bf16[16,1024]{1,0:T(8,128)(2,1)S(1)}, bf16[16,1024]{1,0:T(8,128)(2,1)S(1)}, u32[]{:S(2)}, u32[]{:S(2)}) collective-permute-start(bf16[16,1024]{1,0:T(8,128)(2,1)S(1)} %get-tuple-element.78), channel_id=1, source_target_pairs={{0,8},{1,9},{2,10},{3,11},{4,12},{5,13},{6,14},{7,15},{8,0},{9,1},... | collective-permute-start | bytes 98312 | tf_op jit(solution)/shard_map/ppermute | solution.py:46
  68.6 0.2 collective-permute-start.22
  68.9 0.0 copy-done
  68.9 0.5 gates.1.refs_4_
  69.3 0.0 collective-permute-done.20.refs_0_
  69.3 1.5 %collective-permute-done.21.refs_1_ = bf16[16,1024]{1,0:T(8,128)(2,1)S(1)} collective-permute-done((bf16[16,1024]{1,0:T(8,128)(2,1)S(1)}, bf16[16,1024]{1,0:T(8,128)(2,1)S(1)}, u32[]{:S(2)}, u32[]{:S(2)}) %collective-permute-start.21) | collective-permute-done | bytes 32800 | tf_op jit(solution)/shard_map/ppermute | solution.py:46
  70.9 3.5 %collective-permute-done.22.refs_2_ = bf16[16,1024]{1,0:T(8,128)(2,1)S(1)} collective-permute-done((bf16[16,1024]{1,0:T(8,128)(2,1)S(1)}, bf16[16,1024]{1,0:T(8,128)(2,1)S(1)}, u32[]{:S(2)}, u32[]{:S(2)}) %collective-permute-start.22) | collective-permute-done | bytes 32800 | tf_op jit(solution)/shard_map/ppermute | solution.py:46
  74.3 0.0 copy-done.14
  74.3 1.2 %finish.1 = bf16[16,1024]{1,0:T(8,128)(2,1)} custom-call(f32[16,1024]{1,0:T(8,128)S(1)} %get-tuple-element.76.own_ref, bf16[16,1024]{1,0:T(8,128)(2,1)S(1)} %collective-permute-done.20.refs_0_, bf16[16,1024]{1,0:T(8,128)(2,1)S(1)} %collective-permute-done.21.refs_1_, bf16[16,1024]{1,0:T(8,128)(2,1)S(1)} %collective-permute-done.22.refs_2_, ...), custom_call_target="tpu_custom_call" | custom-call | tf_op jit(solution)/shard_map/finish/pallas_call | solution.py:525
  (23 shorter events, 0.1 us)
Async XLA Ops:
  0.0 3.5 %copy-start.17 = (s32[16]{0:T(128)S(1)}, s32[16]{0:T(128)}, u32[]{:S(2)}) copy-start(s32[16]{0:T(128)} %param.14) | copy-start | bytes 196
  0.0 19.9 %collective-permute-start.9 = (bf16[1024,1024]{1,0:T(8,128)(2,1)}, bf16[1024,1024]{1,0:T(8,128)(2,1)S(1)}, u32[]{:S(2)}, u32[]{:S(2)}) collective-permute-start(bf16[1024,1024]{1,0:T(8,128)(2,1)} %table_hbm.1), channel_id=1, source_target_pairs={{0,1},{1,0},{2,3},{3,2},{4,5},{5,4},{6,7},{7,6},{8,9},{9,8},{10,11... | collective-permute-start | bytes 6291464 | tf_op jit(solution)/shard_map/ppermute | solution.py:46
  0.5 26.4 %collective-permute-start.15 = (bf16[1024,1024]{1,0:T(8,128)(2,1)}, bf16[1024,1024]{1,0:T(8,128)(2,1)S(1)}, u32[]{:S(2)}, u32[]{:S(2)}) collective-permute-start(bf16[1024,1024]{1,0:T(8,128)(2,1)} %refs_0_.3), channel_id=1, source_target_pairs={{0,1},{1,0},{2,3},{3,2},{4,5},{5,4},{6,7},{7,6},{8,9},{9,8},{10,11... | collective-permute-start | bytes 6291464 | tf_op jit(solution)/shard_map/ppermute | solution.py:46
  0.6 30.1 %collective-permute-start.16 = (bf16[1024,1024]{1,0:T(8,128)(2,1)}, bf16[1024,1024]{1,0:T(8,128)(2,1)}, u32[]{:S(2)}, u32[]{:S(2)}) collective-permute-start(bf16[1024,1024]{1,0:T(8,128)(2,1)} %refs_1_.1), channel_id=1, source_target_pairs={{0,1},{1,0},{2,3},{3,2},{4,5},{5,4},{6,7},{7,6},{8,9},{9,8},{10,11... | collective-permute-start | bytes 6291464 | tf_op jit(solution)/shard_map/ppermute | solution.py:46
  3.3 38.4 %collective-permute-start.17 = (bf16[1024,128]{1,0:T(8,128)(2,1)S(1)}, bf16[1024,128]{1,0:T(8,128)(2,1)S(1)}, u32[]{:S(2)}, u32[]{:S(2)}) collective-permute-start(bf16[1024,128]{1,0:T(8,128)(2,1)S(1)} %get-tuple-element.70.refs_11_.refs_4_), channel_id=1, source_target_pairs={{0,1},{1,0},{2,3},{3,2},{4,5},{5,4},{6,7},{7,6},{8,9},{9,8},{10,11... | collective-permute-start | bytes 786440 | tf_op jit(solution)/shard_map/ppermute | solution.py:46
  3.5 4.6 %collective-permute-start.5 = (s32[1,16]{1,0:T(1,128)S(1)}, s32[1,16]{1,0:T(1,128)S(1)}, u32[]{:S(2)}, u32[]{:S(2)}) collective-permute-start(s32[1,16]{1,0:T(1,128)S(1)} %bitcast.13), channel_id=1, source_target_pairs={{0,4},{1,5},{2,6},{3,7},{4,0},{5,1},{6,2},{7,3},{8,12},{9,13},{10,... | collective-permute-start | bytes 200 | tf_op jit(solution)/shard_map/ppermute | solution.py:46
  8.0 4.6 %collective-permute-start.6 = (s32[1,16]{1,0:T(1,128)S(1)}, s32[1,16]{1,0:T(1,128)S(1)}, u32[]{:S(2)}, u32[]{:S(2)}) collective-permute-start(s32[1,16]{1,0:T(1,128)S(1)} %bitcast.14), channel_id=1, source_target_pairs={{0,8},{1,9},{2,10},{3,11},{4,12},{5,13},{6,14},{7,15},{8,0},{9,1},... | collective-permute-start | bytes 200 | tf_op jit(solution)/shard_map/ppermute | solution.py:46
  12.6 5.5 %collective-permute-start.7 = (s32[1,16]{1,0:T(1,128)S(1)}, s32[1,16]{1,0:T(1,128)S(1)}, u32[]{:S(2)}, u32[]{:S(2)}) collective-permute-start(s32[1,16]{1,0:T(1,128)S(1)} %bitcast.15), channel_id=1, source_target_pairs={{0,12},{1,13},{2,14},{3,15},{4,8},{5,9},{6,10},{7,11},{8,4},{9,5},... | collective-permute-start | bytes 200 | tf_op jit(solution)/shard_map/ppermute | solution.py:46
  18.2 3.6 %collective-permute-start.8 = (s32[1,64]{1,0:T(1,128)S(1)}, s32[1,64]{1,0:T(1,128)S(1)}, u32[]{:S(2)}, u32[]{:S(2)}) collective-permute-start(s32[1,64]{1,0:T(1,128)S(1)} %pad_add_fusion.refs_0_), channel_id=1, source_target_pairs={{0,2},{1,3},{2,0},{3,1},{4,6},{5,7},{6,4},{7,5},{8,10},{9,11},{10,... | collective-permute-start | bytes 776 | tf_op jit(solution)/shard_map/ppermute | solution.py:46
  19.9 1.4 %copy-start.15 = (bf16[1024,1024]{1,0:T(8,128)(2,1)}, bf16[1024,1024]{1,0:T(8,128)(2,1)S(1)}, u32[]{:S(2)}) copy-start(bf16[1024,1024]{1,0:T(8,128)(2,1)S(1)} %collective-permute-done.9.refs_0_) | copy-start | bytes 6291460
  22.4 18.9 %collective-permute-start.10 = (bf16[32,1024]{1,0:T(8,128)(2,1)S(1)}, bf16[32,1024]{1,0:T(8,128)(2,1)S(1)}, u32[]{:S(2)}, u32[]{:S(2)}) collective-permute-start(bf16[32,1024]{1,0:T(8,128)(2,1)S(1)} %lookup.2.refs_0_), channel_id=1, source_target_pairs={{0,4},{1,5},{2,6},{3,7},{4,0},{5,1},{6,2},{7,3},{8,12},{9,13},{10,... | collective-permute-start | bytes 196616 | tf_op jit(solution)/shard_map/ppermute | solution.py:46
  22.5 18.8 %collective-permute-start.11 = (bf16[32,1024]{1,0:T(8,128)(2,1)S(1)}, bf16[32,1024]{1,0:T(8,128)(2,1)S(1)}, u32[]{:S(2)}, u32[]{:S(2)}) collective-permute-start(bf16[32,1024]{1,0:T(8,128)(2,1)S(1)} %lookup.2.refs_0_), channel_id=1, source_target_pairs={{0,8},{1,9},{2,10},{3,11},{4,12},{5,13},{6,14},{7,15},{8,0},{9,1},... | collective-permute-start | bytes 196616 | tf_op jit(solution)/shard_map/ppermute | solution.py:46
  26.8 1.3 %copy-start.16 = (bf16[1024,1024]{1,0:T(8,128)(2,1)}, bf16[1024,1024]{1,0:T(8,128)(2,1)S(1)}, u32[]{:S(2)}) copy-start(bf16[1024,1024]{1,0:T(8,128)(2,1)S(1)} %collective-permute-done.15.refs_2_) | copy-start | bytes 6291460
  28.2 13.1 %collective-permute-start.12 = (bf16[32,1024]{1,0:T(8,128)(2,1)S(1)}, bf16[32,1024]{1,0:T(8,128)(2,1)S(1)}, u32[]{:S(2)}, u32[]{:S(2)}) collective-permute-start(bf16[32,1024]{1,0:T(8,128)(2,1)S(1)} %lookup.2.refs_0_), channel_id=1, source_target_pairs={{0,12},{1,13},{2,14},{3,15},{4,8},{5,9},{6,10},{7,11},{8,4},{9,5},... | collective-permute-start | bytes 196616 | tf_op jit(solution)/shard_map/ppermute | solution.py:46
  34.2 1.3 %copy-start.1 = (bf16[1024,1024]{1,0:T(8,128)(2,1)}, bf16[1024,1024]{1,0:T(8,128)(2,1)S(1)}, u32[]{:S(2)}) copy-start(bf16[1024,1024]{1,0:T(8,128)(2,1)S(1)} %get-tuple-element.68.refs_9_.refs_2_) | copy-start | bytes 6291460
  35.6 1.3 %copy-start.4 = (bf16[1024,1024]{1,0:T(8,128)(2,1)}, bf16[1024,1024]{1,0:T(8,128)(2,1)S(1)}, u32[]{:S(2)}) copy-start(bf16[1024,1024]{1,0:T(8,128)(2,1)S(1)} %get-tuple-element.67.refs_8_.refs_1_) | copy-start | bytes 6291460
  36.9 1.4 %copy-start.7 = (bf16[1024,1024]{1,0:T(8,128)(2,1)}, bf16[1024,1024]{1,0:T(8,128)(2,1)S(1)}, u32[]{:S(2)}) copy-start(bf16[1024,1024]{1,0:T(8,128)(2,1)S(1)} %get-tuple-element.69.refs_10_.refs_3_) | copy-start | bytes 6291460
  38.3 1.3 %copy-start.11 = (bf16[1024,1024]{1,0:T(8,128)(2,1)}, bf16[1024,1024]{1,0:T(8,128)(2,1)S(1)}, u32[]{:S(2)}) copy-start(bf16[1024,1024]{1,0:T(8,128)(2,1)S(1)} %get-tuple-element.66.refs_6_) | copy-start | bytes 6291460
  39.6 4.3 %collective-permute-start.13 = (bf16[32,1024]{1,0:T(8,128)(2,1)S(1)}, bf16[32,1024]{1,0:T(8,128)(2,1)S(1)}, u32[]{:S(2)}, u32[]{:S(2)}) collective-permute-start(bf16[32,1024]{1,0:T(8,128)(2,1)S(1)} %lookup.2.refs_0_), channel_id=1, source_target_pairs={{0,2},{1,3},{2,0},{3,1},{4,6},{5,7},{6,4},{7,5},{8,10},{9,11},{10,... | collective-permute-start | bytes 196616 | tf_op jit(solution)/shard_map/ppermute | solution.py:46
  41.3 5.7 %collective-permute-start.14 = (bf16[96,1024]{1,0:T(8,128)(2,1)S(1)}, bf16[96,1024]{1,0:T(8,128)(2,1)S(1)}, u32[]{:S(2)}, u32[]{:S(2)}) collective-permute-start(bf16[96,1024]{1,0:T(8,128)(2,1)S(1)} %join.2.refs_1_), channel_id=1, source_target_pairs={{0,2},{1,3},{2,0},{3,1},{4,6},{5,7},{6,4},{7,5},{8,10},{9,11},{10,... | collective-permute-start | bytes 589832 | tf_op jit(solution)/shard_map/ppermute | solution.py:46
  42.4 4.7 %copy-start.13 = (f32[1024]{0:T(1024)S(1)}, f32[1024]{0:T(1024)}, u32[]{:S(2)}) copy-start(f32[1024]{0:T(1024)} %param.20) | copy-start | bytes 12292
  47.1 1.6 %copy-start.2 = (bf16[1024,1024]{1,0:T(8,128)(2,1)S(1)}, bf16[1024,1024]{1,0:T(8,128)(2,1)}, u32[]{:S(2)}) copy-start(bf16[1024,1024]{1,0:T(8,128)(2,1)} %copy-done.1) | copy-start | bytes 6291460
  48.7 1.6 %copy-start.5 = (bf16[1024,1024]{1,0:T(8,128)(2,1)S(1)}, bf16[1024,1024]{1,0:T(8,128)(2,1)}, u32[]{:S(2)}) copy-start(bf16[1024,1024]{1,0:T(8,128)(2,1)} %copy-done.4) | copy-start | bytes 6291460
  50.3 1.6 %copy-start.8 = (bf16[1024,1024]{1,0:T(8,128)(2,1)S(1)}, bf16[1024,1024]{1,0:T(8,128)(2,1)}, u32[]{:S(2)}) copy-start(bf16[1024,1024]{1,0:T(8,128)(2,1)} %copy-done.7) | copy-start | bytes 6291460
  51.9 1.6 %copy-start.12 = (bf16[1024,1024]{1,0:T(8,128)(2,1)S(1)}, bf16[1024,1024]{1,0:T(8,128)(2,1)}, u32[]{:S(2)}) copy-start(bf16[1024,1024]{1,0:T(8,128)(2,1)} %copy-done.11) | copy-start | bytes 6291460
  53.4 6.2 %copy-start.3 = (bf16[1024,1024]{1,0:T(8,128)(2,1)S(1)}, bf16[1024,1024]{1,0:T(8,128)(2,1)}, u32[]{:S(2)}) copy-start(bf16[1024,1024]{1,0:T(8,128)(2,1)} %copy-done.1) | copy-start | bytes 6291460
  53.5 6.2 %copy-start.6 = (bf16[1024,1024]{1,0:T(8,128)(2,1)S(1)}, bf16[1024,1024]{1,0:T(8,128)(2,1)}, u32[]{:S(2)}) copy-start(bf16[1024,1024]{1,0:T(8,128)(2,1)} %copy-done.4) | copy-start | bytes 6291460
  53.5 6.2 %copy-start.9 = (bf16[1024,1024]{1,0:T(8,128)(2,1)S(1)}, bf16[1024,1024]{1,0:T(8,128)(2,1)}, u32[]{:S(2)}) copy-start(bf16[1024,1024]{1,0:T(8,128)(2,1)} %copy-done.7) | copy-start | bytes 6291460
  59.0 5.4 %collective-permute-start.18 = (bf16[64,896]{1,0:T(8,128)(2,1)S(1)}, bf16[64,896]{1,0:T(8,128)(2,1)S(1)}, u32[]{:S(2)}, u32[]{:S(2)}) collective-permute-start(bf16[64,896]{1,0:T(8,128)(2,1)S(1)} %get-tuple-element.72), channel_id=1, source_target_pairs={{0,2},{1,3},{2,0},{3,1},{4,6},{5,7},{6,4},{7,5},{8,10},{9,11},{10,... | collective-permute-start | bytes 344072 | tf_op jit(solution)/shard_map/ppermute | solution.py:46
  59.6 9.2 %copy-start = (bf16[1024,2048]{1,0:T(8,128)(2,1)S(1)}, bf16[1024,2048]{1,0:T(8,128)(2,1)}, u32[]{:S(2)}) copy-start(bf16[1024,2048]{1,0:T(8,128)(2,1)} %proj_ref.1) | copy-start | bytes 12582916
  60.6 3.8 %collective-permute-start.19 = (bf16[64,128]{1,0:T(8,128)(2,1)S(1)}, bf16[64,128]{1,0:T(8,128)(2,1)S(1)}, u32[]{:S(2)}, u32[]{:S(2)}) collective-permute-start(bf16[64,128]{1,0:T(8,128)(2,1)S(1)} %get-tuple-element.75), channel_id=1, source_target_pairs={{0,2},{1,3},{2,0},{3,1},{4,6},{5,7},{6,4},{7,5},{8,10},{9,11},{10,... | collective-permute-start | bytes 49160 | tf_op jit(solution)/shard_map/ppermute | solution.py:46
  64.4 4.9 %collective-permute-start.20 = (bf16[16,1024]{1,0:T(8,128)(2,1)S(1)}, bf16[16,1024]{1,0:T(8,128)(2,1)S(1)}, u32[]{:S(2)}, u32[]{:S(2)}) collective-permute-start(bf16[16,1024]{1,0:T(8,128)(2,1)S(1)} %get-tuple-element.77), channel_id=1, source_target_pairs={{0,4},{1,5},{2,6},{3,7},{4,0},{5,1},{6,2},{7,3},{8,12},{9,13},{10,... | collective-permute-start | bytes 98312 | tf_op jit(solution)/shard_map/ppermute | solution.py:46
  64.8 6.1 %collective-permute-start.21 = (bf16[16,1024]{1,0:T(8,128)(2,1)S(1)}, bf16[16,1024]{1,0:T(8,128)(2,1)S(1)}, u32[]{:S(2)}, u32[]{:S(2)}) collective-permute-start(bf16[16,1024]{1,0:T(8,128)(2,1)S(1)} %get-tuple-element.78), channel_id=1, source_target_pairs={{0,8},{1,9},{2,10},{3,11},{4,12},{5,13},{6,14},{7,15},{8,0},{9,1},... | collective-permute-start | bytes 98312 | tf_op jit(solution)/shard_map/ppermute | solution.py:46
  68.6 5.7 %collective-permute-start.22 = (bf16[16,1024]{1,0:T(8,128)(2,1)S(1)}, bf16[16,1024]{1,0:T(8,128)(2,1)S(1)}, u32[]{:S(2)}, u32[]{:S(2)}) collective-permute-start(bf16[16,1024]{1,0:T(8,128)(2,1)S(1)} %get-tuple-element.79), channel_id=1, source_target_pairs={{0,12},{1,13},{2,14},{3,15},{4,8},{5,9},{6,10},{7,11},{8,4},{9,5},... | collective-permute-start | bytes 98312 | tf_op jit(solution)/shard_map/ppermute | solution.py:46
  68.9 5.5 %copy-start.10 = (bf16[1024,1024]{1,0:T(8,128)(2,1)S(1)}, bf16[1024,1024]{1,0:T(8,128)(2,1)}, u32[]{:S(2)}) copy-start(bf16[1024,1024]{1,0:T(8,128)(2,1)} %refs_6_.1) | copy-start | bytes 6291460
  68.9 5.5 %copy-start.14 = (f32[1024]{0:T(1024)S(1)}, f32[1024]{0:T(1024)}, u32[]{:S(2)}) copy-start(f32[1024]{0:T(1024)} %param.24) | copy-start | bytes 12292

commit v2 on v1

--- a/solution.py
+++ b/solution.py
@@ -347,21 +347,18 @@
                 send_ref[: first + rows - half, at] = out[half - first :].astype(BF16)
 
 
-def attend_first_kernel(rounds_hbm, pick_ref, *refs, heads, blocks, split):
-    *row_refs, extra_hbm, gain_ref, proj_ref = refs[: -8 - 3 * blocks]
-    caches = refs[-8 - 3 * blocks : -8]
-    own_ref, keep_ref, send_ref, later_ref, emb_ref, query_ref, rounds_ref, sems = refs[-8:]
+def attend_first_kernel(rounds_ref, pick_ref, *refs, heads, blocks, split):
+    *row_refs, extra_hbm, gain_ref, proj_ref = refs[: -7 - 3 * blocks]
+    caches = refs[-7 - 3 * blocks : -7]
+    own_ref, keep_ref, send_ref, later_ref, emb_ref, query_ref, sem = refs[-7:]
     count, width = emb_ref.shape
-    told = pltpu.make_async_copy(rounds_hbm, rounds_ref, sems.at[0])
-    told.start()
     rows = jnp.concatenate([r[...] for r in row_refs], axis=0)
     emb_ref[...] = jnp.dot(pick_ref[...], rows, preferred_element_type=F32).astype(BF16)
 
-    told.wait()
 
     @pl.when(rounds_ref[0] > 1)
     def _():
-        extra = pltpu.make_async_copy(extra_hbm, query_ref, sems.at[1])
+        extra = pltpu.make_async_copy(extra_hbm, query_ref, sem)
         extra.start()
         extra.wait()
         emb_ref[...] = emb_ref[...] + query_ref[...]
@@ -406,13 +403,12 @@
             jax.ShapeDtypeStruct((count // 2, columns), BF16),
             jax.ShapeDtypeStruct((count, width - columns), BF16),
         ),
-        in_specs=[HBM, VMEM] + [VMEM] * len(pieces) + [HBM] + [VMEM] * (2 + 3 * blocks),
+        in_specs=[SMEM, VMEM] + [VMEM] * len(pieces) + [HBM] + [VMEM] * (2 + 3 * blocks),
         out_specs=(VMEM,) * 4,
         scratch_shapes=[
             pltpu.VMEM((count, width), BF16),
             pltpu.VMEM((count, width), BF16),
-            pltpu.SMEM((1,), jnp.int32),
-            pltpu.SemaphoreType.DMA((2,)),
+            pltpu.SemaphoreType.DMA,
         ],
         compiler_params=params(20),
         cost_estimate=attention_cost(count, columns, keys, width // heads),
@@ -581,8 +577,9 @@
     none = jnp.zeros((each * (size // 2), width), BF16)
     _, extra = lax.while_loop(lambda s: s[0] < rounds[0], more, (jnp.int32(1), none))
 
-    (keys,) = stage(width, key_cache)
-    proj, values, other_keys, other_values = stage(width, proj_in, value_cache, other_keys, other_values)
+    proj, keys, values, other_keys, other_values = stage(
+        width, proj_in, key_cache, value_cache, other_keys, other_values
+    )
     caches = ([keys, other_keys], [values, other_values], [bias, other_bias])
     *far, near = stage_masks(size)
     split = max(1, width // LANES * 7 // 8)

time: 75.8 us -> 73.2 us (0.966)
  Pallas kernels: 16.6 us -> 15.3 us
  local copies, waits for them, and re-layouts: 15 us -> 14.1 us
    pallas_call x3 -> x2, Pallas kernels: 5.26 us -> 4.26 us  [stage(): pl.pallas_call(functools.partial(stage_kernel, width=width), out_shape=tu...]
    unnamed x36, local copies, waits for them, and re-layouts: 14.3 us -> 13.4 us
  transfers between devices with their start and end apart: 18 -> 18, of which waited for: 9 -> 9; matrix products, arithmetic and copies ran while one was open for 1% -> 1% of each run, Pallas kernels for 13% -> 12%
where the time goes in v2:
time: 73.2 us; the launch traced here: 72.9 us
  starting transfers between devices  26 us (36%)
  waiting for transfers between devices  16 us (22%)
  Pallas kernels  15.3 us (21%)
  local copies, waits for them, and re-layouts  14.1 us (19%)
  between operations  0.79 us (1%)
    ppermute x18, starting transfers between devices, swap(): return lax.ppermute(x, axis, [(i, i ^ mask) for i in range(size)])  26 us
    ppermute x18, waiting for transfers between devices, swap(): return lax.ppermute(x, axis, [(i, i ^ mask) for i in range(size)])  16 us
    unnamed x36, local copies, waits for them, and re-layouts  13.4 us
    pallas_call x1, Pallas kernels, attend_first(): pl.pallas_call(functools.partial(attend_first_kernel, heads=heads, blocks...  5.2 us
    pallas_call x2, Pallas kernels, stage(): pl.pallas_call(functools.partial(stage_kernel, width=width), out_shape=tu...  4.26 us
    pallas_call x1, Pallas kernels, prepare(): pl.pallas_call(functools.partial(prepare_kernel, axis=axis, npos=pos_bias...  1.68 us
  transfers between devices with their start and end apart: 18, of which 9 were waited for; matrix products, arithmetic and copies ran while one was open for 1% of the time, Pallas kernels for 12%

profile of v2, /device:TPU:0, one launch (start us, length us, event | category | flops | bytes accessed | tf_op | source)
XLA Modules:
  0.0 72.9 jit_solution(4517046862520575052)
XLA Ops:
  0.0 0.5 collective-permute-start.9
  0.5 0.1 collective-permute-start.15
  0.6 0.4 collective-permute-start.16
  1.7 1.7 %prepare.1 = (bf16[1024,128]{1,0:T(8,128)(2,1)S(1)}, bf16[1024,1024]{1,0:T(8,128)(2,1)S(1)}) custom-call(s32[1]{0:T(128)S(6)} %copy.19.start_ref, s32[1,1024]{1,0:T(1,128)} %bitcast.12, f32[16,128]{1,0:T(8,128)} %time_bias_hbm.1, f32[16,18]{1,0:T(8,128)} %pos_bias_hbm.1, bf16[1024,1024]{1,0:T(8,128)(2,1)} %table_hbm.1), custom_call_target="tpu_custom_call" | custom-call | tf_op jit(solution)/shard_map/prepare/pallas_call | solution.py:264
  3.3 0.1 collective-permute-start.17
  3.5 0.0 copy-done.17
  3.5 3.0 %collective-permute-start.5 = (s32[1,16]{1,0:T(1,128)S(1)}, s32[1,16]{1,0:T(1,128)S(1)}, u32[]{:S(2)}, u32[]{:S(2)}) collective-permute-start(s32[1,16]{1,0:T(1,128)S(1)} %bitcast.13), channel_id=1, source_target_pairs={{0,4},{1,5},{2,6},{3,7},{4,0},{5,1},{6,2},{7,3},{8,12},{9,13},{10,... | collective-permute-start | bytes 200 | tf_op jit(solution)/shard_map/ppermute | solution.py:46
  6.5 1.5 %collective-permute-done.5 = s32[1,16]{1,0:T(1,128)S(1)} collective-permute-done((s32[1,16]{1,0:T(1,128)S(1)}, s32[1,16]{1,0:T(1,128)S(1)}, u32[]{:S(2)}, u32[]{:S(2)}) %collective-permute-start.5) | collective-permute-done | bytes 96 | tf_op jit(solution)/shard_map/ppermute | solution.py:46
  8.0 3.0 %collective-permute-start.6 = (s32[1,16]{1,0:T(1,128)S(1)}, s32[1,16]{1,0:T(1,128)S(1)}, u32[]{:S(2)}, u32[]{:S(2)}) collective-permute-start(s32[1,16]{1,0:T(1,128)S(1)} %bitcast.14), channel_id=1, source_target_pairs={{0,8},{1,9},{2,10},{3,11},{4,12},{5,13},{6,14},{7,15},{8,0},{9,1},... | collective-permute-start | bytes 200 | tf_op jit(solution)/shard_map/ppermute | solution.py:46
  11.1 1.5 %collective-permute-done.6 = s32[1,16]{1,0:T(1,128)S(1)} collective-permute-done((s32[1,16]{1,0:T(1,128)S(1)}, s32[1,16]{1,0:T(1,128)S(1)}, u32[]{:S(2)}, u32[]{:S(2)}) %collective-permute-start.6) | collective-permute-done | bytes 96 | tf_op jit(solution)/shard_map/ppermute | solution.py:46
  12.6 3.9 %collective-permute-start.7 = (s32[1,16]{1,0:T(1,128)S(1)}, s32[1,16]{1,0:T(1,128)S(1)}, u32[]{:S(2)}, u32[]{:S(2)}) collective-permute-start(s32[1,16]{1,0:T(1,128)S(1)} %bitcast.15), channel_id=1, source_target_pairs={{0,12},{1,13},{2,14},{3,15},{4,8},{5,9},{6,10},{7,11},{8,4},{9,5},... | collective-permute-start | bytes 200 | tf_op jit(solution)/shard_map/ppermute | solution.py:46
  16.5 1.5 %collective-permute-done.7 = s32[1,16]{1,0:T(1,128)S(1)} collective-permute-done((s32[1,16]{1,0:T(1,128)S(1)}, s32[1,16]{1,0:T(1,128)S(1)}, u32[]{:S(2)}, u32[]{:S(2)}) %collective-permute-start.7) | collective-permute-done | bytes 96 | tf_op jit(solution)/shard_map/ppermute | solution.py:46
  18.1 0.1 pad_add_fusion.refs_0_
  18.2 1.7 %collective-permute-start.8 = (s32[1,64]{1,0:T(1,128)S(1)}, s32[1,64]{1,0:T(1,128)S(1)}, u32[]{:S(2)}, u32[]{:S(2)}) collective-permute-start(s32[1,64]{1,0:T(1,128)S(1)} %pad_add_fusion.refs_0_), channel_id=1, source_target_pairs={{0,2},{1,3},{2,0},{3,1},{4,6},{5,7},{6,4},{7,5},{8,10},{9,11},{10,... | collective-permute-start | bytes 776 | tf_op jit(solution)/shard_map/ppermute | solution.py:46
  19.9 0.0 collective-permute-done.9.refs_0_
  19.9 0.2 stage.2.refs_3_
  20.1 1.2 %copy-done.15 = bf16[1024,1024]{1,0:T(8,128)(2,1)} copy-done((bf16[1024,1024]{1,0:T(8,128)(2,1)}, bf16[1024,1024]{1,0:T(8,128)(2,1)S(1)}, u32[]{:S(2)}) %copy-start.15) | copy-done | bytes 2097176
  21.3 0.4 collective-permute-done.8.refs_1_
  21.7 0.7 lookup.2.refs_0_
  22.4 0.0 collective-permute-start.10
  22.5 4.4 %collective-permute-start.11 = (bf16[32,1024]{1,0:T(8,128)(2,1)S(1)}, bf16[32,1024]{1,0:T(8,128)(2,1)S(1)}, u32[]{:S(2)}, u32[]{:S(2)}) collective-permute-start(bf16[32,1024]{1,0:T(8,128)(2,1)S(1)} %lookup.2.refs_0_), channel_id=1, source_target_pairs={{0,8},{1,9},{2,10},{3,11},{4,12},{5,13},{6,14},{7,15},{8,0},{9,1},... | collective-permute-start | bytes 196616 | tf_op jit(solution)/shard_map/ppermute | solution.py:46
  26.8 0.0 collective-permute-done.15.refs_3_
  26.9 0.0 collective-permute-start.12
  26.9 0.9 %plan.2 = (bf16[128,256]{1,0:T(8,128)(2,1)S(1)}, s32[1]{0:T(128)}) custom-call(s32[1,64]{1,0:T(1,128)S(1)} %pad_add_fusion.refs_0_, s32[1,64]{1,0:T(1,128)S(1)} %collective-permute-done.8.refs_1_), custom_call_target="tpu_custom_call" | custom-call | tf_op jit(solution)/shard_map/plan/pallas_call | solution.py:196
  27.8 0.4 copy-done.16
  28.2 0.0 collective-permute-done.16.refs_4_
  28.2 4.1 %stage.3 = (bf16[1024,1024]{1,0:T(8,128)(2,1)S(1)}, bf16[1024,1024]{1,0:T(8,128)(2,1)S(1)}, bf16[1024,1024]{1,0:T(8,128)(2,1)S(1)}, bf16[1024,1024]{1,0:T(8,128)(2,1)S(1)}, bf16[1024,1024]{1,0:T(8,128)(2,1)S(1)}) custom-call(bf16[1024,2048]{1,0:T(8,128)(2,1)} %proj_ref.1, bf16[1024,1024]{1,0:T(8,128)(2,1)} %refs_1_.1, bf16[1024,1024]{1,0:T(8,128)(2,1)} %refs_2_.1, ...), custom_call_target="tpu_custom_call" | custom-call | tf_op jit(solution)/shard_map/stage/pallas_call | solution.py:478
  32.3 0.0 copy-start.1
  32.3 1.3 %copy-done.1 = bf16[1024,1024]{1,0:T(8,128)(2,1)} copy-done((bf16[1024,1024]{1,0:T(8,128)(2,1)}, bf16[1024,1024]{1,0:T(8,128)(2,1)S(1)}, u32[]{:S(2)}) %copy-start.1) | copy-done | bytes 2097176
  33.6 1.3 %copy-done.4 = bf16[1024,1024]{1,0:T(8,128)(2,1)} copy-done((bf16[1024,1024]{1,0:T(8,128)(2,1)}, bf16[1024,1024]{1,0:T(8,128)(2,1)S(1)}, u32[]{:S(2)}) %copy-start.4) | copy-done | bytes 2097176
  35.0 1.4 %copy-done.7 = bf16[1024,1024]{1,0:T(8,128)(2,1)} copy-done((bf16[1024,1024]{1,0:T(8,128)(2,1)}, bf16[1024,1024]{1,0:T(8,128)(2,1)S(1)}, u32[]{:S(2)}) %copy-start.7) | copy-done | bytes 2097176
  36.3 1.3 %copy-done.11 = bf16[1024,1024]{1,0:T(8,128)(2,1)} copy-done((bf16[1024,1024]{1,0:T(8,128)(2,1)}, bf16[1024,1024]{1,0:T(8,128)(2,1)S(1)}, u32[]{:S(2)}) %copy-start.11) | copy-done | bytes 2097176
  37.7 1.5 %collective-permute-start.13 = (bf16[32,1024]{1,0:T(8,128)(2,1)S(1)}, bf16[32,1024]{1,0:T(8,128)(2,1)S(1)}, u32[]{:S(2)}, u32[]{:S(2)}) collective-permute-start(bf16[32,1024]{1,0:T(8,128)(2,1)S(1)} %lookup.2.refs_0_), channel_id=1, source_target_pairs={{0,2},{1,3},{2,0},{3,1},{4,6},{5,7},{6,4},{7,5},{8,10},{9,11},{10,... | collective-permute-start | bytes 196616 | tf_op jit(solution)/shard_map/ppermute | solution.py:46
  39.2 0.0 collective-permute-done.10.refs_0_
  39.2 0.0 collective-permute-done.11.refs_1_
  39.2 0.0 collective-permute-done.12.refs_2_
  39.2 0.6 collective-permute-start.14
  39.8 0.0 collective-permute-done.17.refs_12_.refs_5_
  39.8 0.7 broadcast_in_dim.21
  40.5 0.7 while.10
  41.2 0.7 %collective-permute-done.13.refs_2_ = bf16[32,1024]{1,0:T(8,128)(2,1)S(1)} collective-permute-done((bf16[32,1024]{1,0:T(8,128)(2,1)S(1)}, bf16[32,1024]{1,0:T(8,128)(2,1)S(1)}, u32[]{:S(2)}, u32[]{:S(2)}) %collective-permute-start.13) | collective-permute-done | bytes 65568 | tf_op jit(solution)/shard_map/ppermute | solution.py:46
  41.9 3.0 %collective-permute-done.14.refs_3_ = bf16[96,1024]{1,0:T(8,128)(2,1)S(1)} collective-permute-done((bf16[96,1024]{1,0:T(8,128)(2,1)S(1)}, bf16[96,1024]{1,0:T(8,128)(2,1)S(1)}, u32[]{:S(2)}, u32[]{:S(2)}) %collective-permute-start.14) | collective-permute-done | bytes 196640 | tf_op jit(solution)/shard_map/ppermute | solution.py:46
  44.9 0.0 copy-done.13
  45.0 1.6 %copy-done.2 = bf16[1024,1024]{1,0:T(8,128)(2,1)S(1)} copy-done((bf16[1024,1024]{1,0:T(8,128)(2,1)S(1)}, bf16[1024,1024]{1,0:T(8,128)(2,1)}, u32[]{:S(2)}) %copy-start.2) | copy-done | bytes 2097176
  46.5 1.6 %copy-done.5 = bf16[1024,1024]{1,0:T(8,128)(2,1)S(1)} copy-done((bf16[1024,1024]{1,0:T(8,128)(2,1)S(1)}, bf16[1024,1024]{1,0:T(8,128)(2,1)}, u32[]{:S(2)}) %copy-start.5) | copy-done | bytes 2097176
  48.1 1.6 %copy-done.8 = bf16[1024,1024]{1,0:T(8,128)(2,1)S(1)} copy-done((bf16[1024,1024]{1,0:T(8,128)(2,1)S(1)}, bf16[1024,1024]{1,0:T(8,128)(2,1)}, u32[]{:S(2)}) %copy-start.8) | copy-done | bytes 2097176
  49.7 1.6 %copy-done.12 = bf16[1024,1024]{1,0:T(8,128)(2,1)S(1)} copy-done((bf16[1024,1024]{1,0:T(8,128)(2,1)S(1)}, bf16[1024,1024]{1,0:T(8,128)(2,1)}, u32[]{:S(2)}) %copy-start.12) | copy-done | bytes 2097176
  51.3 5.2 %attend_first.1 = (bf16[16,1024]{1,0:T(8,128)(2,1)S(1)}, f32[64,896]{1,0:T(8,128)S(1)}, bf16[64,896]{1,0:T(8,128)(2,1)S(1)}, bf16[128,128]{1,0:T(8,128)(2,1)S(1)}) custom-call(s32[1]{0:T(128)} %get-tuple-element.145.rounds_ref, bf16[128,256]{1,0:T(8,128)(2,1)S(1)} %get-tuple-element.64.pick_ref, bf16[32,1024]{1,0:T(8,128)(2,1)S(1)} %lookup.2.refs_0_, ...), custom_call_target="tpu_custom_call" | custom-call | flops 1879048192 | bytes 7340032 | tf_op jit(solution)/shard_map/attend_first/pallas_call | solution.py:398
  56.5 0.7 collective-permute-start.18
  57.2 0.0 copy-done.3
  57.2 0.0 copy-done.6
  57.2 0.9 %attend_later.1 = (f32[64,128]{1,0:T(8,128)S(1)}, bf16[64,128]{1,0:T(8,128)(2,1)S(1)}) custom-call(bf16[128,128]{1,0:T(8,128)(2,1)S(1)} %get-tuple-element.75.query_ref, bf16[1024,1024]{1,0:T(8,128)(2,1)S(1)} %get-tuple-element.68.refs_7_.refs_0_, bf16[1024,1024]{1,0:T(8,128)(2,1)S(1)} %copy-done.6, bf16[1024,1024]{1,0:T(8,128)(2,1)S(1)} %copy-done.3, ...), custom_call_target="tpu_custom_call" | custom-call | flops 268435456 | bytes 1048576 | tf_op jit(solution)/shard_map/attend_later/pallas_call | solution.py:422
  58.1 1.5 %collective-permute-start.19 = (bf16[64,128]{1,0:T(8,128)(2,1)S(1)}, bf16[64,128]{1,0:T(8,128)(2,1)S(1)}, u32[]{:S(2)}, u32[]{:S(2)}) collective-permute-start(bf16[64,128]{1,0:T(8,128)(2,1)S(1)} %get-tuple-element.77), channel_id=1, source_target_pairs={{0,2},{1,3},{2,0},{3,1},{4,6},{5,7},{6,4},{7,5},{8,10},{9,11},{10,... | collective-permute-start | bytes 49160 | tf_op jit(solution)/shard_map/ppermute | solution.py:46
  59.6 2.3 %collective-permute-done.19.refs_3_ = bf16[64,128]{1,0:T(8,128)(2,1)S(1)} collective-permute-done((bf16[64,128]{1,0:T(8,128)(2,1)S(1)}, bf16[64,128]{1,0:T(8,128)(2,1)S(1)}, u32[]{:S(2)}, u32[]{:S(2)}) %collective-permute-start.19) | collective-permute-done | bytes 16416 | tf_op jit(solution)/shard_map/ppermute | solution.py:46
  61.9 0.0 collective-permute-done.18.refs_1_
  62.0 0.3 collective-permute-start.20
  62.2 3.8 %collective-permute-start.21 = (bf16[16,1024]{1,0:T(8,128)(2,1)S(1)}, bf16[16,1024]{1,0:T(8,128)(2,1)S(1)}, u32[]{:S(2)}, u32[]{:S(2)}) collective-permute-start(bf16[16,1024]{1,0:T(8,128)(2,1)S(1)} %get-tuple-element.80), channel_id=1, source_target_pairs={{0,8},{1,9},{2,10},{3,11},{4,12},{5,13},{6,14},{7,15},{8,0},{9,1},... | collective-permute-start | bytes 98312 | tf_op jit(solution)/shard_map/ppermute | solution.py:46
  66.0 0.4 collective-permute-start.22
  66.4 0.5 gates.1.refs_4_
  66.9 0.0 collective-permute-done.20.refs_0_
  66.9 1.0 %collective-permute-done.21.refs_1_ = bf16[16,1024]{1,0:T(8,128)(2,1)S(1)} collective-permute-done((bf16[16,1024]{1,0:T(8,128)(2,1)S(1)}, bf16[16,1024]{1,0:T(8,128)(2,1)S(1)}, u32[]{:S(2)}, u32[]{:S(2)}) %collective-permute-start.21) | collective-permute-done | bytes 32800 | tf_op jit(solution)/shard_map/ppermute | solution.py:46
  67.9 3.8 %collective-permute-done.22.refs_2_ = bf16[16,1024]{1,0:T(8,128)(2,1)S(1)} collective-permute-done((bf16[16,1024]{1,0:T(8,128)(2,1)S(1)}, bf16[16,1024]{1,0:T(8,128)(2,1)S(1)}, u32[]{:S(2)}, u32[]{:S(2)}) %collective-permute-start.22) | collective-permute-done | bytes 32800 | tf_op jit(solution)/shard_map/ppermute | solution.py:46
  71.7 0.0 copy-done.10
  71.7 1.2 %finish.1 = bf16[16,1024]{1,0:T(8,128)(2,1)} custom-call(f32[16,1024]{1,0:T(8,128)S(1)} %get-tuple-element.78.own_ref, bf16[16,1024]{1,0:T(8,128)(2,1)S(1)} %collective-permute-done.20.refs_0_, bf16[16,1024]{1,0:T(8,128)(2,1)S(1)} %collective-permute-done.21.refs_1_, bf16[16,1024]{1,0:T(8,128)(2,1)S(1)} %collective-permute-done.22.refs_2_, ...), custom_call_target="tpu_custom_call" | custom-call | tf_op jit(solution)/shard_map/finish/pallas_call | solution.py:521
  (22 shorter events, 0.1 us)
Async XLA Ops:
  0.0 3.5 %copy-start.17 = (s32[16]{0:T(128)S(1)}, s32[16]{0:T(128)}, u32[]{:S(2)}) copy-start(s32[16]{0:T(128)} %param.14) | copy-start | bytes 196
  0.0 19.9 %collective-permute-start.9 = (bf16[1024,1024]{1,0:T(8,128)(2,1)}, bf16[1024,1024]{1,0:T(8,128)(2,1)S(1)}, u32[]{:S(2)}, u32[]{:S(2)}) collective-permute-start(bf16[1024,1024]{1,0:T(8,128)(2,1)} %table_hbm.1), channel_id=1, source_target_pairs={{0,1},{1,0},{2,3},{3,2},{4,5},{5,4},{6,7},{7,6},{8,9},{9,8},{10,11... | collective-permute-start | bytes 6291464 | tf_op jit(solution)/shard_map/ppermute | solution.py:46
  0.5 26.4 %collective-permute-start.15 = (bf16[1024,1024]{1,0:T(8,128)(2,1)}, bf16[1024,1024]{1,0:T(8,128)(2,1)S(1)}, u32[]{:S(2)}, u32[]{:S(2)}) collective-permute-start(bf16[1024,1024]{1,0:T(8,128)(2,1)} %refs_1_.1), channel_id=1, source_target_pairs={{0,1},{1,0},{2,3},{3,2},{4,5},{5,4},{6,7},{7,6},{8,9},{9,8},{10,11... | collective-permute-start | bytes 6291464 | tf_op jit(solution)/shard_map/ppermute | solution.py:46
  0.6 27.6 %collective-permute-start.16 = (bf16[1024,1024]{1,0:T(8,128)(2,1)}, bf16[1024,1024]{1,0:T(8,128)(2,1)}, u32[]{:S(2)}, u32[]{:S(2)}) collective-permute-start(bf16[1024,1024]{1,0:T(8,128)(2,1)} %refs_2_.1), channel_id=1, source_target_pairs={{0,1},{1,0},{2,3},{3,2},{4,5},{5,4},{6,7},{7,6},{8,9},{9,8},{10,11... | collective-permute-start | bytes 6291464 | tf_op jit(solution)/shard_map/ppermute | solution.py:46
  3.3 36.4 %collective-permute-start.17 = (bf16[1024,128]{1,0:T(8,128)(2,1)S(1)}, bf16[1024,128]{1,0:T(8,128)(2,1)S(1)}, u32[]{:S(2)}, u32[]{:S(2)}) collective-permute-start(bf16[1024,128]{1,0:T(8,128)(2,1)S(1)} %get-tuple-element.72.refs_11_.refs_4_), channel_id=1, source_target_pairs={{0,1},{1,0},{2,3},{3,2},{4,5},{5,4},{6,7},{7,6},{8,9},{9,8},{10,11... | collective-permute-start | bytes 786440 | tf_op jit(solution)/shard_map/ppermute | solution.py:46
  3.5 4.6 %collective-permute-start.5 = (s32[1,16]{1,0:T(1,128)S(1)}, s32[1,16]{1,0:T(1,128)S(1)}, u32[]{:S(2)}, u32[]{:S(2)}) collective-permute-start(s32[1,16]{1,0:T(1,128)S(1)} %bitcast.13), channel_id=1, source_target_pairs={{0,4},{1,5},{2,6},{3,7},{4,0},{5,1},{6,2},{7,3},{8,12},{9,13},{10,... | collective-permute-start | bytes 200 | tf_op jit(solution)/shard_map/ppermute | solution.py:46
  8.0 4.6 %collective-permute-start.6 = (s32[1,16]{1,0:T(1,128)S(1)}, s32[1,16]{1,0:T(1,128)S(1)}, u32[]{:S(2)}, u32[]{:S(2)}) collective-permute-start(s32[1,16]{1,0:T(1,128)S(1)} %bitcast.14), channel_id=1, source_target_pairs={{0,8},{1,9},{2,10},{3,11},{4,12},{5,13},{6,14},{7,15},{8,0},{9,1},... | collective-permute-start | bytes 200 | tf_op jit(solution)/shard_map/ppermute | solution.py:46
  12.6 5.5 %collective-permute-start.7 = (s32[1,16]{1,0:T(1,128)S(1)}, s32[1,16]{1,0:T(1,128)S(1)}, u32[]{:S(2)}, u32[]{:S(2)}) collective-permute-start(s32[1,16]{1,0:T(1,128)S(1)} %bitcast.15), channel_id=1, source_target_pairs={{0,12},{1,13},{2,14},{3,15},{4,8},{5,9},{6,10},{7,11},{8,4},{9,5},... | collective-permute-start | bytes 200 | tf_op jit(solution)/shard_map/ppermute | solution.py:46
  18.2 3.6 %collective-permute-start.8 = (s32[1,64]{1,0:T(1,128)S(1)}, s32[1,64]{1,0:T(1,128)S(1)}, u32[]{:S(2)}, u32[]{:S(2)}) collective-permute-start(s32[1,64]{1,0:T(1,128)S(1)} %pad_add_fusion.refs_0_), channel_id=1, source_target_pairs={{0,2},{1,3},{2,0},{3,1},{4,6},{5,7},{6,4},{7,5},{8,10},{9,11},{10,... | collective-permute-start | bytes 776 | tf_op jit(solution)/shard_map/ppermute | solution.py:46
  19.9 1.4 %copy-start.15 = (bf16[1024,1024]{1,0:T(8,128)(2,1)}, bf16[1024,1024]{1,0:T(8,128)(2,1)S(1)}, u32[]{:S(2)}) copy-start(bf16[1024,1024]{1,0:T(8,128)(2,1)S(1)} %collective-permute-done.9.refs_0_) | copy-start | bytes 6291460
  22.4 16.8 %collective-permute-start.10 = (bf16[32,1024]{1,0:T(8,128)(2,1)S(1)}, bf16[32,1024]{1,0:T(8,128)(2,1)S(1)}, u32[]{:S(2)}, u32[]{:S(2)}) collective-permute-start(bf16[32,1024]{1,0:T(8,128)(2,1)S(1)} %lookup.2.refs_0_), channel_id=1, source_target_pairs={{0,4},{1,5},{2,6},{3,7},{4,0},{5,1},{6,2},{7,3},{8,12},{9,13},{10,... | collective-permute-start | bytes 196616 | tf_op jit(solution)/shard_map/ppermute | solution.py:46
  22.5 16.7 %collective-permute-start.11 = (bf16[32,1024]{1,0:T(8,128)(2,1)S(1)}, bf16[32,1024]{1,0:T(8,128)(2,1)S(1)}, u32[]{:S(2)}, u32[]{:S(2)}) collective-permute-start(bf16[32,1024]{1,0:T(8,128)(2,1)S(1)} %lookup.2.refs_0_), channel_id=1, source_target_pairs={{0,8},{1,9},{2,10},{3,11},{4,12},{5,13},{6,14},{7,15},{8,0},{9,1},... | collective-permute-start | bytes 196616 | tf_op jit(solution)/shard_map/ppermute | solution.py:46
  26.8 1.3 %copy-start.16 = (bf16[1024,1024]{1,0:T(8,128)(2,1)}, bf16[1024,1024]{1,0:T(8,128)(2,1)S(1)}, u32[]{:S(2)}) copy-start(bf16[1024,1024]{1,0:T(8,128)(2,1)S(1)} %collective-permute-done.15.refs_3_) | copy-start | bytes 6291460
  26.9 12.3 %collective-permute-start.12 = (bf16[32,1024]{1,0:T(8,128)(2,1)S(1)}, bf16[32,1024]{1,0:T(8,128)(2,1)S(1)}, u32[]{:S(2)}, u32[]{:S(2)}) collective-permute-start(bf16[32,1024]{1,0:T(8,128)(2,1)S(1)} %lookup.2.refs_0_), channel_id=1, source_target_pairs={{0,12},{1,13},{2,14},{3,15},{4,8},{5,9},{6,10},{7,11},{8,4},{9,5},... | collective-permute-start | bytes 196616 | tf_op jit(solution)/shard_map/ppermute | solution.py:46
  32.3 1.3 %copy-start.1 = (bf16[1024,1024]{1,0:T(8,128)(2,1)}, bf16[1024,1024]{1,0:T(8,128)(2,1)S(1)}, u32[]{:S(2)}) copy-start(bf16[1024,1024]{1,0:T(8,128)(2,1)S(1)} %get-tuple-element.70.refs_9_.refs_2_) | copy-start | bytes 6291460
  33.6 1.3 %copy-start.4 = (bf16[1024,1024]{1,0:T(8,128)(2,1)}, bf16[1024,1024]{1,0:T(8,128)(2,1)S(1)}, u32[]{:S(2)}) copy-start(bf16[1024,1024]{1,0:T(8,128)(2,1)S(1)} %get-tuple-element.69.refs_8_.refs_1_) | copy-start | bytes 6291460
  35.0 1.4 %copy-start.7 = (bf16[1024,1024]{1,0:T(8,128)(2,1)}, bf16[1024,1024]{1,0:T(8,128)(2,1)S(1)}, u32[]{:S(2)}) copy-start(bf16[1024,1024]{1,0:T(8,128)(2,1)S(1)} %get-tuple-element.71.refs_10_.refs_3_) | copy-start | bytes 6291460
  36.3 1.3 %copy-start.11 = (bf16[1024,1024]{1,0:T(8,128)(2,1)}, bf16[1024,1024]{1,0:T(8,128)(2,1)S(1)}, u32[]{:S(2)}) copy-start(bf16[1024,1024]{1,0:T(8,128)(2,1)S(1)} %get-tuple-element.67.refs_6_) | copy-start | bytes 6291460
  37.7 4.3 %collective-permute-start.13 = (bf16[32,1024]{1,0:T(8,128)(2,1)S(1)}, bf16[32,1024]{1,0:T(8,128)(2,1)S(1)}, u32[]{:S(2)}, u32[]{:S(2)}) collective-permute-start(bf16[32,1024]{1,0:T(8,128)(2,1)S(1)} %lookup.2.refs_0_), channel_id=1, source_target_pairs={{0,2},{1,3},{2,0},{3,1},{4,6},{5,7},{6,4},{7,5},{8,10},{9,11},{10,... | collective-permute-start | bytes 196616 | tf_op jit(solution)/shard_map/ppermute | solution.py:46
  39.2 5.7 %collective-permute-start.14 = (bf16[96,1024]{1,0:T(8,128)(2,1)S(1)}, bf16[96,1024]{1,0:T(8,128)(2,1)S(1)}, u32[]{:S(2)}, u32[]{:S(2)}) collective-permute-start(bf16[96,1024]{1,0:T(8,128)(2,1)S(1)} %join.2.refs_1_), channel_id=1, source_target_pairs={{0,2},{1,3},{2,0},{3,1},{4,6},{5,7},{6,4},{7,5},{8,10},{9,11},{10,... | collective-permute-start | bytes 589832 | tf_op jit(solution)/shard_map/ppermute | solution.py:46
  40.5 4.4 %copy-start.13 = (f32[1024]{0:T(1024)S(1)}, f32[1024]{0:T(1024)}, u32[]{:S(2)}) copy-start(f32[1024]{0:T(1024)} %param.20) | copy-start | bytes 12292
  45.0 1.6 %copy-start.2 = (bf16[1024,1024]{1,0:T(8,128)(2,1)S(1)}, bf16[1024,1024]{1,0:T(8,128)(2,1)}, u32[]{:S(2)}) copy-start(bf16[1024,1024]{1,0:T(8,128)(2,1)} %copy-done.1) | copy-start | bytes 6291460
  46.5 1.6 %copy-start.5 = (bf16[1024,1024]{1,0:T(8,128)(2,1)S(1)}, bf16[1024,1024]{1,0:T(8,128)(2,1)}, u32[]{:S(2)}) copy-start(bf16[1024,1024]{1,0:T(8,128)(2,1)} %copy-done.4) | copy-start | bytes 6291460
  48.1 1.6 %copy-start.8 = (bf16[1024,1024]{1,0:T(8,128)(2,1)S(1)}, bf16[1024,1024]{1,0:T(8,128)(2,1)}, u32[]{:S(2)}) copy-start(bf16[1024,1024]{1,0:T(8,128)(2,1)} %copy-done.7) | copy-start | bytes 6291460
  49.7 1.6 %copy-start.12 = (bf16[1024,1024]{1,0:T(8,128)(2,1)S(1)}, bf16[1024,1024]{1,0:T(8,128)(2,1)}, u32[]{:S(2)}) copy-start(bf16[1024,1024]{1,0:T(8,128)(2,1)} %copy-done.11) | copy-start | bytes 6291460
  51.3 5.9 %copy-start.3 = (bf16[1024,1024]{1,0:T(8,128)(2,1)S(1)}, bf16[1024,1024]{1,0:T(8,128)(2,1)}, u32[]{:S(2)}) copy-start(bf16[1024,1024]{1,0:T(8,128)(2,1)} %copy-done.1) | copy-start | bytes 6291460
  51.3 5.9 %copy-start.6 = (bf16[1024,1024]{1,0:T(8,128)(2,1)S(1)}, bf16[1024,1024]{1,0:T(8,128)(2,1)}, u32[]{:S(2)}) copy-start(bf16[1024,1024]{1,0:T(8,128)(2,1)} %copy-done.4) | copy-start | bytes 6291460
  51.3 5.9 %copy-start.9 = (bf16[1024,1024]{1,0:T(8,128)(2,1)S(1)}, bf16[1024,1024]{1,0:T(8,128)(2,1)}, u32[]{:S(2)}) copy-start(bf16[1024,1024]{1,0:T(8,128)(2,1)} %copy-done.7) | copy-start | bytes 6291460
  56.5 5.4 %collective-permute-start.18 = (bf16[64,896]{1,0:T(8,128)(2,1)S(1)}, bf16[64,896]{1,0:T(8,128)(2,1)S(1)}, u32[]{:S(2)}, u32[]{:S(2)}) collective-permute-start(bf16[64,896]{1,0:T(8,128)(2,1)S(1)} %get-tuple-element.74), channel_id=1, source_target_pairs={{0,2},{1,3},{2,0},{3,1},{4,6},{5,7},{6,4},{7,5},{8,10},{9,11},{10,... | collective-permute-start | bytes 344072 | tf_op jit(solution)/shard_map/ppermute | solution.py:46
  57.2 9.2 %copy-start = (bf16[1024,2048]{1,0:T(8,128)(2,1)S(1)}, bf16[1024,2048]{1,0:T(8,128)(2,1)}, u32[]{:S(2)}) copy-start(bf16[1024,2048]{1,0:T(8,128)(2,1)} %proj_ref.1) | copy-start | bytes 12582916
  58.1 3.8 %collective-permute-start.19 = (bf16[64,128]{1,0:T(8,128)(2,1)S(1)}, bf16[64,128]{1,0:T(8,128)(2,1)S(1)}, u32[]{:S(2)}, u32[]{:S(2)}) collective-permute-start(bf16[64,128]{1,0:T(8,128)(2,1)S(1)} %get-tuple-element.77), channel_id=1, source_target_pairs={{0,2},{1,3},{2,0},{3,1},{4,6},{5,7},{6,4},{7,5},{8,10},{9,11},{10,... | collective-permute-start | bytes 49160 | tf_op jit(solution)/shard_map/ppermute | solution.py:46
  62.0 4.9 %collective-permute-start.20 = (bf16[16,1024]{1,0:T(8,128)(2,1)S(1)}, bf16[16,1024]{1,0:T(8,128)(2,1)S(1)}, u32[]{:S(2)}, u32[]{:S(2)}) collective-permute-start(bf16[16,1024]{1,0:T(8,128)(2,1)S(1)} %get-tuple-element.79), channel_id=1, source_target_pairs={{0,4},{1,5},{2,6},{3,7},{4,0},{5,1},{6,2},{7,3},{8,12},{9,13},{10,... | collective-permute-start | bytes 98312 | tf_op jit(solution)/shard_map/ppermute | solution.py:46
  62.2 5.6 %collective-permute-start.21 = (bf16[16,1024]{1,0:T(8,128)(2,1)S(1)}, bf16[16,1024]{1,0:T(8,128)(2,1)S(1)}, u32[]{:S(2)}, u32[]{:S(2)}) collective-permute-start(bf16[16,1024]{1,0:T(8,128)(2,1)S(1)} %get-tuple-element.80), channel_id=1, source_target_pairs={{0,8},{1,9},{2,10},{3,11},{4,12},{5,13},{6,14},{7,15},{8,0},{9,1},... | collective-permute-start | bytes 98312 | tf_op jit(solution)/shard_map/ppermute | solution.py:46
  66.0 5.7 %collective-permute-start.22 = (bf16[16,1024]{1,0:T(8,128)(2,1)S(1)}, bf16[16,1024]{1,0:T(8,128)(2,1)S(1)}, u32[]{:S(2)}, u32[]{:S(2)}) collective-permute-start(bf16[16,1024]{1,0:T(8,128)(2,1)S(1)} %get-tuple-element.81), channel_id=1, source_target_pairs={{0,12},{1,13},{2,14},{3,15},{4,8},{5,9},{6,10},{7,11},{8,4},{9,5},... | collective-permute-start | bytes 98312 | tf_op jit(solution)/shard_map/ppermute | solution.py:46
  66.4 5.3 %copy-start.10 = (bf16[1024,1024]{1,0:T(8,128)(2,1)S(1)}, bf16[1024,1024]{1,0:T(8,128)(2,1)}, u32[]{:S(2)}) copy-start(bf16[1024,1024]{1,0:T(8,128)(2,1)} %refs_6_.1) | copy-start | bytes 6291460
  66.4 5.3 %copy-start.14 = (f32[1024]{0:T(1024)S(1)}, f32[1024]{0:T(1024)}, u32[]{:S(2)}) copy-start(f32[1024]{0:T(1024)} %param.24) | copy-start | bytes 12292

commit v3 on v2

--- a/solution.py
+++ b/solution.py
@@ -78,8 +78,13 @@
     *far, near = stage_masks(size)
     for bits in far[:-1]:
         x = join([x] + [swap(x, m, axis, size) for m in combos(bits)[1:]], 0)
-    pieces = [x, join([swap(x, m, axis, size) for m in combos(far[-1])[1:]], 0)]
-    return pieces + [swap(p, near[0], axis, size) for p in pieces]
+    first, *rest = combos(far[-1])[1:]
+    early = swap(x, near[0], axis, size)
+    beside = swap(x, first, axis, size)
+    others = join([swap(x, m, axis, size) for m in rest], 0)
+    late = swap(others, near[0], axis, size)
+    across = swap(early, first, axis, size)
+    return [x, beside, others, early, across, late]
 
 
 def position_bits(size):
@@ -577,9 +582,8 @@
     none = jnp.zeros((each * (size // 2), width), BF16)
     _, extra = lax.while_loop(lambda s: s[0] < rounds[0], more, (jnp.int32(1), none))
 
-    proj, keys, values, other_keys, other_values = stage(
-        width, proj_in, key_cache, value_cache, other_keys, other_values
-    )
+    (proj,) = stage(width, proj_in)
+    keys, values, other_keys, other_values = stage(width, key_cache, value_cache, other_keys, other_values)
     caches = ([keys, other_keys], [values, other_values], [bias, other_bias])
     *far, near = stage_masks(size)
     split = max(1, width // LANES * 7 // 8)

time: 73.2 us -> 59.6 us (0.81)
  local copies, waits for them, and re-layouts: 14.1 us -> 1.36 us
  starting transfers between devices: 26 us -> 18.4 us
  waiting for transfers between devices: 16 us -> 21.4 us
    unnamed x36 -> x10, local copies, waits for them, and re-layouts: 13.4 us -> 1.34 us
    ppermute x18 -> x19, starting transfers between devices: 26 us -> 18.4 us  [swap(): return lax.ppermute(x, axis, [(i, i ^ mask) for i in range(size)])]
    ppermute x18 -> x19, waiting for transfers between devices: 16 us -> 21.4 us  [swap(): return lax.ppermute(x, axis, [(i, i ^ mask) for i in range(size)])]
    pallas_call x2 -> x3, Pallas kernels: 4.26 us -> 5.25 us  [stage(): pl.pallas_call(functools.partial(stage_kernel, width=width), out_shape=tu...]
  transfers between devices with their start and end apart: 18 -> 19, of which waited for: 9 -> 8; matrix products, arithmetic and copies ran while one was open for 1% -> 1% of each run, Pallas kernels for 12% -> 17%
where the time goes in v3:
time: 59.6 us; the launch traced here: 59.4 us
  waiting for transfers between devices  21.4 us (36%)
  starting transfers between devices  18.4 us (31%)
  Pallas kernels  16 us (27%)
  local copies, waits for them, and re-layouts  1.36 us (2%)
  between operations  0.85 us (1%)
  other arithmetic  0.73 us (1%)
  loops' own time  0.65 us (1%)
    ppermute x19, waiting for transfers between devices, swap(): return lax.ppermute(x, axis, [(i, i ^ mask) for i in range(size)])  21.4 us
    ppermute x19, starting transfers between devices, swap(): return lax.ppermute(x, axis, [(i, i ^ mask) for i in range(size)])  18.4 us
    pallas_call x3, Pallas kernels, stage(): pl.pallas_call(functools.partial(stage_kernel, width=width), out_shape=tu...  5.25 us
    pallas_call x1, Pallas kernels, attend_first(): pl.pallas_call(functools.partial(attend_first_kernel, heads=heads, blocks...  4.94 us
    pallas_call x1, Pallas kernels, prepare(): pl.pallas_call(functools.partial(prepare_kernel, axis=axis, npos=pos_bias...  1.68 us
    unnamed x10, local copies, waits for them, and re-layouts  1.34 us
  transfers between devices with their start and end apart: 19, of which 8 were waited for; matrix products, arithmetic and copies ran while one was open for 1% of the time, Pallas kernels for 17%

profile of v3, /device:TPU:0, one launch (start us, length us, event | category | flops | bytes accessed | tf_op | source)
XLA Modules:
  0.0 59.4 jit_solution(10086680754369190301)
XLA Ops:
  0.0 0.5 collective-permute-start.10
  0.5 2.6 %collective-permute-start.6 = (s32[1,16]{1,0:T(1,128)}, s32[1,16]{1,0:T(1,128)S(1)}, u32[]{:S(2)}, u32[]{:S(2)}) collective-permute-start(s32[1,16]{1,0:T(1,128)} %bitcast.13), channel_id=1, source_target_pairs={{0,4},{1,5},{2,6},{3,7},{4,0},{5,1},{6,2},{7,3},{8,12},{9,13},{10,... | collective-permute-start | bytes 200 | tf_op jit(solution)/shard_map/ppermute | solution.py:46
  3.1 2.6 %collective-permute-start.7 = (s32[1,16]{1,0:T(1,128)}, s32[1,16]{1,0:T(1,128)S(1)}, u32[]{:S(2)}, u32[]{:S(2)}) collective-permute-start(s32[1,16]{1,0:T(1,128)} %bitcast.14), channel_id=1, source_target_pairs={{0,8},{1,9},{2,10},{3,11},{4,12},{5,13},{6,14},{7,15},{8,0},{9,1},... | collective-permute-start | bytes 200 | tf_op jit(solution)/shard_map/ppermute | solution.py:46
  5.6 0.0 collective-permute-start.8
  5.6 0.0 collective-permute-done.6
  5.7 2.0 %collective-permute-done.7 = s32[1,16]{1,0:T(1,128)S(1)} collective-permute-done((s32[1,16]{1,0:T(1,128)}, s32[1,16]{1,0:T(1,128)S(1)}, u32[]{:S(2)}, u32[]{:S(2)}) %collective-permute-start.7) | collective-permute-done | bytes 96 | tf_op jit(solution)/shard_map/ppermute | solution.py:46
  7.7 3.5 %collective-permute-done.8 = s32[1,16]{1,0:T(1,128)S(1)} collective-permute-done((s32[1,16]{1,0:T(1,128)}, s32[1,16]{1,0:T(1,128)S(1)}, u32[]{:S(2)}, u32[]{:S(2)}) %collective-permute-start.8) | collective-permute-done | bytes 96 | tf_op jit(solution)/shard_map/ppermute | solution.py:46
  11.1 0.7 %pad_add_fusion.refs_0_ = s32[1,64]{1,0:T(1,128)S(1)} fusion(s32[1,16]{1,0:T(1,128)S(1)} %collective-permute-done.8, s32[1,16]{1,0:T(1,128)S(1)} %collective-permute-done.7, s32[1,16]{1,0:T(1,128)S(1)} %collective-permute-done.6, s32[1,16]{1,0:T(1,128)} %bitcast.16), kind=kLoop, calls=%fused_computation.6 | loop fusion | flops 192 | bytes 512 | tf_op jit(solution)/shard_map/concatenate | solution.py:58
  11.9 1.5 %collective-permute-start.9 = (s32[1,64]{1,0:T(1,128)S(1)}, s32[1,64]{1,0:T(1,128)S(1)}, u32[]{:S(2)}, u32[]{:S(2)}) collective-permute-start(s32[1,64]{1,0:T(1,128)S(1)} %pad_add_fusion.refs_0_), channel_id=1, source_target_pairs={{0,2},{1,3},{2,0},{3,1},{4,6},{5,7},{6,4},{7,5},{8,10},{9,11},{10,... | collective-permute-start | bytes 776 | tf_op jit(solution)/shard_map/ppermute | solution.py:46
  13.4 0.0 collective-permute-start.17
  13.4 2.0 %collective-permute-done.9.refs_1_ = s32[1,64]{1,0:T(1,128)S(1)} collective-permute-done((s32[1,64]{1,0:T(1,128)S(1)}, s32[1,64]{1,0:T(1,128)S(1)}, u32[]{:S(2)}, u32[]{:S(2)}) %collective-permute-start.9) | collective-permute-done | bytes 288 | tf_op jit(solution)/shard_map/ppermute | solution.py:46
  15.4 0.9 %plan.2 = (bf16[128,256]{1,0:T(8,128)(2,1)S(1)}, s32[1]{0:T(128)}) custom-call(s32[1,64]{1,0:T(1,128)S(1)} %pad_add_fusion.refs_0_, s32[1,64]{1,0:T(1,128)S(1)} %collective-permute-done.9.refs_1_), custom_call_target="tpu_custom_call" | custom-call | tf_op jit(solution)/shard_map/plan/pallas_call | solution.py:201
  16.3 0.0 collective-permute-done.10.refs_0_
  16.4 0.7 %while.10 = (s32[]{:T(128)}, bf16[128,1024]{1,0:T(8,128)(2,1)S(1)}, s32[1]{0:T(128)}, s32[1,64]{1,0:T(1,128)S(1)}, s32[1,64]{1,0:T(1,128)S(1)}, /*index=5*/bf16[...) while((s32[]{:T(128)}, bf16[128,1024]{1,0:T(8,128)(2,1)S(1)}, s32[1]{0:T(128)}, ...), condition=%wide.region_1.0_spmd, body=%wide.region_0.0_spmd.sunk | while | flops 131074 | bytes 20447612 | solution.py:583
  17.0 0.1 collective-permute-start.18
  17.8 1.7 %prepare.1 = (bf16[1024,128]{1,0:T(8,128)(2,1)S(1)}, bf16[1024,1024]{1,0:T(8,128)(2,1)S(1)}) custom-call(s32[1]{0:T(128)S(6)} %copy.24.start_ref, s32[1,1024]{1,0:T(1,128)} %bitcast.12, f32[16,128]{1,0:T(8,128)} %time_bias_hbm.1, f32[16,18]{1,0:T(8,128)} %pos_bias_hbm.1, bf16[1024,1024]{1,0:T(8,128)(2,1)} %get-tuple-element.197), custom_call_target="tpu_custom_call" | custom-call | tf_op jit(solution)/shard_map/prepare/pallas_call | solution.py:269
  19.5 0.6 collective-permute-start.19
  20.0 0.1 stage.3.refs_3_
  20.2 0.7 %lookup.2.refs_0_ = bf16[32,1024]{1,0:T(8,128)(2,1)S(1)} custom-call(s32[1,64]{1,0:T(1,128)S(1)} %get-tuple-element.209, s32[1,64]{1,0:T(1,128)S(1)} %get-tuple-element.211, bf16[1024,1024]{1,0:T(8,128)(2,1)S(1)} %get-tuple-element.64.refs_2_, bf16[1024,1024]{1,0:T(8,128)(2,1)S(1)} %stage.3.refs_3_), custom_call_target="tpu_custom_call" | custom-call | tf_op jit(solution)/shard_map/lookup/pallas_call | solution.py:161
  20.9 0.0 collective-permute-start.12
  20.9 1.0 %collective-permute-start.13 = (bf16[32,1024]{1,0:T(8,128)(2,1)S(1)}, bf16[32,1024]{1,0:T(8,128)(2,1)S(1)}, u32[]{:S(2)}, u32[]{:S(2)}) collective-permute-start(bf16[32,1024]{1,0:T(8,128)(2,1)S(1)} %lookup.2.refs_0_), channel_id=1, source_target_pairs={{0,12},{1,13},{2,14},{3,15},{4,8},{5,9},{6,10},{7,11},{8,4},{9,5},... | collective-permute-start | bytes 196616 | tf_op jit(solution)/shard_map/ppermute | solution.py:46
  21.9 6.0 %collective-permute-done.12.refs_0_ = bf16[32,1024]{1,0:T(8,128)(2,1)S(1)} collective-permute-done((bf16[32,1024]{1,0:T(8,128)(2,1)S(1)}, bf16[32,1024]{1,0:T(8,128)(2,1)S(1)}, u32[]{:S(2)}, u32[]{:S(2)}) %collective-permute-start.12) | collective-permute-done | bytes 65568 | tf_op jit(solution)/shard_map/ppermute | solution.py:46
  27.9 1.5 %collective-permute-start.14 = (bf16[32,1024]{1,0:T(8,128)(2,1)S(1)}, bf16[32,1024]{1,0:T(8,128)(2,1)S(1)}, u32[]{:S(2)}, u32[]{:S(2)}) collective-permute-start(bf16[32,1024]{1,0:T(8,128)(2,1)S(1)} %lookup.2.refs_0_), channel_id=1, source_target_pairs={{0,2},{1,3},{2,0},{3,1},{4,6},{5,7},{6,4},{7,5},{8,10},{9,11},{10,... | collective-permute-start | bytes 196616 | tf_op jit(solution)/shard_map/ppermute | solution.py:46
  29.4 0.0 collective-permute-done.13.refs_1_
  29.5 0.6 collective-permute-start.16
  30.0 0.0 collective-permute-done.17.refs_2_
  30.0 0.8 %collective-permute-start.11 = (bf16[32,1024]{1,0:T(8,128)(2,1)S(1)}, bf16[32,1024]{1,0:T(8,128)(2,1)S(1)}, u32[]{:S(2)}, u32[]{:S(2)}) collective-permute-start(bf16[32,1024]{1,0:T(8,128)(2,1)S(1)} %lookup.2.refs_0_), channel_id=1, source_target_pairs={{0,4},{1,5},{2,6},{3,7},{4,0},{5,1},{6,2},{7,3},{8,12},{9,13},{10,... | collective-permute-start | bytes 196616 | tf_op jit(solution)/shard_map/ppermute | solution.py:46
  30.8 1.4 %collective-permute-done.14.refs_3_ = bf16[32,1024]{1,0:T(8,128)(2,1)S(1)} collective-permute-done((bf16[32,1024]{1,0:T(8,128)(2,1)S(1)}, bf16[32,1024]{1,0:T(8,128)(2,1)S(1)}, u32[]{:S(2)}, u32[]{:S(2)}) %collective-permute-start.14) | collective-permute-done | bytes 65568 | tf_op jit(solution)/shard_map/ppermute | solution.py:46
  32.2 0.0 collective-permute-start.15
  32.2 1.6 %stage.4.refs_8_ = bf16[1024,1024]{1,0:T(8,128)(2,1)S(1)} custom-call(bf16[1024,2048]{1,0:T(8,128)(2,1)} %proj_ref.1), custom_call_target="tpu_custom_call" | custom-call | tf_op jit(solution)/shard_map/stage/pallas_call | solution.py:483
  33.8 0.0 copy-start.2
  33.8 0.0 collective-permute-done.18.refs_3_
  33.8 0.0 copy-start.6
  33.8 1.3 %copy-done.6 = bf16[1024,1024]{1,0:T(8,128)(2,1)} copy-done((bf16[1024,1024]{1,0:T(8,128)(2,1)}, bf16[1024,1024]{1,0:T(8,128)(2,1)S(1)}, u32[]{:S(2)}) %copy-start.6) | copy-done | bytes 2097176
  35.2 3.5 %stage.5 = (bf16[1024,1024]{1,0:T(8,128)(2,1)S(1)}, bf16[1024,1024]{1,0:T(8,128)(2,1)S(1)}, bf16[1024,1024]{1,0:T(8,128)(2,1)S(1)}, bf16[1024,1024]{1,0:T(8,128)(2,1)S(1)}) custom-call(bf16[1024,1024]{1,0:T(8,128)(2,1)} %refs_0_.3, bf16[1024,1024]{1,0:T(8,128)(2,1)} %refs_1_.1, bf16[1024,1024]{1,0:T(8,128)(2,1)} %collective-permute-done.17.refs_2_, ...), custom_call_target="tpu_custom_call" | custom-call | tf_op jit(solution)/shard_map/stage/pallas_call | solution.py:483
  38.7 0.0 collective-permute-done.19.refs_14_.refs_5_
  38.7 0.0 collective-permute-done.11.refs_1_
  38.7 0.0 collective-permute-done.15.refs_4_
  38.7 0.0 collective-permute-done.16.refs_5_
  38.7 0.0 copy-done.2
  38.7 4.9 %attend_first.1 = (bf16[16,1024]{1,0:T(8,128)(2,1)S(1)}, f32[64,896]{1,0:T(8,128)S(1)}, bf16[64,896]{1,0:T(8,128)(2,1)S(1)}, bf16[128,128]{1,0:T(8,128)(2,1)S(1)}) custom-call(s32[1]{0:T(128)} %get-tuple-element.143.rounds_ref, bf16[128,256]{1,0:T(8,128)(2,1)S(1)} %get-tuple-element.63.pick_ref, bf16[32,1024]{1,0:T(8,128)(2,1)S(1)} %lookup.2.refs_0_, ...), custom_call_target="tpu_custom_call" | custom-call | flops 1879048192 | bytes 7340032 | tf_op jit(solution)/shard_map/attend_first/pallas_call | solution.py:403
  43.7 1.6 %collective-permute-start.20 = (bf16[64,896]{1,0:T(8,128)(2,1)S(1)}, bf16[64,896]{1,0:T(8,128)(2,1)S(1)}, u32[]{:S(2)}, u32[]{:S(2)}) collective-permute-start(bf16[64,896]{1,0:T(8,128)(2,1)S(1)} %get-tuple-element.72), channel_id=1, source_target_pairs={{0,2},{1,3},{2,0},{3,1},{4,6},{5,7},{6,4},{7,5},{8,10},{9,11},{10,... | collective-permute-start | bytes 344072 | tf_op jit(solution)/shard_map/ppermute | solution.py:46
  45.2 0.0 copy-start
  45.2 0.9 %attend_later.1 = (f32[64,128]{1,0:T(8,128)S(1)}, bf16[64,128]{1,0:T(8,128)(2,1)S(1)}) custom-call(bf16[128,128]{1,0:T(8,128)(2,1)S(1)} %get-tuple-element.73.query_ref, bf16[1024,1024]{1,0:T(8,128)(2,1)S(1)} %get-tuple-element.66.refs_9_.refs_0_, bf16[1024,1024]{1,0:T(8,128)(2,1)S(1)} %get-tuple-element.67.refs_10_.refs_1_, ...), custom_call_target="tpu_custom_call" | custom-call | flops 268435456 | bytes 1048576 | tf_op jit(solution)/shard_map/attend_later/pallas_call | solution.py:427
  46.2 0.6 collective-permute-start.21
  46.7 3.2 %collective-permute-done.21.refs_3_ = bf16[64,128]{1,0:T(8,128)(2,1)S(1)} collective-permute-done((bf16[64,128]{1,0:T(8,128)(2,1)S(1)}, bf16[64,128]{1,0:T(8,128)(2,1)S(1)}, u32[]{:S(2)}, u32[]{:S(2)}) %collective-permute-start.21) | collective-permute-done | bytes 16416 | tf_op jit(solution)/shard_map/ppermute | solution.py:46
  50.0 0.0 collective-permute-done.20.refs_1_
  50.0 2.1 %collective-permute-start.22 = (bf16[16,1024]{1,0:T(8,128)(2,1)S(1)}, bf16[16,1024]{1,0:T(8,128)(2,1)S(1)}, u32[]{:S(2)}, u32[]{:S(2)}) collective-permute-start(bf16[16,1024]{1,0:T(8,128)(2,1)S(1)} %get-tuple-element.77), channel_id=1, source_target_pairs={{0,4},{1,5},{2,6},{3,7},{4,0},{5,1},{6,2},{7,3},{8,12},{9,13},{10,... | collective-permute-start | bytes 98312 | tf_op jit(solution)/shard_map/ppermute | solution.py:46
  52.1 0.4 collective-permute-start.23
  52.5 2.1 %collective-permute-start.24 = (bf16[16,1024]{1,0:T(8,128)(2,1)S(1)}, bf16[16,1024]{1,0:T(8,128)(2,1)S(1)}, u32[]{:S(2)}, u32[]{:S(2)}) collective-permute-start(bf16[16,1024]{1,0:T(8,128)(2,1)S(1)} %get-tuple-element.79), channel_id=1, source_target_pairs={{0,12},{1,13},{2,14},{3,15},{4,8},{5,9},{6,10},{7,11},{8,4},{9,5},... | collective-permute-start | bytes 98312 | tf_op jit(solution)/shard_map/ppermute | solution.py:46
  54.5 0.0 copy-done
  54.5 0.0 copy-start.1
  54.5 0.0 copy-start.3
  54.5 0.5 gates.1.refs_4_
  55.0 0.0 collective-permute-done.22.refs_0_
  55.0 1.9 %collective-permute-done.23.refs_1_ = bf16[16,1024]{1,0:T(8,128)(2,1)S(1)} collective-permute-done((bf16[16,1024]{1,0:T(8,128)(2,1)S(1)}, bf16[16,1024]{1,0:T(8,128)(2,1)S(1)}, u32[]{:S(2)}, u32[]{:S(2)}) %collective-permute-start.23) | collective-permute-done | bytes 32800 | tf_op jit(solution)/shard_map/ppermute | solution.py:46
  56.9 1.3 %collective-permute-done.24.refs_2_ = bf16[16,1024]{1,0:T(8,128)(2,1)S(1)} collective-permute-done((bf16[16,1024]{1,0:T(8,128)(2,1)S(1)}, bf16[16,1024]{1,0:T(8,128)(2,1)S(1)}, u32[]{:S(2)}, u32[]{:S(2)}) %collective-permute-start.24) | collective-permute-done | bytes 32800 | tf_op jit(solution)/shard_map/ppermute | solution.py:46
  58.2 0.0 copy-done.1
  58.2 0.0 copy-done.3
  58.2 1.2 %finish.1 = bf16[16,1024]{1,0:T(8,128)(2,1)} custom-call(f32[16,1024]{1,0:T(8,128)S(1)} %get-tuple-element.76.own_ref, bf16[16,1024]{1,0:T(8,128)(2,1)S(1)} %collective-permute-done.22.refs_0_, bf16[16,1024]{1,0:T(8,128)(2,1)S(1)} %collective-permute-done.23.refs_1_, bf16[16,1024]{1,0:T(8,128)(2,1)S(1)} %collective-permute-done.24.refs_2_, ...), custom_call_target="tpu_custom_call" | custom-call | tf_op jit(solution)/shard_map/finish/pallas_call | solution.py:526
  (3 shorter events, 0.1 us)
Async XLA Ops:
  0.0 16.3 %collective-permute-start.10 = (bf16[1024,1024]{1,0:T(8,128)(2,1)}, bf16[1024,1024]{1,0:T(8,128)(2,1)S(1)}, u32[]{:S(2)}, u32[]{:S(2)}) collective-permute-start(bf16[1024,1024]{1,0:T(8,128)(2,1)} %table_hbm.1), channel_id=1, source_target_pairs={{0,1},{1,0},{2,3},{3,2},{4,5},{5,4},{6,7},{7,6},{8,9},{9,8},{10,11... | collective-permute-start | bytes 6291464 | tf_op jit(solution)/shard_map/ppermute | solution.py:46
  0.5 5.2 %collective-permute-start.6 = (s32[1,16]{1,0:T(1,128)}, s32[1,16]{1,0:T(1,128)S(1)}, u32[]{:S(2)}, u32[]{:S(2)}) collective-permute-start(s32[1,16]{1,0:T(1,128)} %bitcast.13), channel_id=1, source_target_pairs={{0,4},{1,5},{2,6},{3,7},{4,0},{5,1},{6,2},{7,3},{8,12},{9,13},{10,... | collective-permute-start | bytes 200 | tf_op jit(solution)/shard_map/ppermute | solution.py:46
  3.1 4.6 %collective-permute-start.7 = (s32[1,16]{1,0:T(1,128)}, s32[1,16]{1,0:T(1,128)S(1)}, u32[]{:S(2)}, u32[]{:S(2)}) collective-permute-start(s32[1,16]{1,0:T(1,128)} %bitcast.14), channel_id=1, source_target_pairs={{0,8},{1,9},{2,10},{3,11},{4,12},{5,13},{6,14},{7,15},{8,0},{9,1},... | collective-permute-start | bytes 200 | tf_op jit(solution)/shard_map/ppermute | solution.py:46
  5.6 5.5 %collective-permute-start.8 = (s32[1,16]{1,0:T(1,128)}, s32[1,16]{1,0:T(1,128)S(1)}, u32[]{:S(2)}, u32[]{:S(2)}) collective-permute-start(s32[1,16]{1,0:T(1,128)} %bitcast.15), channel_id=1, source_target_pairs={{0,12},{1,13},{2,14},{3,15},{4,8},{5,9},{6,10},{7,11},{8,4},{9,5},... | collective-permute-start | bytes 200 | tf_op jit(solution)/shard_map/ppermute | solution.py:46
  11.9 3.6 %collective-permute-start.9 = (s32[1,64]{1,0:T(1,128)S(1)}, s32[1,64]{1,0:T(1,128)S(1)}, u32[]{:S(2)}, u32[]{:S(2)}) collective-permute-start(s32[1,64]{1,0:T(1,128)S(1)} %pad_add_fusion.refs_0_), channel_id=1, source_target_pairs={{0,2},{1,3},{2,0},{3,1},{4,6},{5,7},{6,4},{7,5},{8,10},{9,11},{10,... | collective-permute-start | bytes 776 | tf_op jit(solution)/shard_map/ppermute | solution.py:46
  13.4 16.6 %collective-permute-start.17 = (bf16[1024,1024]{1,0:T(8,128)(2,1)}, bf16[1024,1024]{1,0:T(8,128)(2,1)}, u32[]{:S(2)}, u32[]{:S(2)}) collective-permute-start(bf16[1024,1024]{1,0:T(8,128)(2,1)} %refs_0_.3), channel_id=1, source_target_pairs={{0,1},{1,0},{2,3},{3,2},{4,5},{5,4},{6,7},{7,6},{8,9},{9,8},{10,11... | collective-permute-start | bytes 6291464 | tf_op jit(solution)/shard_map/ppermute | solution.py:46
  17.0 16.8 %collective-permute-start.18 = (bf16[1024,1024]{1,0:T(8,128)(2,1)}, bf16[1024,1024]{1,0:T(8,128)(2,1)S(1)}, u32[]{:S(2)}, u32[]{:S(2)}) collective-permute-start(bf16[1024,1024]{1,0:T(8,128)(2,1)} %refs_1_.1), channel_id=1, source_target_pairs={{0,1},{1,0},{2,3},{3,2},{4,5},{5,4},{6,7},{7,6},{8,9},{9,8},{10,11... | collective-permute-start | bytes 6291464 | tf_op jit(solution)/shard_map/ppermute | solution.py:46
  19.5 19.2 %collective-permute-start.19 = (bf16[1024,128]{1,0:T(8,128)(2,1)S(1)}, bf16[1024,128]{1,0:T(8,128)(2,1)S(1)}, u32[]{:S(2)}, u32[]{:S(2)}) collective-permute-start(bf16[1024,128]{1,0:T(8,128)(2,1)S(1)} %get-tuple-element.70.refs_13_.refs_4_), channel_id=1, source_target_pairs={{0,1},{1,0},{2,3},{3,2},{4,5},{5,4},{6,7},{7,6},{8,9},{9,8},{10,11... | collective-permute-start | bytes 786440 | tf_op jit(solution)/shard_map/ppermute | solution.py:46
  20.9 7.1 %collective-permute-start.12 = (bf16[32,1024]{1,0:T(8,128)(2,1)S(1)}, bf16[32,1024]{1,0:T(8,128)(2,1)S(1)}, u32[]{:S(2)}, u32[]{:S(2)}) collective-permute-start(bf16[32,1024]{1,0:T(8,128)(2,1)S(1)} %lookup.2.refs_0_), channel_id=1, source_target_pairs={{0,8},{1,9},{2,10},{3,11},{4,12},{5,13},{6,14},{7,15},{8,0},{9,1},... | collective-permute-start | bytes 196616 | tf_op jit(solution)/shard_map/ppermute | solution.py:46
  20.9 8.5 %collective-permute-start.13 = (bf16[32,1024]{1,0:T(8,128)(2,1)S(1)}, bf16[32,1024]{1,0:T(8,128)(2,1)S(1)}, u32[]{:S(2)}, u32[]{:S(2)}) collective-permute-start(bf16[32,1024]{1,0:T(8,128)(2,1)S(1)} %lookup.2.refs_0_), channel_id=1, source_target_pairs={{0,12},{1,13},{2,14},{3,15},{4,8},{5,9},{6,10},{7,11},{8,4},{9,5},... | collective-permute-start | bytes 196616 | tf_op jit(solution)/shard_map/ppermute | solution.py:46
  27.9 4.3 %collective-permute-start.14 = (bf16[32,1024]{1,0:T(8,128)(2,1)S(1)}, bf16[32,1024]{1,0:T(8,128)(2,1)S(1)}, u32[]{:S(2)}, u32[]{:S(2)}) collective-permute-start(bf16[32,1024]{1,0:T(8,128)(2,1)S(1)} %lookup.2.refs_0_), channel_id=1, source_target_pairs={{0,2},{1,3},{2,0},{3,1},{4,6},{5,7},{6,4},{7,5},{8,10},{9,11},{10,... | collective-permute-start | bytes 196616 | tf_op jit(solution)/shard_map/ppermute | solution.py:46
  29.5 9.2 %collective-permute-start.16 = (bf16[64,1024]{1,0:T(8,128)(2,1)S(1)}, bf16[64,1024]{1,0:T(8,128)(2,1)S(1)}, u32[]{:S(2)}, u32[]{:S(2)}) collective-permute-start(bf16[64,1024]{1,0:T(8,128)(2,1)S(1)} %join.2.refs_2_), channel_id=1, source_target_pairs={{0,2},{1,3},{2,0},{3,1},{4,6},{5,7},{6,4},{7,5},{8,10},{9,11},{10,... | collective-permute-start | bytes 393224 | tf_op jit(solution)/shard_map/ppermute | solution.py:46
  30.0 8.6 %collective-permute-start.11 = (bf16[32,1024]{1,0:T(8,128)(2,1)S(1)}, bf16[32,1024]{1,0:T(8,128)(2,1)S(1)}, u32[]{:S(2)}, u32[]{:S(2)}) collective-permute-start(bf16[32,1024]{1,0:T(8,128)(2,1)S(1)} %lookup.2.refs_0_), channel_id=1, source_target_pairs={{0,4},{1,5},{2,6},{3,7},{4,0},{5,1},{6,2},{7,3},{8,12},{9,13},{10,... | collective-permute-start | bytes 196616 | tf_op jit(solution)/shard_map/ppermute | solution.py:46
  32.2 6.5 %collective-permute-start.15 = (bf16[32,1024]{1,0:T(8,128)(2,1)S(1)}, bf16[32,1024]{1,0:T(8,128)(2,1)S(1)}, u32[]{:S(2)}, u32[]{:S(2)}) collective-permute-start(bf16[32,1024]{1,0:T(8,128)(2,1)S(1)} %collective-permute-done.14.refs_3_), channel_id=1, source_target_pairs={{0,4},{1,5},{2,6},{3,7},{4,0},{5,1},{6,2},{7,3},{8,12},{9,13},{10,... | collective-permute-start | bytes 196616 | tf_op jit(solution)/shard_map/ppermute | solution.py:46
  33.8 4.9 %copy-start.2 = (f32[1024]{0:T(1024)S(1)}, f32[1024]{0:T(1024)}, u32[]{:S(2)}) copy-start(f32[1024]{0:T(1024)} %param.20) | copy-start | bytes 12292
  33.8 1.3 %copy-start.6 = (bf16[1024,1024]{1,0:T(8,128)(2,1)}, bf16[1024,1024]{1,0:T(8,128)(2,1)S(1)}, u32[]{:S(2)}) copy-start(bf16[1024,1024]{1,0:T(8,128)(2,1)S(1)} %collective-permute-done.18.refs_3_) | copy-start | bytes 6291460
  43.7 6.3 %collective-permute-start.20 = (bf16[64,896]{1,0:T(8,128)(2,1)S(1)}, bf16[64,896]{1,0:T(8,128)(2,1)S(1)}, u32[]{:S(2)}, u32[]{:S(2)}) collective-permute-start(bf16[64,896]{1,0:T(8,128)(2,1)S(1)} %get-tuple-element.72), channel_id=1, source_target_pairs={{0,2},{1,3},{2,0},{3,1},{4,6},{5,7},{6,4},{7,5},{8,10},{9,11},{10,... | collective-permute-start | bytes 344072 | tf_op jit(solution)/shard_map/ppermute | solution.py:46
  45.2 9.3 %copy-start = (bf16[1024,2048]{1,0:T(8,128)(2,1)S(1)}, bf16[1024,2048]{1,0:T(8,128)(2,1)}, u32[]{:S(2)}) copy-start(bf16[1024,2048]{1,0:T(8,128)(2,1)} %proj_ref.1) | copy-start | bytes 12582916
  46.2 3.8 %collective-permute-start.21 = (bf16[64,128]{1,0:T(8,128)(2,1)S(1)}, bf16[64,128]{1,0:T(8,128)(2,1)S(1)}, u32[]{:S(2)}, u32[]{:S(2)}) collective-permute-start(bf16[64,128]{1,0:T(8,128)(2,1)S(1)} %get-tuple-element.75), channel_id=1, source_target_pairs={{0,2},{1,3},{2,0},{3,1},{4,6},{5,7},{6,4},{7,5},{8,10},{9,11},{10,... | collective-permute-start | bytes 49160 | tf_op jit(solution)/shard_map/ppermute | solution.py:46
  50.0 5.0 %collective-permute-start.22 = (bf16[16,1024]{1,0:T(8,128)(2,1)S(1)}, bf16[16,1024]{1,0:T(8,128)(2,1)S(1)}, u32[]{:S(2)}, u32[]{:S(2)}) collective-permute-start(bf16[16,1024]{1,0:T(8,128)(2,1)S(1)} %get-tuple-element.77), channel_id=1, source_target_pairs={{0,4},{1,5},{2,6},{3,7},{4,0},{5,1},{6,2},{7,3},{8,12},{9,13},{10,... | collective-permute-start | bytes 98312 | tf_op jit(solution)/shard_map/ppermute | solution.py:46
  52.1 4.8 %collective-permute-start.23 = (bf16[16,1024]{1,0:T(8,128)(2,1)S(1)}, bf16[16,1024]{1,0:T(8,128)(2,1)S(1)}, u32[]{:S(2)}, u32[]{:S(2)}) collective-permute-start(bf16[16,1024]{1,0:T(8,128)(2,1)S(1)} %get-tuple-element.78), channel_id=1, source_target_pairs={{0,8},{1,9},{2,10},{3,11},{4,12},{5,13},{6,14},{7,15},{8,0},{9,1},... | collective-permute-start | bytes 98312 | tf_op jit(solution)/shard_map/ppermute | solution.py:46
  52.5 5.7 %collective-permute-start.24 = (bf16[16,1024]{1,0:T(8,128)(2,1)S(1)}, bf16[16,1024]{1,0:T(8,128)(2,1)S(1)}, u32[]{:S(2)}, u32[]{:S(2)}) collective-permute-start(bf16[16,1024]{1,0:T(8,128)(2,1)S(1)} %get-tuple-element.79), channel_id=1, source_target_pairs={{0,12},{1,13},{2,14},{3,15},{4,8},{5,9},{6,10},{7,11},{8,4},{9,5},... | collective-permute-start | bytes 98312 | tf_op jit(solution)/shard_map/ppermute | solution.py:46
  54.5 3.7 %copy-start.1 = (bf16[1024,1024]{1,0:T(8,128)(2,1)S(1)}, bf16[1024,1024]{1,0:T(8,128)(2,1)}, u32[]{:S(2)}) copy-start(bf16[1024,1024]{1,0:T(8,128)(2,1)} %refs_6_.1) | copy-start | bytes 6291460
  54.5 3.7 %copy-start.3 = (f32[1024]{0:T(1024)S(1)}, f32[1024]{0:T(1024)}, u32[]{:S(2)}) copy-start(f32[1024]{0:T(1024)} %param.24) | copy-start | bytes 12292

commit v4 on v3

--- a/solution.py
+++ b/solution.py
@@ -14,6 +14,7 @@
 ROWS_AT_ONCE = 128
 EVENTS_AT_ONCE = 512
 STEPS_AHEAD = 2
+STAGE_COPIES = 4
 BLOCK = 16
 TN = (((0,), (0,)), ((), ()))
 NT = (((1,), (1,)), ((), ()))
@@ -172,10 +173,10 @@
 
 def plan_kernel(*refs, axis, size, slots, table_rows, first_turn):
     if first_turn:
-        *ids_refs, pick_ref, rounds_ref = refs
+        *ids_refs, pick_ref, rounds_ref, beside_ref = refs
         turn = 0
     else:
-        turn_ref, *ids_refs, pick_ref, rounds_ref = refs
+        turn_ref, *ids_refs, pick_ref, rounds_ref, beside_ref = refs
         turn = turn_ref[0]
     me = lax.axis_index(axis)
     pair, key, _ = candidates_info(ids_refs, me, size, table_rows)
@@ -184,7 +185,9 @@
     pair_col = key_col // count
     before = (key < key_col) & (key >= pair_col * count)
     rank = jnp.sum(before.astype(jnp.int32), axis=1, keepdims=True)
-    rounds_ref[0] = jnp.max(rank) // slots + 1
+    rounds = jnp.max(rank) // slots + 1
+    rounds_ref[0] = rounds
+    beside_ref[...] = jnp.full(beside_ref.shape, rounds, jnp.int32)
     away = pair_col ^ (me >> 1)
     block = jnp.zeros_like(away)
     for k, b in enumerate(position_bits(size)):
@@ -205,9 +208,10 @@
         out_shape=(
             jax.ShapeDtypeStruct((count, size // 2 * slots), BF16),
             jax.ShapeDtypeStruct((1,), jnp.int32),
+            jax.ShapeDtypeStruct((8, LANES), jnp.int32),
         ),
         in_specs=([] if first_turn else [SMEM]) + [VMEM] * len(ids),
-        out_specs=(VMEM, SMEM),
+        out_specs=(VMEM, SMEM, VMEM),
         compiler_params=params(16),
         name="plan",
     )(*([] if first_turn else [turn]), *ids)
@@ -361,7 +365,7 @@
     emb_ref[...] = jnp.dot(pick_ref[...], rows, preferred_element_type=F32).astype(BF16)
 
 
-    @pl.when(rounds_ref[0] > 1)
+    @pl.when(jnp.max(rounds_ref[...]) > 1)
     def _():
         extra = pltpu.make_async_copy(extra_hbm, query_ref, sem)
         extra.start()
@@ -408,7 +412,7 @@
             jax.ShapeDtypeStruct((count // 2, columns), BF16),
             jax.ShapeDtypeStruct((count, width - columns), BF16),
         ),
-        in_specs=[SMEM, VMEM] + [VMEM] * len(pieces) + [HBM] + [VMEM] * (2 + 3 * blocks),
+        in_specs=[VMEM, VMEM] + [VMEM] * len(pieces) + [HBM] + [VMEM] * (2 + 3 * blocks),
         out_specs=(VMEM,) * 4,
         scratch_shapes=[
             pltpu.VMEM((count, width), BF16),
@@ -467,12 +471,12 @@
 def stage_kernel(*refs, width):
     *refs, sems = refs
     count = len(refs) // 2
-    copies = [
-        pltpu.make_async_copy(
-            a if a.shape[1] == width else a.at[:, pl.ds(0, width)], b, sems.at[k]
-        )
-        for k, (a, b) in enumerate(zip(refs[:count], refs[count:]))
-    ]
+    copies = []
+    for k, (a, b) in enumerate(zip(refs[:count], refs[count:])):
+        rows = a.shape[0] // STAGE_COPIES
+        for c in range(STAGE_COPIES):
+            part = pl.ds(c * rows, rows)
+            copies.append(pltpu.make_async_copy(a.at[part, pl.ds(0, width)], b.at[part, :], sems.at[k, c]))
     for c in copies:
         c.start()
     for c in copies:
@@ -485,7 +489,7 @@
         out_shape=tuple(jax.ShapeDtypeStruct((a.shape[0], width), BF16) for a in arrays),
         in_specs=[HBM if held else pl.BlockSpec(memory_space=pl.ANY)] * len(arrays),
         out_specs=(VMEM,) * len(arrays),
-        scratch_shapes=[pltpu.SemaphoreType.DMA((len(arrays),))],
+        scratch_shapes=[pltpu.SemaphoreType.DMA((len(arrays), STAGE_COPIES))],
         compiler_params=params(4),
         name="stage",
     )(*(pltpu.with_memory_space_constraint(a, pltpu.HBM) if held else a for a in arrays))
@@ -571,23 +575,23 @@
     (near_table,) = stage(width, other_table, held=False)
     found = lookup(ids, [own_table, near_table], slots, axis, size)
     pieces = gather_rows(found, axis, size)
-    pick, rounds = plan(ids, slots, table_rows, axis, size)
+    pick, rounds, told = plan(ids, slots, table_rows, axis, size)
 
     def more(state):
         turn, so_far = state
-        picked, _ = plan(ids, slots, table_rows, axis, size, turn[None])
+        picked, *_ = plan(ids, slots, table_rows, axis, size, turn[None])
         found = lookup(ids, [item_table, other_table], slots, axis, size, turn[None])
         return turn + 1, so_far + select(picked, gather_rows(found, axis, size))
 
     none = jnp.zeros((each * (size // 2), width), BF16)
     _, extra = lax.while_loop(lambda s: s[0] < rounds[0], more, (jnp.int32(1), none))
 
-    (proj,) = stage(width, proj_in)
-    keys, values, other_keys, other_values = stage(width, key_cache, value_cache, other_keys, other_values)
+    (keys,) = stage(width, key_cache)
+    proj, values, other_keys, other_values = stage(width, proj_in, value_cache, other_keys, other_values)
     caches = ([keys, other_keys], [values, other_values], [bias, other_bias])
     *far, near = stage_masks(size)
     split = max(1, width // LANES * 7 // 8)
-    own, keep, send, later = attend_first(rounds, pick, pieces, extra, gain, proj, *caches, heads, each, split)
+    own, keep, send, later = attend_first(told, pick, pieces, extra, gain, proj, *caches, heads, each, split)
     halves = [keep, swap(send, near[0], axis, size)]
     keep, send = attend_later(later, *caches, heads, split)
     halves += [keep, swap(send, near[0], axis, size)]

time: 59.6 us -> 59.3 us (level)
  no operation moved by 1% of the time
where the time goes in v4:
time: 59.3 us; the launch traced here: 59.1 us
  waiting for transfers between devices  21.4 us (36%)
  starting transfers between devices  18.4 us (31%)
  Pallas kernels  15.7 us (26%)
  local copies, waits for them, and re-layouts  1.36 us (2%)
  between operations  0.85 us (1%)
  other arithmetic  0.73 us (1%)
  loops' own time  0.69 us (1%)
    ppermute x19, waiting for transfers between devices, swap(): return lax.ppermute(x, axis, [(i, i ^ mask) for i in range(size)])  21.4 us
    ppermute x19, starting transfers between devices, swap(): return lax.ppermute(x, axis, [(i, i ^ mask) for i in range(size)])  18.4 us
    pallas_call x3, Pallas kernels, stage(): pl.pallas_call(functools.partial(stage_kernel, width=width), out_shape=tu...  5.24 us
    pallas_call x1, Pallas kernels, attend_first(): pl.pallas_call(functools.partial(attend_first_kernel, heads=heads, blocks...  4.6 us
    pallas_call x1, Pallas kernels, prepare(): pl.pallas_call(functools.partial(prepare_kernel, axis=axis, npos=pos_bias...  1.68 us
    unnamed x10, local copies, waits for them, and re-layouts  1.34 us
  transfers between devices with their start and end apart: 19, of which 8 were waited for; matrix products, arithmetic and copies ran while one was open for 1% of the time, Pallas kernels for 17%

profile of v4, /device:TPU:0, one launch (start us, length us, event | category | flops | bytes accessed | tf_op | source)
XLA Modules:
  0.0 59.1 jit_solution(8847244485180770678)
XLA Ops:
  0.0 0.5 collective-permute-start.10
  0.5 2.6 %collective-permute-start.6 = (s32[1,16]{1,0:T(1,128)}, s32[1,16]{1,0:T(1,128)S(1)}, u32[]{:S(2)}, u32[]{:S(2)}) collective-permute-start(s32[1,16]{1,0:T(1,128)} %bitcast.13), channel_id=1, source_target_pairs={{0,4},{1,5},{2,6},{3,7},{4,0},{5,1},{6,2},{7,3},{8,12},{9,13},{10,... | collective-permute-start | bytes 200 | tf_op jit(solution)/shard_map/ppermute | solution.py:47
  3.1 2.6 %collective-permute-start.7 = (s32[1,16]{1,0:T(1,128)}, s32[1,16]{1,0:T(1,128)S(1)}, u32[]{:S(2)}, u32[]{:S(2)}) collective-permute-start(s32[1,16]{1,0:T(1,128)} %bitcast.14), channel_id=1, source_target_pairs={{0,8},{1,9},{2,10},{3,11},{4,12},{5,13},{6,14},{7,15},{8,0},{9,1},... | collective-permute-start | bytes 200 | tf_op jit(solution)/shard_map/ppermute | solution.py:47
  5.6 0.0 collective-permute-start.8
  5.6 0.0 collective-permute-done.6
  5.7 2.0 %collective-permute-done.7 = s32[1,16]{1,0:T(1,128)S(1)} collective-permute-done((s32[1,16]{1,0:T(1,128)}, s32[1,16]{1,0:T(1,128)S(1)}, u32[]{:S(2)}, u32[]{:S(2)}) %collective-permute-start.7) | collective-permute-done | bytes 96 | tf_op jit(solution)/shard_map/ppermute | solution.py:47
  7.7 3.5 %collective-permute-done.8 = s32[1,16]{1,0:T(1,128)S(1)} collective-permute-done((s32[1,16]{1,0:T(1,128)}, s32[1,16]{1,0:T(1,128)S(1)}, u32[]{:S(2)}, u32[]{:S(2)}) %collective-permute-start.8) | collective-permute-done | bytes 96 | tf_op jit(solution)/shard_map/ppermute | solution.py:47
  11.1 0.7 %pad_add_fusion.refs_0_ = s32[1,64]{1,0:T(1,128)S(1)} fusion(s32[1,16]{1,0:T(1,128)S(1)} %collective-permute-done.8, s32[1,16]{1,0:T(1,128)S(1)} %collective-permute-done.7, s32[1,16]{1,0:T(1,128)S(1)} %collective-permute-done.6, s32[1,16]{1,0:T(1,128)} %bitcast.16), kind=kLoop, calls=%fused_computation.6 | loop fusion | flops 192 | bytes 512 | tf_op jit(solution)/shard_map/concatenate | solution.py:59
  11.9 1.5 %collective-permute-start.9 = (s32[1,64]{1,0:T(1,128)S(1)}, s32[1,64]{1,0:T(1,128)S(1)}, u32[]{:S(2)}, u32[]{:S(2)}) collective-permute-start(s32[1,64]{1,0:T(1,128)S(1)} %pad_add_fusion.refs_0_), channel_id=1, source_target_pairs={{0,2},{1,3},{2,0},{3,1},{4,6},{5,7},{6,4},{7,5},{8,10},{9,11},{10,... | collective-permute-start | bytes 776 | tf_op jit(solution)/shard_map/ppermute | solution.py:47
  13.4 0.0 collective-permute-start.17
  13.4 2.0 %collective-permute-done.9.refs_1_ = s32[1,64]{1,0:T(1,128)S(1)} collective-permute-done((s32[1,64]{1,0:T(1,128)S(1)}, s32[1,64]{1,0:T(1,128)S(1)}, u32[]{:S(2)}, u32[]{:S(2)}) %collective-permute-start.9) | collective-permute-done | bytes 288 | tf_op jit(solution)/shard_map/ppermute | solution.py:47
  15.4 0.9 %plan.2 = (bf16[128,256]{1,0:T(8,128)(2,1)S(1)}, s32[1]{0:T(128)}, s32[8,128]{1,0:T(8,128)S(1)}) custom-call(s32[1,64]{1,0:T(1,128)S(1)} %pad_add_fusion.refs_0_, s32[1,64]{1,0:T(1,128)S(1)} %collective-permute-done.9.refs_1_), custom_call_target="tpu_custom_call" | custom-call | tf_op jit(solution)/shard_map/plan/pallas_call | solution.py:204
  16.3 0.0 collective-permute-done.10.refs_0_
  16.4 0.7 %while.10 = (s32[]{:T(128)}, bf16[128,1024]{1,0:T(8,128)(2,1)S(1)}, s32[1]{0:T(128)}, s32[1,64]{1,0:T(1,128)S(1)}, s32[1,64]{1,0:T(1,128)S(1)}, /*index=5*/bf16[...) while((s32[]{:T(128)}, bf16[128,1024]{1,0:T(8,128)(2,1)S(1)}, s32[1]{0:T(128)}, ...), condition=%wide.region_1.0_spmd, body=%wide.region_0.0_spmd.sunk | while | flops 131074 | bytes 20447612 | solution.py:587
  17.1 0.1 collective-permute-start.18
  17.8 1.7 %prepare.1 = (bf16[1024,128]{1,0:T(8,128)(2,1)S(1)}, bf16[1024,1024]{1,0:T(8,128)(2,1)S(1)}) custom-call(s32[1]{0:T(128)S(6)} %copy.24.start_ref, s32[1,1024]{1,0:T(1,128)} %bitcast.12, f32[16,128]{1,0:T(8,128)} %time_bias_hbm.1, f32[16,18]{1,0:T(8,128)} %pos_bias_hbm.1, bf16[1024,1024]{1,0:T(8,128)(2,1)} %get-tuple-element.199), custom_call_target="tpu_custom_call" | custom-call | tf_op jit(solution)/shard_map/prepare/pallas_call | solution.py:273
  19.5 0.6 collective-permute-start.19
  20.1 0.2 stage.3.refs_3_
  20.2 0.7 %lookup.2.refs_0_ = bf16[32,1024]{1,0:T(8,128)(2,1)S(1)} custom-call(s32[1,64]{1,0:T(1,128)S(1)} %get-tuple-element.211, s32[1,64]{1,0:T(1,128)S(1)} %get-tuple-element.213, bf16[1024,1024]{1,0:T(8,128)(2,1)S(1)} %get-tuple-element.65.refs_2_, bf16[1024,1024]{1,0:T(8,128)(2,1)S(1)} %stage.3.refs_3_), custom_call_target="tpu_custom_call" | custom-call | tf_op jit(solution)/shard_map/lookup/pallas_call | solution.py:162
  20.9 0.0 collective-permute-start.12
  21.0 1.0 %collective-permute-start.13 = (bf16[32,1024]{1,0:T(8,128)(2,1)S(1)}, bf16[32,1024]{1,0:T(8,128)(2,1)S(1)}, u32[]{:S(2)}, u32[]{:S(2)}) collective-permute-start(bf16[32,1024]{1,0:T(8,128)(2,1)S(1)} %lookup.2.refs_0_), channel_id=1, source_target_pairs={{0,12},{1,13},{2,14},{3,15},{4,8},{5,9},{6,10},{7,11},{8,4},{9,5},... | collective-permute-start | bytes 196616 | tf_op jit(solution)/shard_map/ppermute | solution.py:47
  22.0 6.0 %collective-permute-done.12.refs_0_ = bf16[32,1024]{1,0:T(8,128)(2,1)S(1)} collective-permute-done((bf16[32,1024]{1,0:T(8,128)(2,1)S(1)}, bf16[32,1024]{1,0:T(8,128)(2,1)S(1)}, u32[]{:S(2)}, u32[]{:S(2)}) %collective-permute-start.12) | collective-permute-done | bytes 65568 | tf_op jit(solution)/shard_map/ppermute | solution.py:47
  28.0 1.5 %collective-permute-start.14 = (bf16[32,1024]{1,0:T(8,128)(2,1)S(1)}, bf16[32,1024]{1,0:T(8,128)(2,1)S(1)}, u32[]{:S(2)}, u32[]{:S(2)}) collective-permute-start(bf16[32,1024]{1,0:T(8,128)(2,1)S(1)} %lookup.2.refs_0_), channel_id=1, source_target_pairs={{0,2},{1,3},{2,0},{3,1},{4,6},{5,7},{6,4},{7,5},{8,10},{9,11},{10,... | collective-permute-start | bytes 196616 | tf_op jit(solution)/shard_map/ppermute | solution.py:47
  29.5 0.0 collective-permute-done.13.refs_1_
  29.5 0.6 collective-permute-start.16
  30.1 0.0 collective-permute-done.17.refs_2_
  30.1 0.8 %collective-permute-start.11 = (bf16[32,1024]{1,0:T(8,128)(2,1)S(1)}, bf16[32,1024]{1,0:T(8,128)(2,1)S(1)}, u32[]{:S(2)}, u32[]{:S(2)}) collective-permute-start(bf16[32,1024]{1,0:T(8,128)(2,1)S(1)} %lookup.2.refs_0_), channel_id=1, source_target_pairs={{0,4},{1,5},{2,6},{3,7},{4,0},{5,1},{6,2},{7,3},{8,12},{9,13},{10,... | collective-permute-start | bytes 196616 | tf_op jit(solution)/shard_map/ppermute | solution.py:47
  30.8 1.4 %collective-permute-done.14.refs_3_ = bf16[32,1024]{1,0:T(8,128)(2,1)S(1)} collective-permute-done((bf16[32,1024]{1,0:T(8,128)(2,1)S(1)}, bf16[32,1024]{1,0:T(8,128)(2,1)S(1)}, u32[]{:S(2)}, u32[]{:S(2)}) %collective-permute-start.14) | collective-permute-done | bytes 65568 | tf_op jit(solution)/shard_map/ppermute | solution.py:47
  32.2 0.0 collective-permute-start.15
  32.2 1.5 %stage.5.refs_9_.refs_0_ = bf16[1024,1024]{1,0:T(8,128)(2,1)S(1)} custom-call(bf16[1024,1024]{1,0:T(8,128)(2,1)} %refs_0_.3), custom_call_target="tpu_custom_call" | custom-call | tf_op jit(solution)/shard_map/stage/pallas_call | solution.py:487
  33.8 0.0 copy-start.2
  33.8 0.0 collective-permute-done.18.refs_3_
  33.8 0.0 copy-start.6
  33.8 1.3 %copy-done.6 = bf16[1024,1024]{1,0:T(8,128)(2,1)} copy-done((bf16[1024,1024]{1,0:T(8,128)(2,1)}, bf16[1024,1024]{1,0:T(8,128)(2,1)S(1)}, u32[]{:S(2)}) %copy-start.6) | copy-done | bytes 2097176
  35.2 3.5 %stage.4 = (bf16[1024,1024]{1,0:T(8,128)(2,1)S(1)}, bf16[1024,1024]{1,0:T(8,128)(2,1)S(1)}, bf16[1024,1024]{1,0:T(8,128)(2,1)S(1)}, bf16[1024,1024]{1,0:T(8,128)(2,1)S(1)}) custom-call(bf16[1024,2048]{1,0:T(8,128)(2,1)} %proj_ref.1, bf16[1024,1024]{1,0:T(8,128)(2,1)} %refs_1_.1, bf16[1024,1024]{1,0:T(8,128)(2,1)} %collective-permute-done.17.refs_2_, ...), custom_call_target="tpu_custom_call" | custom-call | tf_op jit(solution)/shard_map/stage/pallas_call | solution.py:487
  38.7 0.0 collective-permute-done.19.refs_14_.refs_5_
  38.7 0.0 collective-permute-done.11.refs_1_
  38.7 0.0 collective-permute-done.15.refs_4_
  38.7 0.0 collective-permute-done.16.refs_5_
  38.7 0.0 copy-done.2
  38.7 4.6 %attend_first.1 = (bf16[16,1024]{1,0:T(8,128)(2,1)S(1)}, f32[64,896]{1,0:T(8,128)S(1)}, bf16[64,896]{1,0:T(8,128)(2,1)S(1)}, bf16[128,128]{1,0:T(8,128)(2,1)S(1)}) custom-call(s32[8,128]{1,0:T(8,128)S(1)} %get-tuple-element.63.rounds_ref, bf16[128,256]{1,0:T(8,128)(2,1)S(1)} %get-tuple-element.64.pick_ref, bf16[32,1024]{1,0:T(8,128)(2,1)S(1)} %lookup.2.refs_0_, ...), custom_call_target="tpu_custom_call" | custom-call | flops 1879048192 | bytes 7340032 | tf_op jit(solution)/shard_map/attend_first/pallas_call | solution.py:407
  43.3 1.6 %collective-permute-start.20 = (bf16[64,896]{1,0:T(8,128)(2,1)S(1)}, bf16[64,896]{1,0:T(8,128)(2,1)S(1)}, u32[]{:S(2)}, u32[]{:S(2)}) collective-permute-start(bf16[64,896]{1,0:T(8,128)(2,1)S(1)} %get-tuple-element.74), channel_id=1, source_target_pairs={{0,2},{1,3},{2,0},{3,1},{4,6},{5,7},{6,4},{7,5},{8,10},{9,11},{10,... | collective-permute-start | bytes 344072 | tf_op jit(solution)/shard_map/ppermute | solution.py:47
  44.9 0.0 copy-start
  44.9 0.9 %attend_later.1 = (f32[64,128]{1,0:T(8,128)S(1)}, bf16[64,128]{1,0:T(8,128)(2,1)S(1)}) custom-call(bf16[128,128]{1,0:T(8,128)(2,1)S(1)} %get-tuple-element.75.query_ref, bf16[1024,1024]{1,0:T(8,128)(2,1)S(1)} %stage.5.refs_9_.refs_0_, bf16[1024,1024]{1,0:T(8,128)(2,1)S(1)} %get-tuple-element.69.refs_10_.refs_1_, ...), custom_call_target="tpu_custom_call" | custom-call | flops 268435456 | bytes 1048576 | tf_op jit(solution)/shard_map/attend_later/pallas_call | solution.py:431
  45.8 0.6 collective-permute-start.21
  46.4 3.2 %collective-permute-done.21.refs_3_ = bf16[64,128]{1,0:T(8,128)(2,1)S(1)} collective-permute-done((bf16[64,128]{1,0:T(8,128)(2,1)S(1)}, bf16[64,128]{1,0:T(8,128)(2,1)S(1)}, u32[]{:S(2)}, u32[]{:S(2)}) %collective-permute-start.21) | collective-permute-done | bytes 16416 | tf_op jit(solution)/shard_map/ppermute | solution.py:47
  49.6 0.0 collective-permute-done.20.refs_1_
  49.7 2.1 %collective-permute-start.22 = (bf16[16,1024]{1,0:T(8,128)(2,1)S(1)}, bf16[16,1024]{1,0:T(8,128)(2,1)S(1)}, u32[]{:S(2)}, u32[]{:S(2)}) collective-permute-start(bf16[16,1024]{1,0:T(8,128)(2,1)S(1)} %get-tuple-element.79), channel_id=1, source_target_pairs={{0,4},{1,5},{2,6},{3,7},{4,0},{5,1},{6,2},{7,3},{8,12},{9,13},{10,... | collective-permute-start | bytes 98312 | tf_op jit(solution)/shard_map/ppermute | solution.py:47
  51.8 0.4 collective-permute-start.23
  52.2 2.0 %collective-permute-start.24 = (bf16[16,1024]{1,0:T(8,128)(2,1)S(1)}, bf16[16,1024]{1,0:T(8,128)(2,1)S(1)}, u32[]{:S(2)}, u32[]{:S(2)}) collective-permute-start(bf16[16,1024]{1,0:T(8,128)(2,1)S(1)} %get-tuple-element.81), channel_id=1, source_target_pairs={{0,12},{1,13},{2,14},{3,15},{4,8},{5,9},{6,10},{7,11},{8,4},{9,5},... | collective-permute-start | bytes 98312 | tf_op jit(solution)/shard_map/ppermute | solution.py:47
  54.2 0.0 copy-done
  54.2 0.0 copy-start.1
  54.2 0.0 copy-start.3
  54.2 0.5 gates.1.refs_4_
  54.7 0.0 collective-permute-done.22.refs_0_
  54.7 1.9 %collective-permute-done.23.refs_1_ = bf16[16,1024]{1,0:T(8,128)(2,1)S(1)} collective-permute-done((bf16[16,1024]{1,0:T(8,128)(2,1)S(1)}, bf16[16,1024]{1,0:T(8,128)(2,1)S(1)}, u32[]{:S(2)}, u32[]{:S(2)}) %collective-permute-start.23) | collective-permute-done | bytes 32800 | tf_op jit(solution)/shard_map/ppermute | solution.py:47
  56.6 1.3 %collective-permute-done.24.refs_2_ = bf16[16,1024]{1,0:T(8,128)(2,1)S(1)} collective-permute-done((bf16[16,1024]{1,0:T(8,128)(2,1)S(1)}, bf16[16,1024]{1,0:T(8,128)(2,1)S(1)}, u32[]{:S(2)}, u32[]{:S(2)}) %collective-permute-start.24) | collective-permute-done | bytes 32800 | tf_op jit(solution)/shard_map/ppermute | solution.py:47
  57.9 0.0 copy-done.1
  57.9 0.0 copy-done.3
  57.9 1.2 %finish.1 = bf16[16,1024]{1,0:T(8,128)(2,1)} custom-call(f32[16,1024]{1,0:T(8,128)S(1)} %get-tuple-element.78.own_ref, bf16[16,1024]{1,0:T(8,128)(2,1)S(1)} %collective-permute-done.22.refs_0_, bf16[16,1024]{1,0:T(8,128)(2,1)S(1)} %collective-permute-done.23.refs_1_, bf16[16,1024]{1,0:T(8,128)(2,1)S(1)} %collective-permute-done.24.refs_2_, ...), custom_call_target="tpu_custom_call" | custom-call | tf_op jit(solution)/shard_map/finish/pallas_call | solution.py:530
  (3 shorter events, 0.1 us)
Async XLA Ops:
  0.0 16.3 %collective-permute-start.10 = (bf16[1024,1024]{1,0:T(8,128)(2,1)}, bf16[1024,1024]{1,0:T(8,128)(2,1)S(1)}, u32[]{:S(2)}, u32[]{:S(2)}) collective-permute-start(bf16[1024,1024]{1,0:T(8,128)(2,1)} %table_hbm.1), channel_id=1, source_target_pairs={{0,1},{1,0},{2,3},{3,2},{4,5},{5,4},{6,7},{7,6},{8,9},{9,8},{10,11... | collective-permute-start | bytes 6291464 | tf_op jit(solution)/shard_map/ppermute | solution.py:47
  0.5 5.2 %collective-permute-start.6 = (s32[1,16]{1,0:T(1,128)}, s32[1,16]{1,0:T(1,128)S(1)}, u32[]{:S(2)}, u32[]{:S(2)}) collective-permute-start(s32[1,16]{1,0:T(1,128)} %bitcast.13), channel_id=1, source_target_pairs={{0,4},{1,5},{2,6},{3,7},{4,0},{5,1},{6,2},{7,3},{8,12},{9,13},{10,... | collective-permute-start | bytes 200 | tf_op jit(solution)/shard_map/ppermute | solution.py:47
  3.1 4.6 %collective-permute-start.7 = (s32[1,16]{1,0:T(1,128)}, s32[1,16]{1,0:T(1,128)S(1)}, u32[]{:S(2)}, u32[]{:S(2)}) collective-permute-start(s32[1,16]{1,0:T(1,128)} %bitcast.14), channel_id=1, source_target_pairs={{0,8},{1,9},{2,10},{3,11},{4,12},{5,13},{6,14},{7,15},{8,0},{9,1},... | collective-permute-start | bytes 200 | tf_op jit(solution)/shard_map/ppermute | solution.py:47
  5.6 5.5 %collective-permute-start.8 = (s32[1,16]{1,0:T(1,128)}, s32[1,16]{1,0:T(1,128)S(1)}, u32[]{:S(2)}, u32[]{:S(2)}) collective-permute-start(s32[1,16]{1,0:T(1,128)} %bitcast.15), channel_id=1, source_target_pairs={{0,12},{1,13},{2,14},{3,15},{4,8},{5,9},{6,10},{7,11},{8,4},{9,5},... | collective-permute-start | bytes 200 | tf_op jit(solution)/shard_map/ppermute | solution.py:47
  11.9 3.6 %collective-permute-start.9 = (s32[1,64]{1,0:T(1,128)S(1)}, s32[1,64]{1,0:T(1,128)S(1)}, u32[]{:S(2)}, u32[]{:S(2)}) collective-permute-start(s32[1,64]{1,0:T(1,128)S(1)} %pad_add_fusion.refs_0_), channel_id=1, source_target_pairs={{0,2},{1,3},{2,0},{3,1},{4,6},{5,7},{6,4},{7,5},{8,10},{9,11},{10,... | collective-permute-start | bytes 776 | tf_op jit(solution)/shard_map/ppermute | solution.py:47
  13.4 16.7 %collective-permute-start.17 = (bf16[1024,1024]{1,0:T(8,128)(2,1)}, bf16[1024,1024]{1,0:T(8,128)(2,1)}, u32[]{:S(2)}, u32[]{:S(2)}) collective-permute-start(bf16[1024,1024]{1,0:T(8,128)(2,1)} %refs_0_.3), channel_id=1, source_target_pairs={{0,1},{1,0},{2,3},{3,2},{4,5},{5,4},{6,7},{7,6},{8,9},{9,8},{10,11... | collective-permute-start | bytes 6291464 | tf_op jit(solution)/shard_map/ppermute | solution.py:47
  17.1 16.7 %collective-permute-start.18 = (bf16[1024,1024]{1,0:T(8,128)(2,1)}, bf16[1024,1024]{1,0:T(8,128)(2,1)S(1)}, u32[]{:S(2)}, u32[]{:S(2)}) collective-permute-start(bf16[1024,1024]{1,0:T(8,128)(2,1)} %refs_1_.1), channel_id=1, source_target_pairs={{0,1},{1,0},{2,3},{3,2},{4,5},{5,4},{6,7},{7,6},{8,9},{9,8},{10,11... | collective-permute-start | bytes 6291464 | tf_op jit(solution)/shard_map/ppermute | solution.py:47
  19.5 19.2 %collective-permute-start.19 = (bf16[1024,128]{1,0:T(8,128)(2,1)S(1)}, bf16[1024,128]{1,0:T(8,128)(2,1)S(1)}, u32[]{:S(2)}, u32[]{:S(2)}) collective-permute-start(bf16[1024,128]{1,0:T(8,128)(2,1)S(1)} %get-tuple-element.72.refs_13_.refs_4_), channel_id=1, source_target_pairs={{0,1},{1,0},{2,3},{3,2},{4,5},{5,4},{6,7},{7,6},{8,9},{9,8},{10,11... | collective-permute-start | bytes 786440 | tf_op jit(solution)/shard_map/ppermute | solution.py:47
  20.9 7.0 %collective-permute-start.12 = (bf16[32,1024]{1,0:T(8,128)(2,1)S(1)}, bf16[32,1024]{1,0:T(8,128)(2,1)S(1)}, u32[]{:S(2)}, u32[]{:S(2)}) collective-permute-start(bf16[32,1024]{1,0:T(8,128)(2,1)S(1)} %lookup.2.refs_0_), channel_id=1, source_target_pairs={{0,8},{1,9},{2,10},{3,11},{4,12},{5,13},{6,14},{7,15},{8,0},{9,1},... | collective-permute-start | bytes 196616 | tf_op jit(solution)/shard_map/ppermute | solution.py:47
  21.0 8.5 %collective-permute-start.13 = (bf16[32,1024]{1,0:T(8,128)(2,1)S(1)}, bf16[32,1024]{1,0:T(8,128)(2,1)S(1)}, u32[]{:S(2)}, u32[]{:S(2)}) collective-permute-start(bf16[32,1024]{1,0:T(8,128)(2,1)S(1)} %lookup.2.refs_0_), channel_id=1, source_target_pairs={{0,12},{1,13},{2,14},{3,15},{4,8},{5,9},{6,10},{7,11},{8,4},{9,5},... | collective-permute-start | bytes 196616 | tf_op jit(solution)/shard_map/ppermute | solution.py:47
  28.0 4.3 %collective-permute-start.14 = (bf16[32,1024]{1,0:T(8,128)(2,1)S(1)}, bf16[32,1024]{1,0:T(8,128)(2,1)S(1)}, u32[]{:S(2)}, u32[]{:S(2)}) collective-permute-start(bf16[32,1024]{1,0:T(8,128)(2,1)S(1)} %lookup.2.refs_0_), channel_id=1, source_target_pairs={{0,2},{1,3},{2,0},{3,1},{4,6},{5,7},{6,4},{7,5},{8,10},{9,11},{10,... | collective-permute-start | bytes 196616 | tf_op jit(solution)/shard_map/ppermute | solution.py:47
  29.5 9.2 %collective-permute-start.16 = (bf16[64,1024]{1,0:T(8,128)(2,1)S(1)}, bf16[64,1024]{1,0:T(8,128)(2,1)S(1)}, u32[]{:S(2)}, u32[]{:S(2)}) collective-permute-start(bf16[64,1024]{1,0:T(8,128)(2,1)S(1)} %join.2.refs_2_), channel_id=1, source_target_pairs={{0,2},{1,3},{2,0},{3,1},{4,6},{5,7},{6,4},{7,5},{8,10},{9,11},{10,... | collective-permute-start | bytes 393224 | tf_op jit(solution)/shard_map/ppermute | solution.py:47
  30.1 8.6 %collective-permute-start.11 = (bf16[32,1024]{1,0:T(8,128)(2,1)S(1)}, bf16[32,1024]{1,0:T(8,128)(2,1)S(1)}, u32[]{:S(2)}, u32[]{:S(2)}) collective-permute-start(bf16[32,1024]{1,0:T(8,128)(2,1)S(1)} %lookup.2.refs_0_), channel_id=1, source_target_pairs={{0,4},{1,5},{2,6},{3,7},{4,0},{5,1},{6,2},{7,3},{8,12},{9,13},{10,... | collective-permute-start | bytes 196616 | tf_op jit(solution)/shard_map/ppermute | solution.py:47
  32.2 6.5 %collective-permute-start.15 = (bf16[32,1024]{1,0:T(8,128)(2,1)S(1)}, bf16[32,1024]{1,0:T(8,128)(2,1)S(1)}, u32[]{:S(2)}, u32[]{:S(2)}) collective-permute-start(bf16[32,1024]{1,0:T(8,128)(2,1)S(1)} %collective-permute-done.14.refs_3_), channel_id=1, source_target_pairs={{0,4},{1,5},{2,6},{3,7},{4,0},{5,1},{6,2},{7,3},{8,12},{9,13},{10,... | collective-permute-start | bytes 196616 | tf_op jit(solution)/shard_map/ppermute | solution.py:47
  33.8 4.9 %copy-start.2 = (f32[1024]{0:T(1024)S(1)}, f32[1024]{0:T(1024)}, u32[]{:S(2)}) copy-start(f32[1024]{0:T(1024)} %param.20) | copy-start | bytes 12292
  33.8 1.3 %copy-start.6 = (bf16[1024,1024]{1,0:T(8,128)(2,1)}, bf16[1024,1024]{1,0:T(8,128)(2,1)S(1)}, u32[]{:S(2)}) copy-start(bf16[1024,1024]{1,0:T(8,128)(2,1)S(1)} %collective-permute-done.18.refs_3_) | copy-start | bytes 6291460
  43.3 6.3 %collective-permute-start.20 = (bf16[64,896]{1,0:T(8,128)(2,1)S(1)}, bf16[64,896]{1,0:T(8,128)(2,1)S(1)}, u32[]{:S(2)}, u32[]{:S(2)}) collective-permute-start(bf16[64,896]{1,0:T(8,128)(2,1)S(1)} %get-tuple-element.74), channel_id=1, source_target_pairs={{0,2},{1,3},{2,0},{3,1},{4,6},{5,7},{6,4},{7,5},{8,10},{9,11},{10,... | collective-permute-start | bytes 344072 | tf_op jit(solution)/shard_map/ppermute | solution.py:47
  44.9 9.3 %copy-start = (bf16[1024,2048]{1,0:T(8,128)(2,1)S(1)}, bf16[1024,2048]{1,0:T(8,128)(2,1)}, u32[]{:S(2)}) copy-start(bf16[1024,2048]{1,0:T(8,128)(2,1)} %proj_ref.1) | copy-start | bytes 12582916
  45.8 3.8 %collective-permute-start.21 = (bf16[64,128]{1,0:T(8,128)(2,1)S(1)}, bf16[64,128]{1,0:T(8,128)(2,1)S(1)}, u32[]{:S(2)}, u32[]{:S(2)}) collective-permute-start(bf16[64,128]{1,0:T(8,128)(2,1)S(1)} %get-tuple-element.77), channel_id=1, source_target_pairs={{0,2},{1,3},{2,0},{3,1},{4,6},{5,7},{6,4},{7,5},{8,10},{9,11},{10,... | collective-permute-start | bytes 49160 | tf_op jit(solution)/shard_map/ppermute | solution.py:47
  49.7 5.0 %collective-permute-start.22 = (bf16[16,1024]{1,0:T(8,128)(2,1)S(1)}, bf16[16,1024]{1,0:T(8,128)(2,1)S(1)}, u32[]{:S(2)}, u32[]{:S(2)}) collective-permute-start(bf16[16,1024]{1,0:T(8,128)(2,1)S(1)} %get-tuple-element.79), channel_id=1, source_target_pairs={{0,4},{1,5},{2,6},{3,7},{4,0},{5,1},{6,2},{7,3},{8,12},{9,13},{10,... | collective-permute-start | bytes 98312 | tf_op jit(solution)/shard_map/ppermute | solution.py:47
  51.8 4.8 %collective-permute-start.23 = (bf16[16,1024]{1,0:T(8,128)(2,1)S(1)}, bf16[16,1024]{1,0:T(8,128)(2,1)S(1)}, u32[]{:S(2)}, u32[]{:S(2)}) collective-permute-start(bf16[16,1024]{1,0:T(8,128)(2,1)S(1)} %get-tuple-element.80), channel_id=1, source_target_pairs={{0,8},{1,9},{2,10},{3,11},{4,12},{5,13},{6,14},{7,15},{8,0},{9,1},... | collective-permute-start | bytes 98312 | tf_op jit(solution)/shard_map/ppermute | solution.py:47
  52.2 5.7 %collective-permute-start.24 = (bf16[16,1024]{1,0:T(8,128)(2,1)S(1)}, bf16[16,1024]{1,0:T(8,128)(2,1)S(1)}, u32[]{:S(2)}, u32[]{:S(2)}) collective-permute-start(bf16[16,1024]{1,0:T(8,128)(2,1)S(1)} %get-tuple-element.81), channel_id=1, source_target_pairs={{0,12},{1,13},{2,14},{3,15},{4,8},{5,9},{6,10},{7,11},{8,4},{9,5},... | collective-permute-start | bytes 98312 | tf_op jit(solution)/shard_map/ppermute | solution.py:47
  54.2 3.7 %copy-start.1 = (bf16[1024,1024]{1,0:T(8,128)(2,1)S(1)}, bf16[1024,1024]{1,0:T(8,128)(2,1)}, u32[]{:S(2)}) copy-start(bf16[1024,1024]{1,0:T(8,128)(2,1)} %refs_6_.1) | copy-start | bytes 6291460
  54.2 3.7 %copy-start.3 = (f32[1024]{0:T(1024)S(1)}, f32[1024]{0:T(1024)}, u32[]{:S(2)}) copy-start(f32[1024]{0:T(1024)} %param.24) | copy-start | bytes 12292

commit v5 on v4

--- a/solution.py
+++ b/solution.py
@@ -14,7 +14,6 @@
 ROWS_AT_ONCE = 128
 EVENTS_AT_ONCE = 512
 STEPS_AHEAD = 2
-STAGE_COPIES = 4
 BLOCK = 16
 TN = (((0,), (0,)), ((), ()))
 NT = (((1,), (1,)), ((), ()))
@@ -357,9 +356,9 @@
 
 
 def attend_first_kernel(rounds_ref, pick_ref, *refs, heads, blocks, split):
-    *row_refs, extra_hbm, gain_ref, proj_ref = refs[: -7 - 3 * blocks]
-    caches = refs[-7 - 3 * blocks : -7]
-    own_ref, keep_ref, send_ref, later_ref, emb_ref, query_ref, sem = refs[-7:]
+    *row_refs, extra_hbm, gain_ref, proj_ref = refs[: -6 - 3 * blocks]
+    caches = refs[-6 - 3 * blocks : -6]
+    own_ref, keep_ref, send_ref, emb_ref, query_ref, sem = refs[-6:]
     count, width = emb_ref.shape
     rows = jnp.concatenate([r[...] for r in row_refs], axis=0)
     emb_ref[...] = jnp.dot(pick_ref[...], rows, preferred_element_type=F32).astype(BF16)
@@ -380,15 +379,8 @@
         projected = jnp.dot(normed, proj_ref[:, :width], preferred_element_type=F32)
         query = silu(projected).astype(BF16) * jnp.asarray(0.5 * head_dim**-0.5, BF16)
         query_ref[first : first + rows, :] = query
-        later_ref[first : first + rows, :] = query[:, split * LANES :]
     parts = [caches[k * blocks : (k + 1) * blocks] for k in range(3)]
     attend_groups(query_ref, parts, range(split), heads, keep_ref, send_ref)
-
-
-def attend_later_kernel(query_ref, *refs, heads, blocks, split):
-    *caches, keep_ref, send_ref = refs
-    parts = [caches[k * blocks : (k + 1) * blocks] for k in range(3)]
-    attend_groups(query_ref, parts, range(split, parts[0][0].shape[1] // LANES), heads, keep_ref, send_ref)
 
 
 def attention_cost(count, columns, keys, head_dim):
@@ -410,10 +402,9 @@
             jax.ShapeDtypeStruct((each, width), BF16),
             jax.ShapeDtypeStruct((count // 2, columns), F32),
             jax.ShapeDtypeStruct((count // 2, columns), BF16),
-            jax.ShapeDtypeStruct((count, width - columns), BF16),
         ),
         in_specs=[VMEM, VMEM] + [VMEM] * len(pieces) + [HBM] + [VMEM] * (2 + 3 * blocks),
-        out_specs=(VMEM,) * 4,
+        out_specs=(VMEM,) * 3,
         scratch_shapes=[
             pltpu.VMEM((count, width), BF16),
             pltpu.VMEM((count, width), BF16),
@@ -423,23 +414,6 @@
         cost_estimate=attention_cost(count, columns, keys, width // heads),
         name="attend_first",
     )(rounds, pick, *pieces, extra, gain, proj, *keys, *values, *biases)
-
-
-def attend_later(queries, keys, values, biases, heads, split):
-    count, columns = queries.shape
-    blocks = len(keys)
-    return pl.pallas_call(
-        functools.partial(attend_later_kernel, heads=heads, blocks=blocks, split=split),
-        out_shape=(
-            jax.ShapeDtypeStruct((count // 2, columns), F32),
-            jax.ShapeDtypeStruct((count // 2, columns), BF16),
-        ),
-        in_specs=[VMEM] * (1 + 3 * blocks),
-        out_specs=(VMEM, VMEM),
-        compiler_params=params(20),
-        cost_estimate=attention_cost(count, columns, keys, keys[0].shape[1] // heads),
-        name="attend_later",
-    )(queries, *keys, *values, *biases)
 
 
 def combine_kernel(*refs, count):
@@ -471,12 +445,12 @@
 def stage_kernel(*refs, width):
     *refs, sems = refs
     count = len(refs) // 2
-    copies = []
-    for k, (a, b) in enumerate(zip(refs[:count], refs[count:])):
-        rows = a.shape[0] // STAGE_COPIES
-        for c in range(STAGE_COPIES):
-            part = pl.ds(c * rows, rows)
-            copies.append(pltpu.make_async_copy(a.at[part, pl.ds(0, width)], b.at[part, :], sems.at[k, c]))
+    copies = [
+        pltpu.make_async_copy(
+            a if a.shape[1] == width else a.at[:, pl.ds(0, width)], b, sems.at[k]
+        )
+        for k, (a, b) in enumerate(zip(refs[:count], refs[count:]))
+    ]
     for c in copies:
         c.start()
     for c in copies:
@@ -489,7 +463,7 @@
         out_shape=tuple(jax.ShapeDtypeStruct((a.shape[0], width), BF16) for a in arrays),
         in_specs=[HBM if held else pl.BlockSpec(memory_space=pl.ANY)] * len(arrays),
         out_specs=(VMEM,) * len(arrays),
-        scratch_shapes=[pltpu.SemaphoreType.DMA((len(arrays), STAGE_COPIES))],
+        scratch_shapes=[pltpu.SemaphoreType.DMA((len(arrays),))],
         compiler_params=params(4),
         name="stage",
     )(*(pltpu.with_memory_space_constraint(a, pltpu.HBM) if held else a for a in arrays))
@@ -586,15 +560,13 @@
     none = jnp.zeros((each * (size // 2), width), BF16)
     _, extra = lax.while_loop(lambda s: s[0] < rounds[0], more, (jnp.int32(1), none))
 
-    (keys,) = stage(width, key_cache)
-    proj, values, other_keys, other_values = stage(width, proj_in, value_cache, other_keys, other_values)
+    proj, keys, values, other_keys, other_values = stage(
+        width, proj_in, key_cache, value_cache, other_keys, other_values
+    )
     caches = ([keys, other_keys], [values, other_values], [bias, other_bias])
     *far, near = stage_masks(size)
-    split = max(1, width // LANES * 7 // 8)
-    own, keep, send, later = attend_first(told, pick, pieces, extra, gain, proj, *caches, heads, each, split)
+    own, keep, send = attend_first(told, pick, pieces, extra, gain, proj, *caches, heads, each, width // LANES)
     halves = [keep, swap(send, near[0], axis, size)]
-    keep, send = attend_later(later, *caches, heads, split)
-    halves += [keep, swap(send, near[0], axis, size)]
     gates = gates_of(own, gain, proj_in)
 
     total, *going = combine(halves, len(combos(far[-1])))

time: 59.3 us -> 57.3 us (0.966)
  Pallas kernels: 15.7 us -> 14.6 us
  starting transfers between devices: 18.4 us -> 17.8 us
    pallas_call x3 -> x2, Pallas kernels: 5.24 us -> 4.26 us  [stage(): pl.pallas_call(functools.partial(stage_kernel, width=width), out_shape=tu...]
    pallas_call x1 -> x0, Pallas kernels: 0.92 us -> none  [attend_later(): pl.pallas_call(functools.partial(attend_later_kernel, heads=heads, blocks...]
    pallas_call x1, Pallas kernels: 4.6 us -> 5.38 us  [attend_first(): pl.pallas_call(functools.partial(attend_first_kernel, heads=heads, blocks...]
    ppermute x19 -> x18, starting transfers between devices: 18.4 us -> 17.8 us  [swap(): return lax.ppermute(x, axis, [(i, i ^ mask) for i in range(size)])]
    ppermute x19 -> x18, waiting for transfers between devices: 21.4 us -> 21.2 us  [swap(): return lax.ppermute(x, axis, [(i, i ^ mask) for i in range(size)])]
  transfers between devices with their start and end apart: 19 -> 18, of which waited for: 8 -> 8; matrix products, arithmetic and copies ran while one was open for 1% -> 1% of each run, Pallas kernels for 17% -> 14%
where the time goes in v5:
time: 57.3 us; the launch traced here: 57.1 us
  waiting for transfers between devices  21.2 us (37%)
  starting transfers between devices  17.8 us (31%)
  Pallas kernels  14.6 us (25%)
  local copies, waits for them, and re-layouts  1.38 us (2%)
  between operations  0.83 us (1%)
  other arithmetic  0.73 us (1%)
  loops' own time  0.64 us (1%)
    ppermute x18, waiting for transfers between devices, swap(): return lax.ppermute(x, axis, [(i, i ^ mask) for i in range(size)])  21.2 us
    ppermute x18, starting transfers between devices, swap(): return lax.ppermute(x, axis, [(i, i ^ mask) for i in range(size)])  17.8 us
    pallas_call x1, Pallas kernels, attend_first(): pl.pallas_call(functools.partial(attend_first_kernel, heads=heads, blocks...  5.38 us
    pallas_call x2, Pallas kernels, stage(): pl.pallas_call(functools.partial(stage_kernel, width=width), out_shape=tu...  4.26 us
    pallas_call x1, Pallas kernels, prepare(): pl.pallas_call(functools.partial(prepare_kernel, axis=axis, npos=pos_bias...  1.68 us
    unnamed x10, local copies, waits for them, and re-layouts  1.36 us
    pallas_call x1, Pallas kernels, finish(): pl.pallas_call(finish_kernel, out_shape=jax.ShapeDtypeStruct(embedded.sha...  1.16 us
  transfers between devices with their start and end apart: 18, of which 8 were waited for; matrix products, arithmetic and copies ran while one was open for 1% of the time, Pallas kernels for 14%

profile of v5, /device:TPU:0, one launch (start us, length us, event | category | flops | bytes accessed | tf_op | source)
XLA Modules:
  0.0 57.1 jit_solution(124595284563035625)
XLA Ops:
  0.0 0.5 collective-permute-start.10
  0.5 2.6 %collective-permute-start.6 = (s32[1,16]{1,0:T(1,128)}, s32[1,16]{1,0:T(1,128)S(1)}, u32[]{:S(2)}, u32[]{:S(2)}) collective-permute-start(s32[1,16]{1,0:T(1,128)} %bitcast.13), channel_id=1, source_target_pairs={{0,4},{1,5},{2,6},{3,7},{4,0},{5,1},{6,2},{7,3},{8,12},{9,13},{10,... | collective-permute-start | bytes 200 | tf_op jit(solution)/shard_map/ppermute | solution.py:46
  3.1 2.6 %collective-permute-start.7 = (s32[1,16]{1,0:T(1,128)}, s32[1,16]{1,0:T(1,128)S(1)}, u32[]{:S(2)}, u32[]{:S(2)}) collective-permute-start(s32[1,16]{1,0:T(1,128)} %bitcast.14), channel_id=1, source_target_pairs={{0,8},{1,9},{2,10},{3,11},{4,12},{5,13},{6,14},{7,15},{8,0},{9,1},... | collective-permute-start | bytes 200 | tf_op jit(solution)/shard_map/ppermute | solution.py:46
  5.6 0.0 collective-permute-start.8
  5.6 0.0 collective-permute-done.6
  5.7 2.0 %collective-permute-done.7 = s32[1,16]{1,0:T(1,128)S(1)} collective-permute-done((s32[1,16]{1,0:T(1,128)}, s32[1,16]{1,0:T(1,128)S(1)}, u32[]{:S(2)}, u32[]{:S(2)}) %collective-permute-start.7) | collective-permute-done | bytes 96 | tf_op jit(solution)/shard_map/ppermute | solution.py:46
  7.7 3.5 %collective-permute-done.8 = s32[1,16]{1,0:T(1,128)S(1)} collective-permute-done((s32[1,16]{1,0:T(1,128)}, s32[1,16]{1,0:T(1,128)S(1)}, u32[]{:S(2)}, u32[]{:S(2)}) %collective-permute-start.8) | collective-permute-done | bytes 96 | tf_op jit(solution)/shard_map/ppermute | solution.py:46
  11.1 0.7 %pad_add_fusion.refs_0_ = s32[1,64]{1,0:T(1,128)S(1)} fusion(s32[1,16]{1,0:T(1,128)S(1)} %collective-permute-done.8, s32[1,16]{1,0:T(1,128)S(1)} %collective-permute-done.7, s32[1,16]{1,0:T(1,128)S(1)} %collective-permute-done.6, s32[1,16]{1,0:T(1,128)} %bitcast.16), kind=kLoop, calls=%fused_computation.6 | loop fusion | flops 192 | bytes 512 | tf_op jit(solution)/shard_map/concatenate | solution.py:58
  11.9 1.5 %collective-permute-start.9 = (s32[1,64]{1,0:T(1,128)S(1)}, s32[1,64]{1,0:T(1,128)S(1)}, u32[]{:S(2)}, u32[]{:S(2)}) collective-permute-start(s32[1,64]{1,0:T(1,128)S(1)} %pad_add_fusion.refs_0_), channel_id=1, source_target_pairs={{0,2},{1,3},{2,0},{3,1},{4,6},{5,7},{6,4},{7,5},{8,10},{9,11},{10,... | collective-permute-start | bytes 776 | tf_op jit(solution)/shard_map/ppermute | solution.py:46
  13.4 0.0 collective-permute-start.17
  13.4 2.0 %collective-permute-done.9.refs_1_ = s32[1,64]{1,0:T(1,128)S(1)} collective-permute-done((s32[1,64]{1,0:T(1,128)S(1)}, s32[1,64]{1,0:T(1,128)S(1)}, u32[]{:S(2)}, u32[]{:S(2)}) %collective-permute-start.9) | collective-permute-done | bytes 288 | tf_op jit(solution)/shard_map/ppermute | solution.py:46
  15.4 0.9 %plan.2 = (bf16[128,256]{1,0:T(8,128)(2,1)S(1)}, s32[1]{0:T(128)}, s32[8,128]{1,0:T(8,128)S(1)}) custom-call(s32[1,64]{1,0:T(1,128)S(1)} %pad_add_fusion.refs_0_, s32[1,64]{1,0:T(1,128)S(1)} %collective-permute-done.9.refs_1_), custom_call_target="tpu_custom_call" | custom-call | tf_op jit(solution)/shard_map/plan/pallas_call | solution.py:203
  16.3 0.0 collective-permute-done.10.refs_0_
  16.4 0.6 %while.10 = (s32[]{:T(128)}, bf16[128,1024]{1,0:T(8,128)(2,1)S(1)}, s32[1]{0:T(128)}, s32[1,64]{1,0:T(1,128)S(1)}, s32[1,64]{1,0:T(1,128)S(1)}, /*index=5*/bf16[...) while((s32[]{:T(128)}, bf16[128,1024]{1,0:T(8,128)(2,1)S(1)}, s32[1]{0:T(128)}, ...), condition=%wide.region_1.0_spmd, body=%wide.region_0.0_spmd.sunk | while | flops 131074 | bytes 20447612 | solution.py:561
  17.0 0.1 collective-permute-start.18
  17.8 1.7 %prepare.1 = (bf16[1024,128]{1,0:T(8,128)(2,1)S(1)}, bf16[1024,1024]{1,0:T(8,128)(2,1)S(1)}) custom-call(s32[1]{0:T(128)S(6)} %copy.24.start_ref, s32[1,1024]{1,0:T(1,128)} %bitcast.12, f32[16,128]{1,0:T(8,128)} %time_bias_hbm.1, f32[16,18]{1,0:T(8,128)} %pos_bias_hbm.1, bf16[1024,1024]{1,0:T(8,128)(2,1)} %get-tuple-element.193), custom_call_target="tpu_custom_call" | custom-call | tf_op jit(solution)/shard_map/prepare/pallas_call | solution.py:272
  19.4 0.6 collective-permute-start.19
  20.0 0.1 stage.2.refs_3_
  20.2 0.7 %lookup.2.refs_0_ = bf16[32,1024]{1,0:T(8,128)(2,1)S(1)} custom-call(s32[1,64]{1,0:T(1,128)S(1)} %get-tuple-element.205, s32[1,64]{1,0:T(1,128)S(1)} %get-tuple-element.207, bf16[1024,1024]{1,0:T(8,128)(2,1)S(1)} %get-tuple-element.63.refs_2_, bf16[1024,1024]{1,0:T(8,128)(2,1)S(1)} %stage.2.refs_3_), custom_call_target="tpu_custom_call" | custom-call | tf_op jit(solution)/shard_map/lookup/pallas_call | solution.py:161
  20.9 0.0 collective-permute-start.12
  20.9 1.0 %collective-permute-start.13 = (bf16[32,1024]{1,0:T(8,128)(2,1)S(1)}, bf16[32,1024]{1,0:T(8,128)(2,1)S(1)}, u32[]{:S(2)}, u32[]{:S(2)}) collective-permute-start(bf16[32,1024]{1,0:T(8,128)(2,1)S(1)} %lookup.2.refs_0_), channel_id=1, source_target_pairs={{0,12},{1,13},{2,14},{3,15},{4,8},{5,9},{6,10},{7,11},{8,4},{9,5},... | collective-permute-start | bytes 196616 | tf_op jit(solution)/shard_map/ppermute | solution.py:46
  21.9 6.0 %collective-permute-done.12.refs_0_ = bf16[32,1024]{1,0:T(8,128)(2,1)S(1)} collective-permute-done((bf16[32,1024]{1,0:T(8,128)(2,1)S(1)}, bf16[32,1024]{1,0:T(8,128)(2,1)S(1)}, u32[]{:S(2)}, u32[]{:S(2)}) %collective-permute-start.12) | collective-permute-done | bytes 65568 | tf_op jit(solution)/shard_map/ppermute | solution.py:46
  27.9 1.5 %collective-permute-start.14 = (bf16[32,1024]{1,0:T(8,128)(2,1)S(1)}, bf16[32,1024]{1,0:T(8,128)(2,1)S(1)}, u32[]{:S(2)}, u32[]{:S(2)}) collective-permute-start(bf16[32,1024]{1,0:T(8,128)(2,1)S(1)} %lookup.2.refs_0_), channel_id=1, source_target_pairs={{0,2},{1,3},{2,0},{3,1},{4,6},{5,7},{6,4},{7,5},{8,10},{9,11},{10,... | collective-permute-start | bytes 196616 | tf_op jit(solution)/shard_map/ppermute | solution.py:46
  29.4 0.0 collective-permute-done.13.refs_1_
  29.4 0.0 copy-start.2
  29.4 0.6 %collective-permute-start.16 = (bf16[64,1024]{1,0:T(8,128)(2,1)S(1)}, bf16[64,1024]{1,0:T(8,128)(2,1)S(1)}, u32[]{:S(2)}, u32[]{:S(2)}) collective-permute-start(bf16[64,1024]{1,0:T(8,128)(2,1)S(1)} %join.2.refs_2_), channel_id=1, source_target_pairs={{0,2},{1,3},{2,0},{3,1},{4,6},{5,7},{6,4},{7,5},{8,10},{9,11},{10,... | collective-permute-start | bytes 393224 | tf_op jit(solution)/shard_map/ppermute | solution.py:46
  30.0 0.0 collective-permute-done.17.refs_3_
  30.0 0.8 %collective-permute-start.11 = (bf16[32,1024]{1,0:T(8,128)(2,1)S(1)}, bf16[32,1024]{1,0:T(8,128)(2,1)S(1)}, u32[]{:S(2)}, u32[]{:S(2)}) collective-permute-start(bf16[32,1024]{1,0:T(8,128)(2,1)S(1)} %lookup.2.refs_0_), channel_id=1, source_target_pairs={{0,4},{1,5},{2,6},{3,7},{4,0},{5,1},{6,2},{7,3},{8,12},{9,13},{10,... | collective-permute-start | bytes 196616 | tf_op jit(solution)/shard_map/ppermute | solution.py:46
  30.8 1.4 %collective-permute-done.14.refs_3_ = bf16[32,1024]{1,0:T(8,128)(2,1)S(1)} collective-permute-done((bf16[32,1024]{1,0:T(8,128)(2,1)S(1)}, bf16[32,1024]{1,0:T(8,128)(2,1)S(1)}, u32[]{:S(2)}, u32[]{:S(2)}) %collective-permute-start.14) | collective-permute-done | bytes 65568 | tf_op jit(solution)/shard_map/ppermute | solution.py:46
  32.2 0.0 collective-permute-start.15
  32.2 0.0 collective-permute-done.18.refs_4_
  32.2 0.0 copy-start.6
  32.2 1.3 %copy-done.6 = bf16[1024,1024]{1,0:T(8,128)(2,1)} copy-done((bf16[1024,1024]{1,0:T(8,128)(2,1)}, bf16[1024,1024]{1,0:T(8,128)(2,1)S(1)}, u32[]{:S(2)}) %copy-start.6) | copy-done | bytes 2097176
  33.5 4.1 %stage.3 = (bf16[1024,1024]{1,0:T(8,128)(2,1)S(1)}, bf16[1024,1024]{1,0:T(8,128)(2,1)S(1)}, bf16[1024,1024]{1,0:T(8,128)(2,1)S(1)}, bf16[1024,1024]{1,0:T(8,128)(2,1)S(1)}, bf16[1024,1024]{1,0:T(8,128)(2,1)S(1)}) custom-call(bf16[1024,2048]{1,0:T(8,128)(2,1)} %proj_ref.1, bf16[1024,1024]{1,0:T(8,128)(2,1)} %refs_1_.1, bf16[1024,1024]{1,0:T(8,128)(2,1)} %refs_2_.1, ...), custom_call_target="tpu_custom_call" | custom-call | tf_op jit(solution)/shard_map/stage/pallas_call | solution.py:461
  37.6 0.0 collective-permute-done.19.refs_14_
  37.6 0.0 collective-permute-done.11.refs_1_
  37.6 0.0 collective-permute-done.15.refs_4_
  37.7 0.0 collective-permute-done.16.refs_5_
  37.7 0.0 copy-done.2
  37.7 0.0 copy-start
  37.7 5.4 %attend_first.1 = (bf16[16,1024]{1,0:T(8,128)(2,1)S(1)}, f32[64,1024]{1,0:T(8,128)S(1)}, bf16[64,1024]{1,0:T(8,128)(2,1)S(1)}) custom-call(s32[8,128]{1,0:T(8,128)S(1)} %get-tuple-element.61.rounds_ref, bf16[128,256]{1,0:T(8,128)(2,1)S(1)} %get-tuple-element.62.pick_ref, bf16[32,1024]{1,0:T(8,128)(2,1)S(1)} %lookup.2.refs_0_, ...), custom_call_target="tpu_custom_call" | custom-call | flops 2147483648 | bytes 8388608 | tf_op jit(solution)/shard_map/attend_first/pallas_call | solution.py:399
  43.1 1.6 %collective-permute-start.20 = (bf16[64,1024]{1,0:T(8,128)(2,1)S(1)}, bf16[64,1024]{1,0:T(8,128)(2,1)S(1)}, u32[]{:S(2)}, u32[]{:S(2)}) collective-permute-start(bf16[64,1024]{1,0:T(8,128)(2,1)S(1)} %get-tuple-element.73), channel_id=1, source_target_pairs={{0,2},{1,3},{2,0},{3,1},{4,6},{5,7},{6,4},{7,5},{8,10},{9,11},{10,... | collective-permute-start | bytes 393224 | tf_op jit(solution)/shard_map/ppermute | solution.py:46
  44.7 3.4 %collective-permute-done.20.refs_1_ = bf16[64,1024]{1,0:T(8,128)(2,1)S(1)} collective-permute-done((bf16[64,1024]{1,0:T(8,128)(2,1)S(1)}, bf16[64,1024]{1,0:T(8,128)(2,1)S(1)}, u32[]{:S(2)}, u32[]{:S(2)}) %collective-permute-start.20) | collective-permute-done | bytes 131104 | tf_op jit(solution)/shard_map/ppermute | solution.py:46
  48.1 2.1 %collective-permute-start.21 = (bf16[16,1024]{1,0:T(8,128)(2,1)S(1)}, bf16[16,1024]{1,0:T(8,128)(2,1)S(1)}, u32[]{:S(2)}, u32[]{:S(2)}) collective-permute-start(bf16[16,1024]{1,0:T(8,128)(2,1)S(1)} %get-tuple-element.75), channel_id=1, source_target_pairs={{0,4},{1,5},{2,6},{3,7},{4,0},{5,1},{6,2},{7,3},{8,12},{9,13},{10,... | collective-permute-start | bytes 98312 | tf_op jit(solution)/shard_map/ppermute | solution.py:46
  50.2 0.0 collective-permute-start.22
  50.2 2.4 %collective-permute-start.23 = (bf16[16,1024]{1,0:T(8,128)(2,1)S(1)}, bf16[16,1024]{1,0:T(8,128)(2,1)S(1)}, u32[]{:S(2)}, u32[]{:S(2)}) collective-permute-start(bf16[16,1024]{1,0:T(8,128)(2,1)S(1)} %get-tuple-element.77), channel_id=1, source_target_pairs={{0,12},{1,13},{2,14},{3,15},{4,8},{5,9},{6,10},{7,11},{8,4},{9,5},... | collective-permute-start | bytes 98312 | tf_op jit(solution)/shard_map/ppermute | solution.py:46
  52.7 0.0 copy-done
  52.7 0.0 copy-start.1
  52.7 0.0 copy-start.3
  52.7 0.5 gates.1.refs_4_
  53.1 0.0 collective-permute-done.21.refs_0_
  53.1 1.9 %collective-permute-done.22.refs_1_ = bf16[16,1024]{1,0:T(8,128)(2,1)S(1)} collective-permute-done((bf16[16,1024]{1,0:T(8,128)(2,1)S(1)}, bf16[16,1024]{1,0:T(8,128)(2,1)S(1)}, u32[]{:S(2)}, u32[]{:S(2)}) %collective-permute-start.22) | collective-permute-done | bytes 32800 | tf_op jit(solution)/shard_map/ppermute | solution.py:46
  55.0 0.9 %collective-permute-done.23.refs_2_ = bf16[16,1024]{1,0:T(8,128)(2,1)S(1)} collective-permute-done((bf16[16,1024]{1,0:T(8,128)(2,1)S(1)}, bf16[16,1024]{1,0:T(8,128)(2,1)S(1)}, u32[]{:S(2)}, u32[]{:S(2)}) %collective-permute-start.23) | collective-permute-done | bytes 32800 | tf_op jit(solution)/shard_map/ppermute | solution.py:46
  55.9 0.0 copy-done.1
  55.9 0.0 copy-done.3
  55.9 1.2 %finish.1 = bf16[16,1024]{1,0:T(8,128)(2,1)} custom-call(f32[16,1024]{1,0:T(8,128)S(1)} %get-tuple-element.74.own_ref, bf16[16,1024]{1,0:T(8,128)(2,1)S(1)} %collective-permute-done.21.refs_0_, bf16[16,1024]{1,0:T(8,128)(2,1)S(1)} %collective-permute-done.22.refs_1_, bf16[16,1024]{1,0:T(8,128)(2,1)S(1)} %collective-permute-done.23.refs_2_, ...), custom_call_target="tpu_custom_call" | custom-call | tf_op jit(solution)/shard_map/finish/pallas_call | solution.py:504
  (3 shorter events, 0.1 us)
Async XLA Ops:
  0.0 16.3 %collective-permute-start.10 = (bf16[1024,1024]{1,0:T(8,128)(2,1)}, bf16[1024,1024]{1,0:T(8,128)(2,1)S(1)}, u32[]{:S(2)}, u32[]{:S(2)}) collective-permute-start(bf16[1024,1024]{1,0:T(8,128)(2,1)} %table_hbm.1), channel_id=1, source_target_pairs={{0,1},{1,0},{2,3},{3,2},{4,5},{5,4},{6,7},{7,6},{8,9},{9,8},{10,11... | collective-permute-start | bytes 6291464 | tf_op jit(solution)/shard_map/ppermute | solution.py:46
  0.5 5.2 %collective-permute-start.6 = (s32[1,16]{1,0:T(1,128)}, s32[1,16]{1,0:T(1,128)S(1)}, u32[]{:S(2)}, u32[]{:S(2)}) collective-permute-start(s32[1,16]{1,0:T(1,128)} %bitcast.13), channel_id=1, source_target_pairs={{0,4},{1,5},{2,6},{3,7},{4,0},{5,1},{6,2},{7,3},{8,12},{9,13},{10,... | collective-permute-start | bytes 200 | tf_op jit(solution)/shard_map/ppermute | solution.py:46
  3.1 4.6 %collective-permute-start.7 = (s32[1,16]{1,0:T(1,128)}, s32[1,16]{1,0:T(1,128)S(1)}, u32[]{:S(2)}, u32[]{:S(2)}) collective-permute-start(s32[1,16]{1,0:T(1,128)} %bitcast.14), channel_id=1, source_target_pairs={{0,8},{1,9},{2,10},{3,11},{4,12},{5,13},{6,14},{7,15},{8,0},{9,1},... | collective-permute-start | bytes 200 | tf_op jit(solution)/shard_map/ppermute | solution.py:46
  5.6 5.5 %collective-permute-start.8 = (s32[1,16]{1,0:T(1,128)}, s32[1,16]{1,0:T(1,128)S(1)}, u32[]{:S(2)}, u32[]{:S(2)}) collective-permute-start(s32[1,16]{1,0:T(1,128)} %bitcast.15), channel_id=1, source_target_pairs={{0,12},{1,13},{2,14},{3,15},{4,8},{5,9},{6,10},{7,11},{8,4},{9,5},... | collective-permute-start | bytes 200 | tf_op jit(solution)/shard_map/ppermute | solution.py:46
  11.9 3.6 %collective-permute-start.9 = (s32[1,64]{1,0:T(1,128)S(1)}, s32[1,64]{1,0:T(1,128)S(1)}, u32[]{:S(2)}, u32[]{:S(2)}) collective-permute-start(s32[1,64]{1,0:T(1,128)S(1)} %pad_add_fusion.refs_0_), channel_id=1, source_target_pairs={{0,2},{1,3},{2,0},{3,1},{4,6},{5,7},{6,4},{7,5},{8,10},{9,11},{10,... | collective-permute-start | bytes 776 | tf_op jit(solution)/shard_map/ppermute | solution.py:46
  13.4 16.6 %collective-permute-start.17 = (bf16[1024,1024]{1,0:T(8,128)(2,1)}, bf16[1024,1024]{1,0:T(8,128)(2,1)}, u32[]{:S(2)}, u32[]{:S(2)}) collective-permute-start(bf16[1024,1024]{1,0:T(8,128)(2,1)} %refs_1_.1), channel_id=1, source_target_pairs={{0,1},{1,0},{2,3},{3,2},{4,5},{5,4},{6,7},{7,6},{8,9},{9,8},{10,11... | collective-permute-start | bytes 6291464 | tf_op jit(solution)/shard_map/ppermute | solution.py:46
  17.0 15.1 %collective-permute-start.18 = (bf16[1024,1024]{1,0:T(8,128)(2,1)}, bf16[1024,1024]{1,0:T(8,128)(2,1)S(1)}, u32[]{:S(2)}, u32[]{:S(2)}) collective-permute-start(bf16[1024,1024]{1,0:T(8,128)(2,1)} %refs_2_.1), channel_id=1, source_target_pairs={{0,1},{1,0},{2,3},{3,2},{4,5},{5,4},{6,7},{7,6},{8,9},{9,8},{10,11... | collective-permute-start | bytes 6291464 | tf_op jit(solution)/shard_map/ppermute | solution.py:46
  19.4 18.2 %collective-permute-start.19 = (bf16[1024,128]{1,0:T(8,128)(2,1)S(1)}, bf16[1024,128]{1,0:T(8,128)(2,1)S(1)}, u32[]{:S(2)}, u32[]{:S(2)}) collective-permute-start(bf16[1024,128]{1,0:T(8,128)(2,1)S(1)} %get-tuple-element.71.refs_13_), channel_id=1, source_target_pairs={{0,1},{1,0},{2,3},{3,2},{4,5},{5,4},{6,7},{7,6},{8,9},{9,8},{10,11... | collective-permute-start | bytes 786440 | tf_op jit(solution)/shard_map/ppermute | solution.py:46
  20.9 7.0 %collective-permute-start.12 = (bf16[32,1024]{1,0:T(8,128)(2,1)S(1)}, bf16[32,1024]{1,0:T(8,128)(2,1)S(1)}, u32[]{:S(2)}, u32[]{:S(2)}) collective-permute-start(bf16[32,1024]{1,0:T(8,128)(2,1)S(1)} %lookup.2.refs_0_), channel_id=1, source_target_pairs={{0,8},{1,9},{2,10},{3,11},{4,12},{5,13},{6,14},{7,15},{8,0},{9,1},... | collective-permute-start | bytes 196616 | tf_op jit(solution)/shard_map/ppermute | solution.py:46
  20.9 8.5 %collective-permute-start.13 = (bf16[32,1024]{1,0:T(8,128)(2,1)S(1)}, bf16[32,1024]{1,0:T(8,128)(2,1)S(1)}, u32[]{:S(2)}, u32[]{:S(2)}) collective-permute-start(bf16[32,1024]{1,0:T(8,128)(2,1)S(1)} %lookup.2.refs_0_), channel_id=1, source_target_pairs={{0,12},{1,13},{2,14},{3,15},{4,8},{5,9},{6,10},{7,11},{8,4},{9,5},... | collective-permute-start | bytes 196616 | tf_op jit(solution)/shard_map/ppermute | solution.py:46
  27.9 4.3 %collective-permute-start.14 = (bf16[32,1024]{1,0:T(8,128)(2,1)S(1)}, bf16[32,1024]{1,0:T(8,128)(2,1)S(1)}, u32[]{:S(2)}, u32[]{:S(2)}) collective-permute-start(bf16[32,1024]{1,0:T(8,128)(2,1)S(1)} %lookup.2.refs_0_), channel_id=1, source_target_pairs={{0,2},{1,3},{2,0},{3,1},{4,6},{5,7},{6,4},{7,5},{8,10},{9,11},{10,... | collective-permute-start | bytes 196616 | tf_op jit(solution)/shard_map/ppermute | solution.py:46
  29.4 8.2 %copy-start.2 = (f32[1024]{0:T(1024)S(1)}, f32[1024]{0:T(1024)}, u32[]{:S(2)}) copy-start(f32[1024]{0:T(1024)} %param.20) | copy-start | bytes 12292
  29.4 8.2 %collective-permute-start.16 = (bf16[64,1024]{1,0:T(8,128)(2,1)S(1)}, bf16[64,1024]{1,0:T(8,128)(2,1)S(1)}, u32[]{:S(2)}, u32[]{:S(2)}) collective-permute-start(bf16[64,1024]{1,0:T(8,128)(2,1)S(1)} %join.2.refs_2_), channel_id=1, source_target_pairs={{0,2},{1,3},{2,0},{3,1},{4,6},{5,7},{6,4},{7,5},{8,10},{9,11},{10,... | collective-permute-start | bytes 393224 | tf_op jit(solution)/shard_map/ppermute | solution.py:46
  30.0 7.6 %collective-permute-start.11 = (bf16[32,1024]{1,0:T(8,128)(2,1)S(1)}, bf16[32,1024]{1,0:T(8,128)(2,1)S(1)}, u32[]{:S(2)}, u32[]{:S(2)}) collective-permute-start(bf16[32,1024]{1,0:T(8,128)(2,1)S(1)} %lookup.2.refs_0_), channel_id=1, source_target_pairs={{0,4},{1,5},{2,6},{3,7},{4,0},{5,1},{6,2},{7,3},{8,12},{9,13},{10,... | collective-permute-start | bytes 196616 | tf_op jit(solution)/shard_map/ppermute | solution.py:46
  32.2 5.5 %collective-permute-start.15 = (bf16[32,1024]{1,0:T(8,128)(2,1)S(1)}, bf16[32,1024]{1,0:T(8,128)(2,1)S(1)}, u32[]{:S(2)}, u32[]{:S(2)}) collective-permute-start(bf16[32,1024]{1,0:T(8,128)(2,1)S(1)} %collective-permute-done.14.refs_3_), channel_id=1, source_target_pairs={{0,4},{1,5},{2,6},{3,7},{4,0},{5,1},{6,2},{7,3},{8,12},{9,13},{10,... | collective-permute-start | bytes 196616 | tf_op jit(solution)/shard_map/ppermute | solution.py:46
  32.2 1.3 %copy-start.6 = (bf16[1024,1024]{1,0:T(8,128)(2,1)}, bf16[1024,1024]{1,0:T(8,128)(2,1)S(1)}, u32[]{:S(2)}) copy-start(bf16[1024,1024]{1,0:T(8,128)(2,1)S(1)} %collective-permute-done.18.refs_4_) | copy-start | bytes 6291460
  37.7 15.0 %copy-start = (bf16[1024,2048]{1,0:T(8,128)(2,1)S(1)}, bf16[1024,2048]{1,0:T(8,128)(2,1)}, u32[]{:S(2)}) copy-start(bf16[1024,2048]{1,0:T(8,128)(2,1)} %proj_ref.1) | copy-start | bytes 12582916
  43.1 5.0 %collective-permute-start.20 = (bf16[64,1024]{1,0:T(8,128)(2,1)S(1)}, bf16[64,1024]{1,0:T(8,128)(2,1)S(1)}, u32[]{:S(2)}, u32[]{:S(2)}) collective-permute-start(bf16[64,1024]{1,0:T(8,128)(2,1)S(1)} %get-tuple-element.73), channel_id=1, source_target_pairs={{0,2},{1,3},{2,0},{3,1},{4,6},{5,7},{6,4},{7,5},{8,10},{9,11},{10,... | collective-permute-start | bytes 393224 | tf_op jit(solution)/shard_map/ppermute | solution.py:46
  48.1 5.0 %collective-permute-start.21 = (bf16[16,1024]{1,0:T(8,128)(2,1)S(1)}, bf16[16,1024]{1,0:T(8,128)(2,1)S(1)}, u32[]{:S(2)}, u32[]{:S(2)}) collective-permute-start(bf16[16,1024]{1,0:T(8,128)(2,1)S(1)} %get-tuple-element.75), channel_id=1, source_target_pairs={{0,4},{1,5},{2,6},{3,7},{4,0},{5,1},{6,2},{7,3},{8,12},{9,13},{10,... | collective-permute-start | bytes 98312 | tf_op jit(solution)/shard_map/ppermute | solution.py:46
  50.2 4.8 %collective-permute-start.22 = (bf16[16,1024]{1,0:T(8,128)(2,1)S(1)}, bf16[16,1024]{1,0:T(8,128)(2,1)S(1)}, u32[]{:S(2)}, u32[]{:S(2)}) collective-permute-start(bf16[16,1024]{1,0:T(8,128)(2,1)S(1)} %get-tuple-element.76), channel_id=1, source_target_pairs={{0,8},{1,9},{2,10},{3,11},{4,12},{5,13},{6,14},{7,15},{8,0},{9,1},... | collective-permute-start | bytes 98312 | tf_op jit(solution)/shard_map/ppermute | solution.py:46
  50.2 5.7 %collective-permute-start.23 = (bf16[16,1024]{1,0:T(8,128)(2,1)S(1)}, bf16[16,1024]{1,0:T(8,128)(2,1)S(1)}, u32[]{:S(2)}, u32[]{:S(2)}) collective-permute-start(bf16[16,1024]{1,0:T(8,128)(2,1)S(1)} %get-tuple-element.77), channel_id=1, source_target_pairs={{0,12},{1,13},{2,14},{3,15},{4,8},{5,9},{6,10},{7,11},{8,4},{9,5},... | collective-permute-start | bytes 98312 | tf_op jit(solution)/shard_map/ppermute | solution.py:46
  52.7 3.3 %copy-start.1 = (bf16[1024,1024]{1,0:T(8,128)(2,1)S(1)}, bf16[1024,1024]{1,0:T(8,128)(2,1)}, u32[]{:S(2)}) copy-start(bf16[1024,1024]{1,0:T(8,128)(2,1)} %refs_6_.1) | copy-start | bytes 6291460
  52.7 3.3 %copy-start.3 = (f32[1024]{0:T(1024)S(1)}, f32[1024]{0:T(1024)}, u32[]{:S(2)}) copy-start(f32[1024]{0:T(1024)} %param.24) | copy-start | bytes 12292

commit v6 on v4

--- a/solution.py
+++ b/solution.py
@@ -13,8 +13,7 @@
 LANES = 128
 ROWS_AT_ONCE = 128
 EVENTS_AT_ONCE = 512
-STEPS_AHEAD = 2
-STAGE_COPIES = 4
+STEPS_AHEAD = 3
 BLOCK = 16
 TN = (((0,), (0,)), ((), ()))
 NT = (((1,), (1,)), ((), ()))
@@ -471,12 +470,12 @@
 def stage_kernel(*refs, width):
     *refs, sems = refs
     count = len(refs) // 2
-    copies = []
-    for k, (a, b) in enumerate(zip(refs[:count], refs[count:])):
-        rows = a.shape[0] // STAGE_COPIES
-        for c in range(STAGE_COPIES):
-            part = pl.ds(c * rows, rows)
-            copies.append(pltpu.make_async_copy(a.at[part, pl.ds(0, width)], b.at[part, :], sems.at[k, c]))
+    copies = [
+        pltpu.make_async_copy(
+            a if a.shape[1] == width else a.at[:, pl.ds(0, width)], b, sems.at[k]
+        )
+        for k, (a, b) in enumerate(zip(refs[:count], refs[count:]))
+    ]
     for c in copies:
         c.start()
     for c in copies:
@@ -489,7 +488,7 @@
         out_shape=tuple(jax.ShapeDtypeStruct((a.shape[0], width), BF16) for a in arrays),
         in_specs=[HBM if held else pl.BlockSpec(memory_space=pl.ANY)] * len(arrays),
         out_specs=(VMEM,) * len(arrays),
-        scratch_shapes=[pltpu.SemaphoreType.DMA((len(arrays), STAGE_COPIES))],
+        scratch_shapes=[pltpu.SemaphoreType.DMA((len(arrays),))],
         compiler_params=params(4),
         name="stage",
     )(*(pltpu.with_memory_space_constraint(a, pltpu.HBM) if held else a for a in arrays))
@@ -586,8 +585,9 @@
     none = jnp.zeros((each * (size // 2), width), BF16)
     _, extra = lax.while_loop(lambda s: s[0] < rounds[0], more, (jnp.int32(1), none))
 
-    (keys,) = stage(width, key_cache)
-    proj, values, other_keys, other_values = stage(width, proj_in, value_cache, other_keys, other_values)
+    proj, keys, values, other_keys, other_values = stage(
+        width, proj_in, key_cache, value_cache, other_keys, other_values
+    )
     caches = ([keys, other_keys], [values, other_values], [bias, other_bias])
     *far, near = stage_masks(size)
     split = max(1, width // LANES * 7 // 8)

time: 59.3 us -> 58.4 us (0.985)
  Pallas kernels: 15.7 us -> 14.9 us
    pallas_call x3 -> x2, Pallas kernels: 5.24 us -> 4.26 us  [stage(): pl.pallas_call(functools.partial(stage_kernel, width=width), out_shape=tu...]
  transfers between devices with their start and end apart: 19 -> 19, of which waited for: 8 -> 8; matrix products, arithmetic and copies ran while one was open for 1% -> 1% of each run, Pallas kernels for 17% -> 15%
where the time goes in v6:
time: 58.4 us; the launch traced here: 58.2 us
  waiting for transfers between devices  21.4 us (37%)
  starting transfers between devices  18.3 us (31%)
  Pallas kernels  14.9 us (26%)
  local copies, waits for them, and re-layouts  1.36 us (2%)
  between operations  0.83 us (1%)
  other arithmetic  0.73 us (1%)
  loops' own time  0.69 us (1%)
    ppermute x19, waiting for transfers between devices, swap(): return lax.ppermute(x, axis, [(i, i ^ mask) for i in range(size)])  21.4 us
    ppermute x19, starting transfers between devices, swap(): return lax.ppermute(x, axis, [(i, i ^ mask) for i in range(size)])  18.3 us
    pallas_call x1, Pallas kernels, attend_first(): pl.pallas_call(functools.partial(attend_first_kernel, heads=heads, blocks...  4.81 us
    pallas_call x2, Pallas kernels, stage(): pl.pallas_call(functools.partial(stage_kernel, width=width), out_shape=tu...  4.26 us
    pallas_call x1, Pallas kernels, prepare(): pl.pallas_call(functools.partial(prepare_kernel, axis=axis, npos=pos_bias...  1.68 us
    unnamed x10, local copies, waits for them, and re-layouts  1.34 us
  transfers between devices with their start and end apart: 19, of which 8 were waited for; matrix products, arithmetic and copies ran while one was open for 1% of the time, Pallas kernels for 15%

profile of v6, /device:TPU:0, one launch (start us, length us, event | category | flops | bytes accessed | tf_op | source)
XLA Modules:
  0.0 58.2 jit_solution(14319548255441699249)
XLA Ops:
  0.0 0.5 collective-permute-start.10
  0.5 2.6 %collective-permute-start.6 = (s32[1,16]{1,0:T(1,128)}, s32[1,16]{1,0:T(1,128)S(1)}, u32[]{:S(2)}, u32[]{:S(2)}) collective-permute-start(s32[1,16]{1,0:T(1,128)} %bitcast.13), channel_id=1, source_target_pairs={{0,4},{1,5},{2,6},{3,7},{4,0},{5,1},{6,2},{7,3},{8,12},{9,13},{10,... | collective-permute-start | bytes 200 | tf_op jit(solution)/shard_map/ppermute | solution.py:46
  3.1 2.6 %collective-permute-start.7 = (s32[1,16]{1,0:T(1,128)}, s32[1,16]{1,0:T(1,128)S(1)}, u32[]{:S(2)}, u32[]{:S(2)}) collective-permute-start(s32[1,16]{1,0:T(1,128)} %bitcast.14), channel_id=1, source_target_pairs={{0,8},{1,9},{2,10},{3,11},{4,12},{5,13},{6,14},{7,15},{8,0},{9,1},... | collective-permute-start | bytes 200 | tf_op jit(solution)/shard_map/ppermute | solution.py:46
  5.6 0.0 collective-permute-start.8
  5.6 0.0 collective-permute-done.6
  5.7 2.0 %collective-permute-done.7 = s32[1,16]{1,0:T(1,128)S(1)} collective-permute-done((s32[1,16]{1,0:T(1,128)}, s32[1,16]{1,0:T(1,128)S(1)}, u32[]{:S(2)}, u32[]{:S(2)}) %collective-permute-start.7) | collective-permute-done | bytes 96 | tf_op jit(solution)/shard_map/ppermute | solution.py:46
  7.7 3.5 %collective-permute-done.8 = s32[1,16]{1,0:T(1,128)S(1)} collective-permute-done((s32[1,16]{1,0:T(1,128)}, s32[1,16]{1,0:T(1,128)S(1)}, u32[]{:S(2)}, u32[]{:S(2)}) %collective-permute-start.8) | collective-permute-done | bytes 96 | tf_op jit(solution)/shard_map/ppermute | solution.py:46
  11.1 0.7 %pad_add_fusion.refs_0_ = s32[1,64]{1,0:T(1,128)S(1)} fusion(s32[1,16]{1,0:T(1,128)S(1)} %collective-permute-done.8, s32[1,16]{1,0:T(1,128)S(1)} %collective-permute-done.7, s32[1,16]{1,0:T(1,128)S(1)} %collective-permute-done.6, s32[1,16]{1,0:T(1,128)} %bitcast.16), kind=kLoop, calls=%fused_computation.6 | loop fusion | flops 192 | bytes 512 | tf_op jit(solution)/shard_map/concatenate | solution.py:58
  11.9 1.5 %collective-permute-start.9 = (s32[1,64]{1,0:T(1,128)S(1)}, s32[1,64]{1,0:T(1,128)S(1)}, u32[]{:S(2)}, u32[]{:S(2)}) collective-permute-start(s32[1,64]{1,0:T(1,128)S(1)} %pad_add_fusion.refs_0_), channel_id=1, source_target_pairs={{0,2},{1,3},{2,0},{3,1},{4,6},{5,7},{6,4},{7,5},{8,10},{9,11},{10,... | collective-permute-start | bytes 776 | tf_op jit(solution)/shard_map/ppermute | solution.py:46
  13.4 0.0 collective-permute-start.17
  13.4 2.0 %collective-permute-done.9.refs_1_ = s32[1,64]{1,0:T(1,128)S(1)} collective-permute-done((s32[1,64]{1,0:T(1,128)S(1)}, s32[1,64]{1,0:T(1,128)S(1)}, u32[]{:S(2)}, u32[]{:S(2)}) %collective-permute-start.9) | collective-permute-done | bytes 288 | tf_op jit(solution)/shard_map/ppermute | solution.py:46
  15.4 0.9 %plan.2 = (bf16[128,256]{1,0:T(8,128)(2,1)S(1)}, s32[1]{0:T(128)}, s32[8,128]{1,0:T(8,128)S(1)}) custom-call(s32[1,64]{1,0:T(1,128)S(1)} %pad_add_fusion.refs_0_, s32[1,64]{1,0:T(1,128)S(1)} %collective-permute-done.9.refs_1_), custom_call_target="tpu_custom_call" | custom-call | tf_op jit(solution)/shard_map/plan/pallas_call | solution.py:203
  16.3 0.0 collective-permute-done.10.refs_0_
  16.4 0.7 %while.10 = (s32[]{:T(128)}, bf16[128,1024]{1,0:T(8,128)(2,1)S(1)}, s32[1]{0:T(128)}, s32[1,64]{1,0:T(1,128)S(1)}, s32[1,64]{1,0:T(1,128)S(1)}, /*index=5*/bf16[...) while((s32[]{:T(128)}, bf16[128,1024]{1,0:T(8,128)(2,1)S(1)}, s32[1]{0:T(128)}, ...), condition=%wide.region_1.0_spmd, body=%wide.region_0.0_spmd.sunk | while | flops 131074 | bytes 20447612 | solution.py:586
  17.1 0.1 collective-permute-start.18
  17.8 1.7 %prepare.1 = (bf16[1024,128]{1,0:T(8,128)(2,1)S(1)}, bf16[1024,1024]{1,0:T(8,128)(2,1)S(1)}) custom-call(s32[1]{0:T(128)S(6)} %copy.24.start_ref, s32[1,1024]{1,0:T(1,128)} %bitcast.12, f32[16,128]{1,0:T(8,128)} %time_bias_hbm.1, f32[16,18]{1,0:T(8,128)} %pos_bias_hbm.1, bf16[1024,1024]{1,0:T(8,128)(2,1)} %get-tuple-element.201), custom_call_target="tpu_custom_call" | custom-call | tf_op jit(solution)/shard_map/prepare/pallas_call | solution.py:272
  19.5 0.6 collective-permute-start.19
  20.1 0.1 stage.2.refs_3_
  20.2 0.7 %lookup.2.refs_0_ = bf16[32,1024]{1,0:T(8,128)(2,1)S(1)} custom-call(s32[1,64]{1,0:T(1,128)S(1)} %get-tuple-element.213, s32[1,64]{1,0:T(1,128)S(1)} %get-tuple-element.215, bf16[1024,1024]{1,0:T(8,128)(2,1)S(1)} %get-tuple-element.66.refs_2_, bf16[1024,1024]{1,0:T(8,128)(2,1)S(1)} %stage.2.refs_3_), custom_call_target="tpu_custom_call" | custom-call | tf_op jit(solution)/shard_map/lookup/pallas_call | solution.py:161
  20.9 0.0 collective-permute-start.12
  20.9 1.0 %collective-permute-start.13 = (bf16[32,1024]{1,0:T(8,128)(2,1)S(1)}, bf16[32,1024]{1,0:T(8,128)(2,1)S(1)}, u32[]{:S(2)}, u32[]{:S(2)}) collective-permute-start(bf16[32,1024]{1,0:T(8,128)(2,1)S(1)} %lookup.2.refs_0_), channel_id=1, source_target_pairs={{0,12},{1,13},{2,14},{3,15},{4,8},{5,9},{6,10},{7,11},{8,4},{9,5},... | collective-permute-start | bytes 196616 | tf_op jit(solution)/shard_map/ppermute | solution.py:46
  21.9 6.0 %collective-permute-done.12.refs_0_ = bf16[32,1024]{1,0:T(8,128)(2,1)S(1)} collective-permute-done((bf16[32,1024]{1,0:T(8,128)(2,1)S(1)}, bf16[32,1024]{1,0:T(8,128)(2,1)S(1)}, u32[]{:S(2)}, u32[]{:S(2)}) %collective-permute-start.12) | collective-permute-done | bytes 65568 | tf_op jit(solution)/shard_map/ppermute | solution.py:46
  27.9 1.5 %collective-permute-start.14 = (bf16[32,1024]{1,0:T(8,128)(2,1)S(1)}, bf16[32,1024]{1,0:T(8,128)(2,1)S(1)}, u32[]{:S(2)}, u32[]{:S(2)}) collective-permute-start(bf16[32,1024]{1,0:T(8,128)(2,1)S(1)} %lookup.2.refs_0_), channel_id=1, source_target_pairs={{0,2},{1,3},{2,0},{3,1},{4,6},{5,7},{6,4},{7,5},{8,10},{9,11},{10,... | collective-permute-start | bytes 196616 | tf_op jit(solution)/shard_map/ppermute | solution.py:46
  29.5 0.0 collective-permute-done.13.refs_1_
  29.5 0.0 copy-start.2
  29.5 0.6 collective-permute-start.16
  30.1 0.0 collective-permute-done.17.refs_3_
  30.1 0.8 %collective-permute-start.11 = (bf16[32,1024]{1,0:T(8,128)(2,1)S(1)}, bf16[32,1024]{1,0:T(8,128)(2,1)S(1)}, u32[]{:S(2)}, u32[]{:S(2)}) collective-permute-start(bf16[32,1024]{1,0:T(8,128)(2,1)S(1)} %lookup.2.refs_0_), channel_id=1, source_target_pairs={{0,4},{1,5},{2,6},{3,7},{4,0},{5,1},{6,2},{7,3},{8,12},{9,13},{10,... | collective-permute-start | bytes 196616 | tf_op jit(solution)/shard_map/ppermute | solution.py:46
  30.8 1.4 %collective-permute-done.14.refs_3_ = bf16[32,1024]{1,0:T(8,128)(2,1)S(1)} collective-permute-done((bf16[32,1024]{1,0:T(8,128)(2,1)S(1)}, bf16[32,1024]{1,0:T(8,128)(2,1)S(1)}, u32[]{:S(2)}, u32[]{:S(2)}) %collective-permute-start.14) | collective-permute-done | bytes 65568 | tf_op jit(solution)/shard_map/ppermute | solution.py:46
  32.2 0.0 collective-permute-start.15
  32.2 0.0 collective-permute-done.18.refs_4_
  32.2 0.0 copy-start.6
  32.2 1.3 %copy-done.6 = bf16[1024,1024]{1,0:T(8,128)(2,1)} copy-done((bf16[1024,1024]{1,0:T(8,128)(2,1)}, bf16[1024,1024]{1,0:T(8,128)(2,1)S(1)}, u32[]{:S(2)}) %copy-start.6) | copy-done | bytes 2097176
  33.5 4.1 %stage.3 = (bf16[1024,1024]{1,0:T(8,128)(2,1)S(1)}, bf16[1024,1024]{1,0:T(8,128)(2,1)S(1)}, bf16[1024,1024]{1,0:T(8,128)(2,1)S(1)}, bf16[1024,1024]{1,0:T(8,128)(2,1)S(1)}, bf16[1024,1024]{1,0:T(8,128)(2,1)S(1)}) custom-call(bf16[1024,2048]{1,0:T(8,128)(2,1)} %proj_ref.1, bf16[1024,1024]{1,0:T(8,128)(2,1)} %refs_1_.1, bf16[1024,1024]{1,0:T(8,128)(2,1)} %refs_2_.1, ...), custom_call_target="tpu_custom_call" | custom-call | tf_op jit(solution)/shard_map/stage/pallas_call | solution.py:486
  37.7 0.0 collective-permute-done.19.refs_14_.refs_5_
  37.7 0.0 collective-permute-done.11.refs_1_
  37.7 0.0 collective-permute-done.15.refs_4_
  37.7 0.0 collective-permute-done.16.refs_5_
  37.7 0.0 copy-done.2
  37.7 4.8 %attend_first.1 = (bf16[16,1024]{1,0:T(8,128)(2,1)S(1)}, f32[64,896]{1,0:T(8,128)S(1)}, bf16[64,896]{1,0:T(8,128)(2,1)S(1)}, bf16[128,128]{1,0:T(8,128)(2,1)S(1)}) custom-call(s32[8,128]{1,0:T(8,128)S(1)} %get-tuple-element.64.rounds_ref, bf16[128,256]{1,0:T(8,128)(2,1)S(1)} %get-tuple-element.65.pick_ref, bf16[32,1024]{1,0:T(8,128)(2,1)S(1)} %lookup.2.refs_0_, ...), custom_call_target="tpu_custom_call" | custom-call | flops 1879048192 | bytes 7340032 | tf_op jit(solution)/shard_map/attend_first/pallas_call | solution.py:406
  42.5 1.6 %collective-permute-start.20 = (bf16[64,896]{1,0:T(8,128)(2,1)S(1)}, bf16[64,896]{1,0:T(8,128)(2,1)S(1)}, u32[]{:S(2)}, u32[]{:S(2)}) collective-permute-start(bf16[64,896]{1,0:T(8,128)(2,1)S(1)} %get-tuple-element.76), channel_id=1, source_target_pairs={{0,2},{1,3},{2,0},{3,1},{4,6},{5,7},{6,4},{7,5},{8,10},{9,11},{10,... | collective-permute-start | bytes 344072 | tf_op jit(solution)/shard_map/ppermute | solution.py:46
  44.1 0.0 copy-start
  44.1 0.9 %attend_later.1 = (f32[64,128]{1,0:T(8,128)S(1)}, bf16[64,128]{1,0:T(8,128)(2,1)S(1)}) custom-call(bf16[128,128]{1,0:T(8,128)(2,1)S(1)} %get-tuple-element.77.query_ref, bf16[1024,1024]{1,0:T(8,128)(2,1)S(1)} %get-tuple-element.70.refs_9_.refs_0_, bf16[1024,1024]{1,0:T(8,128)(2,1)S(1)} %get-tuple-element.71.refs_10_.refs_1_, ...), custom_call_target="tpu_custom_call" | custom-call | flops 268435456 | bytes 1048576 | tf_op jit(solution)/shard_map/attend_later/pallas_call | solution.py:430
  45.0 0.6 collective-permute-start.21
  45.6 3.2 %collective-permute-done.21.refs_3_ = bf16[64,128]{1,0:T(8,128)(2,1)S(1)} collective-permute-done((bf16[64,128]{1,0:T(8,128)(2,1)S(1)}, bf16[64,128]{1,0:T(8,128)(2,1)S(1)}, u32[]{:S(2)}, u32[]{:S(2)}) %collective-permute-start.21) | collective-permute-done | bytes 16416 | tf_op jit(solution)/shard_map/ppermute | solution.py:46
  48.8 0.0 collective-permute-done.20.refs_1_
  48.9 2.1 %collective-permute-start.22 = (bf16[16,1024]{1,0:T(8,128)(2,1)S(1)}, bf16[16,1024]{1,0:T(8,128)(2,1)S(1)}, u32[]{:S(2)}, u32[]{:S(2)}) collective-permute-start(bf16[16,1024]{1,0:T(8,128)(2,1)S(1)} %get-tuple-element.81), channel_id=1, source_target_pairs={{0,4},{1,5},{2,6},{3,7},{4,0},{5,1},{6,2},{7,3},{8,12},{9,13},{10,... | collective-permute-start | bytes 98312 | tf_op jit(solution)/shard_map/ppermute | solution.py:46
  51.0 0.4 collective-permute-start.23
  51.3 2.1 %collective-permute-start.24 = (bf16[16,1024]{1,0:T(8,128)(2,1)S(1)}, bf16[16,1024]{1,0:T(8,128)(2,1)S(1)}, u32[]{:S(2)}, u32[]{:S(2)}) collective-permute-start(bf16[16,1024]{1,0:T(8,128)(2,1)S(1)} %get-tuple-element.83), channel_id=1, source_target_pairs={{0,12},{1,13},{2,14},{3,15},{4,8},{5,9},{6,10},{7,11},{8,4},{9,5},... | collective-permute-start | bytes 98312 | tf_op jit(solution)/shard_map/ppermute | solution.py:46
  53.4 0.0 copy-done
  53.4 0.0 copy-start.1
  53.4 0.0 copy-start.3
  53.4 0.5 gates.1.refs_4_
  53.9 0.0 collective-permute-done.22.refs_0_
  53.9 1.9 %collective-permute-done.23.refs_1_ = bf16[16,1024]{1,0:T(8,128)(2,1)S(1)} collective-permute-done((bf16[16,1024]{1,0:T(8,128)(2,1)S(1)}, bf16[16,1024]{1,0:T(8,128)(2,1)S(1)}, u32[]{:S(2)}, u32[]{:S(2)}) %collective-permute-start.23) | collective-permute-done | bytes 32800 | tf_op jit(solution)/shard_map/ppermute | solution.py:46
  55.8 1.3 %collective-permute-done.24.refs_2_ = bf16[16,1024]{1,0:T(8,128)(2,1)S(1)} collective-permute-done((bf16[16,1024]{1,0:T(8,128)(2,1)S(1)}, bf16[16,1024]{1,0:T(8,128)(2,1)S(1)}, u32[]{:S(2)}, u32[]{:S(2)}) %collective-permute-start.24) | collective-permute-done | bytes 32800 | tf_op jit(solution)/shard_map/ppermute | solution.py:46
  57.1 0.0 copy-done.1
  57.1 0.0 copy-done.3
  57.1 1.2 %finish.1 = bf16[16,1024]{1,0:T(8,128)(2,1)} custom-call(f32[16,1024]{1,0:T(8,128)S(1)} %get-tuple-element.80.own_ref, bf16[16,1024]{1,0:T(8,128)(2,1)S(1)} %collective-permute-done.22.refs_0_, bf16[16,1024]{1,0:T(8,128)(2,1)S(1)} %collective-permute-done.23.refs_1_, bf16[16,1024]{1,0:T(8,128)(2,1)S(1)} %collective-permute-done.24.refs_2_, ...), custom_call_target="tpu_custom_call" | custom-call | tf_op jit(solution)/shard_map/finish/pallas_call | solution.py:529
  (3 shorter events, 0.1 us)
Async XLA Ops:
  0.0 16.3 %collective-permute-start.10 = (bf16[1024,1024]{1,0:T(8,128)(2,1)}, bf16[1024,1024]{1,0:T(8,128)(2,1)S(1)}, u32[]{:S(2)}, u32[]{:S(2)}) collective-permute-start(bf16[1024,1024]{1,0:T(8,128)(2,1)} %table_hbm.1), channel_id=1, source_target_pairs={{0,1},{1,0},{2,3},{3,2},{4,5},{5,4},{6,7},{7,6},{8,9},{9,8},{10,11... | collective-permute-start | bytes 6291464 | tf_op jit(solution)/shard_map/ppermute | solution.py:46
  0.5 5.2 %collective-permute-start.6 = (s32[1,16]{1,0:T(1,128)}, s32[1,16]{1,0:T(1,128)S(1)}, u32[]{:S(2)}, u32[]{:S(2)}) collective-permute-start(s32[1,16]{1,0:T(1,128)} %bitcast.13), channel_id=1, source_target_pairs={{0,4},{1,5},{2,6},{3,7},{4,0},{5,1},{6,2},{7,3},{8,12},{9,13},{10,... | collective-permute-start | bytes 200 | tf_op jit(solution)/shard_map/ppermute | solution.py:46
  3.1 4.6 %collective-permute-start.7 = (s32[1,16]{1,0:T(1,128)}, s32[1,16]{1,0:T(1,128)S(1)}, u32[]{:S(2)}, u32[]{:S(2)}) collective-permute-start(s32[1,16]{1,0:T(1,128)} %bitcast.14), channel_id=1, source_target_pairs={{0,8},{1,9},{2,10},{3,11},{4,12},{5,13},{6,14},{7,15},{8,0},{9,1},... | collective-permute-start | bytes 200 | tf_op jit(solution)/shard_map/ppermute | solution.py:46
  5.6 5.5 %collective-permute-start.8 = (s32[1,16]{1,0:T(1,128)}, s32[1,16]{1,0:T(1,128)S(1)}, u32[]{:S(2)}, u32[]{:S(2)}) collective-permute-start(s32[1,16]{1,0:T(1,128)} %bitcast.15), channel_id=1, source_target_pairs={{0,12},{1,13},{2,14},{3,15},{4,8},{5,9},{6,10},{7,11},{8,4},{9,5},... | collective-permute-start | bytes 200 | tf_op jit(solution)/shard_map/ppermute | solution.py:46
  11.9 3.6 %collective-permute-start.9 = (s32[1,64]{1,0:T(1,128)S(1)}, s32[1,64]{1,0:T(1,128)S(1)}, u32[]{:S(2)}, u32[]{:S(2)}) collective-permute-start(s32[1,64]{1,0:T(1,128)S(1)} %pad_add_fusion.refs_0_), channel_id=1, source_target_pairs={{0,2},{1,3},{2,0},{3,1},{4,6},{5,7},{6,4},{7,5},{8,10},{9,11},{10,... | collective-permute-start | bytes 776 | tf_op jit(solution)/shard_map/ppermute | solution.py:46
  13.4 16.7 %collective-permute-start.17 = (bf16[1024,1024]{1,0:T(8,128)(2,1)}, bf16[1024,1024]{1,0:T(8,128)(2,1)}, u32[]{:S(2)}, u32[]{:S(2)}) collective-permute-start(bf16[1024,1024]{1,0:T(8,128)(2,1)} %refs_1_.1), channel_id=1, source_target_pairs={{0,1},{1,0},{2,3},{3,2},{4,5},{5,4},{6,7},{7,6},{8,9},{9,8},{10,11... | collective-permute-start | bytes 6291464 | tf_op jit(solution)/shard_map/ppermute | solution.py:46
  17.1 15.1 %collective-permute-start.18 = (bf16[1024,1024]{1,0:T(8,128)(2,1)}, bf16[1024,1024]{1,0:T(8,128)(2,1)S(1)}, u32[]{:S(2)}, u32[]{:S(2)}) collective-permute-start(bf16[1024,1024]{1,0:T(8,128)(2,1)} %refs_2_.1), channel_id=1, source_target_pairs={{0,1},{1,0},{2,3},{3,2},{4,5},{5,4},{6,7},{7,6},{8,9},{9,8},{10,11... | collective-permute-start | bytes 6291464 | tf_op jit(solution)/shard_map/ppermute | solution.py:46
  19.5 18.2 %collective-permute-start.19 = (bf16[1024,128]{1,0:T(8,128)(2,1)S(1)}, bf16[1024,128]{1,0:T(8,128)(2,1)S(1)}, u32[]{:S(2)}, u32[]{:S(2)}) collective-permute-start(bf16[1024,128]{1,0:T(8,128)(2,1)S(1)} %get-tuple-element.74.refs_13_.refs_4_), channel_id=1, source_target_pairs={{0,1},{1,0},{2,3},{3,2},{4,5},{5,4},{6,7},{7,6},{8,9},{9,8},{10,11... | collective-permute-start | bytes 786440 | tf_op jit(solution)/shard_map/ppermute | solution.py:46
  20.9 7.0 %collective-permute-start.12 = (bf16[32,1024]{1,0:T(8,128)(2,1)S(1)}, bf16[32,1024]{1,0:T(8,128)(2,1)S(1)}, u32[]{:S(2)}, u32[]{:S(2)}) collective-permute-start(bf16[32,1024]{1,0:T(8,128)(2,1)S(1)} %lookup.2.refs_0_), channel_id=1, source_target_pairs={{0,8},{1,9},{2,10},{3,11},{4,12},{5,13},{6,14},{7,15},{8,0},{9,1},... | collective-permute-start | bytes 196616 | tf_op jit(solution)/shard_map/ppermute | solution.py:46
  20.9 8.5 %collective-permute-start.13 = (bf16[32,1024]{1,0:T(8,128)(2,1)S(1)}, bf16[32,1024]{1,0:T(8,128)(2,1)S(1)}, u32[]{:S(2)}, u32[]{:S(2)}) collective-permute-start(bf16[32,1024]{1,0:T(8,128)(2,1)S(1)} %lookup.2.refs_0_), channel_id=1, source_target_pairs={{0,12},{1,13},{2,14},{3,15},{4,8},{5,9},{6,10},{7,11},{8,4},{9,5},... | collective-permute-start | bytes 196616 | tf_op jit(solution)/shard_map/ppermute | solution.py:46
  27.9 4.3 %collective-permute-start.14 = (bf16[32,1024]{1,0:T(8,128)(2,1)S(1)}, bf16[32,1024]{1,0:T(8,128)(2,1)S(1)}, u32[]{:S(2)}, u32[]{:S(2)}) collective-permute-start(bf16[32,1024]{1,0:T(8,128)(2,1)S(1)} %lookup.2.refs_0_), channel_id=1, source_target_pairs={{0,2},{1,3},{2,0},{3,1},{4,6},{5,7},{6,4},{7,5},{8,10},{9,11},{10,... | collective-permute-start | bytes 196616 | tf_op jit(solution)/shard_map/ppermute | solution.py:46
  29.5 8.2 %copy-start.2 = (f32[1024]{0:T(1024)S(1)}, f32[1024]{0:T(1024)}, u32[]{:S(2)}) copy-start(f32[1024]{0:T(1024)} %param.20) | copy-start | bytes 12292
  29.5 8.2 %collective-permute-start.16 = (bf16[64,1024]{1,0:T(8,128)(2,1)S(1)}, bf16[64,1024]{1,0:T(8,128)(2,1)S(1)}, u32[]{:S(2)}, u32[]{:S(2)}) collective-permute-start(bf16[64,1024]{1,0:T(8,128)(2,1)S(1)} %join.2.refs_2_), channel_id=1, source_target_pairs={{0,2},{1,3},{2,0},{3,1},{4,6},{5,7},{6,4},{7,5},{8,10},{9,11},{10,... | collective-permute-start | bytes 393224 | tf_op jit(solution)/shard_map/ppermute | solution.py:46
  30.1 7.6 %collective-permute-start.11 = (bf16[32,1024]{1,0:T(8,128)(2,1)S(1)}, bf16[32,1024]{1,0:T(8,128)(2,1)S(1)}, u32[]{:S(2)}, u32[]{:S(2)}) collective-permute-start(bf16[32,1024]{1,0:T(8,128)(2,1)S(1)} %lookup.2.refs_0_), channel_id=1, source_target_pairs={{0,4},{1,5},{2,6},{3,7},{4,0},{5,1},{6,2},{7,3},{8,12},{9,13},{10,... | collective-permute-start | bytes 196616 | tf_op jit(solution)/shard_map/ppermute | solution.py:46
  32.2 5.5 %collective-permute-start.15 = (bf16[32,1024]{1,0:T(8,128)(2,1)S(1)}, bf16[32,1024]{1,0:T(8,128)(2,1)S(1)}, u32[]{:S(2)}, u32[]{:S(2)}) collective-permute-start(bf16[32,1024]{1,0:T(8,128)(2,1)S(1)} %collective-permute-done.14.refs_3_), channel_id=1, source_target_pairs={{0,4},{1,5},{2,6},{3,7},{4,0},{5,1},{6,2},{7,3},{8,12},{9,13},{10,... | collective-permute-start | bytes 196616 | tf_op jit(solution)/shard_map/ppermute | solution.py:46
  32.2 1.3 %copy-start.6 = (bf16[1024,1024]{1,0:T(8,128)(2,1)}, bf16[1024,1024]{1,0:T(8,128)(2,1)S(1)}, u32[]{:S(2)}) copy-start(bf16[1024,1024]{1,0:T(8,128)(2,1)S(1)} %collective-permute-done.18.refs_4_) | copy-start | bytes 6291460
  42.5 6.3 %collective-permute-start.20 = (bf16[64,896]{1,0:T(8,128)(2,1)S(1)}, bf16[64,896]{1,0:T(8,128)(2,1)S(1)}, u32[]{:S(2)}, u32[]{:S(2)}) collective-permute-start(bf16[64,896]{1,0:T(8,128)(2,1)S(1)} %get-tuple-element.76), channel_id=1, source_target_pairs={{0,2},{1,3},{2,0},{3,1},{4,6},{5,7},{6,4},{7,5},{8,10},{9,11},{10,... | collective-permute-start | bytes 344072 | tf_op jit(solution)/shard_map/ppermute | solution.py:46
  44.1 9.3 %copy-start = (bf16[1024,2048]{1,0:T(8,128)(2,1)S(1)}, bf16[1024,2048]{1,0:T(8,128)(2,1)}, u32[]{:S(2)}) copy-start(bf16[1024,2048]{1,0:T(8,128)(2,1)} %proj_ref.1) | copy-start | bytes 12582916
  45.0 3.8 %collective-permute-start.21 = (bf16[64,128]{1,0:T(8,128)(2,1)S(1)}, bf16[64,128]{1,0:T(8,128)(2,1)S(1)}, u32[]{:S(2)}, u32[]{:S(2)}) collective-permute-start(bf16[64,128]{1,0:T(8,128)(2,1)S(1)} %get-tuple-element.79), channel_id=1, source_target_pairs={{0,2},{1,3},{2,0},{3,1},{4,6},{5,7},{6,4},{7,5},{8,10},{9,11},{10,... | collective-permute-start | bytes 49160 | tf_op jit(solution)/shard_map/ppermute | solution.py:46
  48.9 5.0 %collective-permute-start.22 = (bf16[16,1024]{1,0:T(8,128)(2,1)S(1)}, bf16[16,1024]{1,0:T(8,128)(2,1)S(1)}, u32[]{:S(2)}, u32[]{:S(2)}) collective-permute-start(bf16[16,1024]{1,0:T(8,128)(2,1)S(1)} %get-tuple-element.81), channel_id=1, source_target_pairs={{0,4},{1,5},{2,6},{3,7},{4,0},{5,1},{6,2},{7,3},{8,12},{9,13},{10,... | collective-permute-start | bytes 98312 | tf_op jit(solution)/shard_map/ppermute | solution.py:46
  51.0 4.8 %collective-permute-start.23 = (bf16[16,1024]{1,0:T(8,128)(2,1)S(1)}, bf16[16,1024]{1,0:T(8,128)(2,1)S(1)}, u32[]{:S(2)}, u32[]{:S(2)}) collective-permute-start(bf16[16,1024]{1,0:T(8,128)(2,1)S(1)} %get-tuple-element.82), channel_id=1, source_target_pairs={{0,8},{1,9},{2,10},{3,11},{4,12},{5,13},{6,14},{7,15},{8,0},{9,1},... | collective-permute-start | bytes 98312 | tf_op jit(solution)/shard_map/ppermute | solution.py:46
  51.3 5.7 %collective-permute-start.24 = (bf16[16,1024]{1,0:T(8,128)(2,1)S(1)}, bf16[16,1024]{1,0:T(8,128)(2,1)S(1)}, u32[]{:S(2)}, u32[]{:S(2)}) collective-permute-start(bf16[16,1024]{1,0:T(8,128)(2,1)S(1)} %get-tuple-element.83), channel_id=1, source_target_pairs={{0,12},{1,13},{2,14},{3,15},{4,8},{5,9},{6,10},{7,11},{8,4},{9,5},... | collective-permute-start | bytes 98312 | tf_op jit(solution)/shard_map/ppermute | solution.py:46
  53.4 3.7 %copy-start.1 = (bf16[1024,1024]{1,0:T(8,128)(2,1)S(1)}, bf16[1024,1024]{1,0:T(8,128)(2,1)}, u32[]{:S(2)}) copy-start(bf16[1024,1024]{1,0:T(8,128)(2,1)} %refs_6_.1) | copy-start | bytes 6291460
  53.4 3.7 %copy-start.3 = (f32[1024]{0:T(1024)S(1)}, f32[1024]{0:T(1024)}, u32[]{:S(2)}) copy-start(f32[1024]{0:T(1024)} %param.24) | copy-start | bytes 12292
